TPU v7x, 128 devices: a whole 4x4x4 slice. The times are simulated.
128 devices in a mesh: row: 16 (over x, z_hi, core), col: 8 (over y, z_lo).
Axes of the slice: x: 4, y: 4, z: 4 (z_hi: 2, z_lo: 2; z = z_hi * 2 + z_lo), core: 2. Of those that a mesh axis runs over, the one named last changes fastest.
Arguments:
- features: bfloat16 [1024, 128], P(('row', 'col')), may hold values from -6 to 6
- row_weight: bfloat16 [128, 32], replicated, may hold values from -0.5 to 0.5
- col_weight: bfloat16 [128, 32], replicated, may hold values from -0.5 to 0.5
- conv_weight: bfloat16 [2, 9, 64, 64], replicated, may hold values from -0.25 to 0.25
- conv_bias: float32 [2, 64], replicated, may hold values from -3 to 3
- dilations: int32 [2], replicated, may hold values from 1 to 4, as said below
Outputs:
- pair_map: bfloat16 [64, 1024, 1024], P(None, 'row', 'col')
Inputs may be any that keep to these rules, and one draw needn't show every extreme that they name: `dilations`: one dilation a layer; at least one layer uses exactly 4.
All inputs are finite; a program needn't handle non-finite values.
Results may differ from a plain program's by a relative error of at most 0.008.
Values may be sent and summed in bfloat16 or wider, within the bound.
A program may use at most 64 MiB of HBM per device.

v0:
```python
import jax
import jax.numpy as jnp
from jax import lax
from jax.sharding import PartitionSpec as P

MAXDIL = 4
REACH = 2 * MAXDIL


def gather_projections(proj):
    along_col = lax.all_gather(proj, "col", axis=0, tiled=True)
    return lax.all_gather(along_col, "row", axis=0, tiled=True)


def inside(places, bins_total):
    return ((places >= 0) & (places < bins_total)).astype(jnp.float32)


def tap_groups(padded, weights, dilation):
    out_channels = weights.shape[1]
    in_channels = weights.shape[2]
    row_count = padded.shape[1] - 2 * MAXDIL
    col_count = padded.shape[2] - 2 * MAXDIL
    zero_index = jnp.zeros((), jnp.int32)
    summed = jnp.zeros((out_channels, row_count * col_count), jnp.float32)
    for group_index in range(3):
        row_step = group_index - 1
        pieces = []
        for inner_index in range(3):
            col_step = inner_index - 1
            row_index = MAXDIL + row_step * dilation
            col_index = MAXDIL + col_step * dilation
            pieces.append(
                lax.dynamic_slice(
                    padded, (zero_index, row_index, col_index), (in_channels, row_count, col_count)
                )
            )
        stacked = jnp.concatenate(pieces, axis=0).reshape(3 * in_channels, row_count * col_count)
        group_weight = jnp.transpose(
            weights[3 * group_index : 3 * group_index + 3], (1, 0, 2)
        ).reshape(out_channels, 3 * in_channels)
        summed = summed + jnp.dot(group_weight, stacked, preferred_element_type=jnp.float32)
    return summed.reshape(out_channels, row_count, col_count)


def mirrored_taps(weights):
    return weights.reshape(3, 3, *weights.shape[1:]).swapaxes(0, 1).reshape(weights.shape)


def first_layer(every, taps, shift_bias, dilation, row_start, rows, col_start, cols):
    bins_total = every.shape[0]
    half = every.shape[1] // 2
    active = jnp.pad(jax.nn.relu(every), ((REACH, REACH), (0, 0)))
    row_part = jnp.einsum(
        "nk,tok->tno", active[:, :half], taps[:, :, :half], preferred_element_type=jnp.float32
    )
    col_part = jnp.einsum(
        "nk,tok->tno", active[:, half:], taps[:, :, half:], preferred_element_type=jnp.float32
    )
    span = bins_total + 2 * MAXDIL
    by_col, by_row = [], []
    for outer in range(3):
        along_rows = None
        along_cols = None
        for inner in range(3):
            piece_r = lax.dynamic_slice_in_dim(
                row_part[3 * inner + outer], MAXDIL + (inner - 1) * dilation, span, 0
            )
            piece_c = lax.dynamic_slice_in_dim(
                col_part[3 * outer + inner], MAXDIL + (inner - 1) * dilation, span, 0
            )
            along_rows = piece_r if along_rows is None else along_rows + piece_r
            along_cols = piece_c if along_cols is None else along_cols + piece_c
        by_col.append(along_rows)
        by_row.append(along_cols)

    def at(table, start, count):
        return lax.dynamic_slice_in_dim(table, start, count, 0)

    row_places = row_start - MAXDIL + jnp.arange(rows)
    col_places = col_start - MAXDIL + jnp.arange(cols)

    def conv_at(p_start, p_places, q_start, q_places, p_count, q_count, p_axis):
        total = None
        for step in range(3):
            q_in = inside(q_places + (step - 1) * dilation, bins_total)
            p_in = inside(p_places + (step - 1) * dilation, bins_total)
            term_p = at(by_col[step], p_start, p_count).T
            term_q = at(by_row[step], q_start, q_count).T
            if p_axis == 1:
                piece = term_p[:, :, None] * q_in[None, None, :] + term_q[:, None, :] * p_in[
                    None, :, None
                ]
            else:
                piece = term_p[:, None, :] * q_in[None, :, None] + term_q[:, :, None] * p_in[
                    None, None, :
                ]
            total = piece if total is None else total + piece
        return total

    padded = jnp.pad(every, ((MAXDIL, MAXDIL), (0, 0)))
    rows_here = at(padded, row_start, rows)
    cols_here = at(padded, col_start, cols)
    shape = (half, rows, cols)
    map0 = jnp.concatenate(
        [
            jnp.broadcast_to(rows_here[:, :half].T[:, :, None], shape),
            jnp.broadcast_to(cols_here[:, half:].T[:, None, :], shape),
        ],
        axis=0,
    )
    map0_mirror = jnp.concatenate(
        [
            jnp.broadcast_to(cols_here[:, :half].T[:, None, :], shape),
            jnp.broadcast_to(rows_here[:, half:].T[:, :, None], shape),
        ],
        axis=0,
    )
    bias = shift_bias[:, None, None]
    conv = conv_at(row_start, row_places, col_start, col_places, rows, cols, 1)
    conv_mirror = conv_at(col_start, col_places, row_start, row_places, cols, rows, 2)
    mixed = (map0.astype(jnp.float32) + bias + conv).astype(jnp.bfloat16)
    mixed_mirror = (map0_mirror.astype(jnp.float32) + bias + conv_mirror).astype(jnp.bfloat16)
    return mixed, mixed_mirror, row_places, col_places


def local(features, row_weight, col_weight, conv_weight, conv_bias, dilations):
    both = jnp.concatenate([row_weight, col_weight], axis=1)
    proj = jnp.dot(features, both, preferred_element_type=jnp.float32).astype(jnp.bfloat16)
    every = gather_projections(proj)
    bins_total = every.shape[0]
    row_size = bins_total // lax.axis_size("row")
    col_size = bins_total // lax.axis_size("col")
    row_start = lax.axis_index("row") * row_size
    col_start = lax.axis_index("col") * col_size
    rows1 = row_size + 2 * MAXDIL
    cols1 = col_size + 2 * MAXDIL

    mixed0, mixed0_mirror, row_places, col_places = first_layer(
        every, conv_weight[0], conv_bias[0], dilations[0], row_start, rows1, col_start, cols1
    )
    map1 = (0.5 * (mixed0.astype(jnp.float32) + mixed0_mirror.astype(jnp.float32))).astype(
        jnp.bfloat16
    )

    mask1 = (
        inside(row_places, bins_total)[:, None] * inside(col_places, bins_total)[None, :]
    ).astype(jnp.bfloat16)
    taps1 = jnp.concatenate([conv_weight[1], mirrored_taps(conv_weight[1])], axis=1)
    conv1 = tap_groups(jax.nn.relu(map1) * mask1, taps1, dilations[1])
    channels = conv_weight.shape[2]
    core = (slice(None), slice(MAXDIL, MAXDIL + row_size), slice(MAXDIL, MAXDIL + col_size))
    base1 = map1[core].astype(jnp.float32) + conv_bias[1][:, None, None]
    mixed1 = (base1 + conv1[:channels]).astype(jnp.bfloat16)
    mixed1_mirror = (base1 + conv1[channels:]).astype(jnp.bfloat16)
    return (0.5 * (mixed1.astype(jnp.float32) + mixed1_mirror.astype(jnp.float32))).astype(
        jnp.bfloat16
    )


def solution(mesh):
    placed = (P(("row", "col"), None), P(), P(), P(), P(), P())
    return jax.shard_map(
        local, mesh=mesh, in_specs=placed, out_specs=P(None, "row", "col"), check_vma=False
    )
```

profile of v0, /device:TPU:1, one launch (start us, length us, event | category | flops | bytes accessed | tf_op | source)
XLA Modules:
  0.0 100.5 jit_solution(16029481936310377751)
XLA Ops:
  0.0 0.8 slice_bitcast_fusion.2
  0.8 1.3 %fusion.39 = (s32[1]{0:T(128)}, s32[1]{0:T(128)}) fusion(s32[2]{0:T(128)} %param.11), kind=kLoop, calls=%fused_computation.104 | loop fusion | bytes 16 | tf_op jit(solution)/shard_map/slice | solution.py:150
  6.6 0.6 and_convert_fusion
  7.2 0.6 and_convert_fusion.1
  7.9 0.8 fusion.9
  8.7 20.5 %all_gather.6 = bf16[64,64]{1,0:T(8,128)(2,1)S(1)} all-gather(bf16[8,64]{1,0:T(8,128)(2,1)S(1)} %fusion.9), channel_id=1, replica_groups=mesh['row'=16,'col'=8] {'col'}, dimensions={0}, use_global_device_ids=true | all-gather | bytes 9216 | tf_op jit(solution)/shard_map/all_gather | solution.py:11
  29.3 30.9 %all_gather.7 = bf16[1024,64]{1,0:T(8,128)(2,1)S(1)} all-gather(bf16[64,64]{1,0:T(8,128)(2,1)S(1)} %all_gather.6), channel_id=1, replica_groups=mesh['row'=16,'col'=8] {'row'}, dimensions={0}, use_global_device_ids=true | all-gather | bytes 139264 | tf_op jit(solution)/shard_map/all_gather | solution.py:12
  60.8 1.0 %fusion.38 = (bf16[1,9,64,64]{3,2,1,0:T(8,128)(2,1)S(1)}, bf16[1,9,64,64]{3,2,1,0:T(8,128)(2,1)S(1)}) fusion(bf16[2,9,64,64]{3,2,1,0:T(8,128)(2,1)} %param.9), kind=kLoop, calls=%fused_computation.103 | loop fusion | bytes 294912 | tf_op jit(solution)/shard_map/slice | solution.py:140
  62.6 0.4 broadcast_in_dim.11
  63.4 0.6 convolution_bitcast_fusion
  64.1 0.8 fusion.14
  65.1 0.6 convolution_bitcast_fusion.1
  65.8 0.8 fusion.15
  67.0 8.5 %maximum_multiply_fusion = (bf16[64,72,136]{2,1,0:T(8,128)(2,1)S(1)}, bf16[64,72,136]{2,1,0:T(8,128)(2,1)S(1)}) fusion(bf16[72,136]{1,0:T(8,128)(2,1)S(1)} %multiply_convert_fusion.2, f32[64,72]{1,0:T(8,128)S(1)} %get-tuple-element.55, f32[64,136]{1,0:T(8,128)S(1)} %get-tuple-element.61, f32[64,72]{1,0:T(8,128)S(1)} %get-tuple-element.56, ...), kind=kLoop, calls=%fused_computation.17 | loop fusion | flops 24440832 | bytes 5355328 | tf_op jit(solution)/shard_map/mul | solution.py:150
  75.5 13.2 %constant_dynamic-slice_fusion.5 = (bf16[64,64,128]{2,1,0:T(8,128)(2,1)S(1)}, bf16[64,64,128]{2,1,0:T(8,128)(2,1)S(1)}, bf16[64,64,128]{2,1,0:T(8,128)(2,1)S(1)}...) fusion(bf16[64,72,136]{2,1,0:T(8,128)(2,1)S(1)} %get-tuple-elem, ...), kind=kLoop, calls=%fused_computation.85 | loop fusion | bytes 18874384 | tf_op jit(solution)/shard_map/dynamic_slice | solution.py:34
  88.7 0.4 pad_maximum_fusion.2
  89.1 0.4 pad_maximum_fusion.1
  89.5 0.6 pad_maximum_fusion
  90.1 2.2 %fusion.4 = f32[128,8192]{1,0:T(8,128)S(1)} fusion(bf16[128,192]{0,1:T(8,128)(2,1)S(1)} %bitcast.137, bf16[24,8,64,128]{3,2,1,0:T(8,128)(2,1)S(1)} %bitcast.127), kind=kOutput, calls=%fused_computation.11 | convolution fusion | flops 402653184 | bytes 7389184 | tf_op jit(solution)/shard_map/dot_general | solution.py:42
  92.3 2.3 %convolution_add_fusion.1 = f32[128,8192]{1,0:T(8,128)S(1)} fusion(f32[128,8192]{1,0:T(8,128)S(1)} %fusion.4, bf16[128,192]{0,1:T(8,128)(2,1)S(1)} %bitcast.136, bf16[24,8,64,128]{3,2,1,0:T(8,128)(2,1)S(1)} %bitcast.129), kind=kOutput, calls=%fused_computation.1 | convolution fusion | flops 403701760 | bytes 11583488 | tf_op jit(solution)/shard_map/dot_general | solution.py:42
  94.6 2.3 %convolution_add_fusion = f32[128,8192]{1,0:T(8,128)S(1)} fusion(f32[128,8192]{1,0:T(8,128)S(1)} %convolution_add_fusion.1, bf16[128,192]{0,1:T(8,128)(2,1)S(1)} %bitcast.135, bf16[24,8,64,128]{3,2,1,0:T(8,128)(2,1)S(1)} %bitcast.128), kind=kOutput, calls=%fused_computation | convolution fusion | flops 403701760 | bytes 11583488 | tf_op jit(solution)/shard_map/dot_general | solution.py:42
  97.3 0.4 copy.35
  97.7 0.4 copy.34
  98.1 2.5 %multiply_convert_fusion.1 = bf16[64,64,128]{2,1,0:T(8,128)(2,1)} fusion(f32[8,8,64,128]{3,2,1,0:T(8,128)S(1)} %copy.34, f32[8,8,64,128]{3,2,1,0:T(8,128)S(1)} %copy.35, bf16[64,72,136]{2,1,0:T(8,128)(2,1)S(1)} %get-tuple-element.6, f32[64]{0:T(128)S(1)} %get-tuple-element.45), kind=kLoop, calls=%fused_computation.24 | loop fusion | flops 5767168 | bytes 6291712 | tf_op jit(solution)/shard_map/convert_element_type | solution.py:156
  (28 shorter events, 3.0 us)
Async XLA Ops:
  0.0 7.9 %copy-start = (bf16[8,128]{1,0:T(8,128)(2,1)S(1)}, bf16[8,128]{1,0:T(8,128)(2,1)}, u32[]{:S(2)}) copy-start(bf16[8,128]{1,0:T(8,128)(2,1)} %param.6) | copy-start | bytes 6148
where the time goes:
time: 101 us
  blocking collectives  51.4 us (51%)
  local copies, waits for them, and re-layouts  20.2 us (20%)
  other arithmetic  15.4 us (15%)
  matrix products  8.81 us (9%)
  between operations  4.75 us (5%)
    all_gather x1, blocking collectives, gather_projections(): return lax.all_gather(along_col, 'row', axis=0, tiled=True)  30.9 us
    all_gather x1, blocking collectives, gather_projections(): along_col = lax.all_gather(proj, 'col', axis=0, tiled=True)  20.5 us
    dynamic_slice x1, local copies, waits for them, and re-layouts, tap_groups(): lax.dynamic_slice(padded, (zero_index, row_index, col_index), (in_channel...  13.2 us
    mul x1, other arithmetic, local(): conv1 = tap_groups(jax.nn.relu(map1) * mask1, taps1, dilations[1])  8.49 us
    dot_general x3, matrix products, tap_groups(): jnp.dot(group_weight, stacked, preferred_element_type=jnp.float32)  6.78 us
    convert_element_type x1, other arithmetic, local(): (0.5 * (mixed1.astype(jnp.float32) + mixed1_mirror.astype(jnp.float32)))....  2.48 us

commit v1 on v0

--- a/solution.py
+++ b/solution.py
@@ -8,8 +8,10 @@
 
 
 def gather_projections(proj):
-    along_col = lax.all_gather(proj, "col", axis=0, tiled=True)
-    return lax.all_gather(along_col, "row", axis=0, tiled=True)
+    axes = ("row", "col")
+    count = lax.axis_size("row") * lax.axis_size("col")
+    copies = jnp.broadcast_to(proj[None], (count,) + proj.shape)
+    return lax.all_to_all(copies, axes, 0, 0, tiled=True).reshape(-1, proj.shape[1])
 
 
 def inside(places, bins_total):

time: 101 us -> 63.4 us (0.63)
  blocking collectives: 51.4 us -> 0 us
  starting transfers between devices: 0 us -> 11.5 us
  local copies, waits for them, and re-layouts: 20.2 us -> 22.4 us
    all_gather x2 -> x0, blocking collectives: 51.4 us -> none  [the longest x1 30.9 us: gather_projections(): return lax.all_gather(along_col, 'row', axis=0, tiled=True)]
    all_to_all x0 -> x1, starting transfers between devices: none -> 11.5 us  [gather_projections(): lax.all_to_all(copies, axes, 0, 0, tiled=True).reshape(-1, proj.shape[1])]
    unnamed x7 -> x9, local copies, waits for them, and re-layouts: 1.44 us -> 3.2 us
  transfers between devices with their start and end apart: 0 -> 1, of which waited for: 0 -> 1; matrix products, arithmetic and copies ran while one was open for 0% -> 8% of each run, Pallas kernels for 0% -> 0%
where the time goes in v1:
time: 63.4 us; the launch traced here: 63.1 us
  local copies, waits for them, and re-layouts  22.4 us (35%)
  other arithmetic  15.2 us (24%)
  starting transfers between devices  11.5 us (18%)
  matrix products  8.77 us (14%)
  between operations  4.95 us (8%)
    dynamic_slice x1, local copies, waits for them, and re-layouts, tap_groups(): lax.dynamic_slice(padded, (zero_index, row_index, col_index), (in_channel...  13.4 us
    all_to_all x1, starting transfers between devices, gather_projections(): lax.all_to_all(copies, axes, 0, 0, tiled=True).reshape(-1, proj.shape[1])  11.5 us
    mul x1, other arithmetic, local(): conv1 = tap_groups(jax.nn.relu(map1) * mask1, taps1, dilations[1])  8.35 us
    dot_general x3, matrix products, tap_groups(): jnp.dot(group_weight, stacked, preferred_element_type=jnp.float32)  6.78 us
    unnamed x9, local copies, waits for them, and re-layouts  3.2 us
    convert_element_type x1, other arithmetic, local(): (0.5 * (mixed1.astype(jnp.float32) + mixed1_mirror.astype(jnp.float32)))....  2.48 us
    concatenate x3, other arithmetic, tap_groups(): jnp.concatenate(pieces, axis=0)  1.4 us
    slice x1, local copies, waits for them, and re-layouts, local(): conv1 = tap_groups(jax.nn.relu(map1) * mask1, taps1, dilations[1])  1.39 us
  transfers between devices with their start and end apart: 1, of which 1 were waited for; matrix products, arithmetic and copies ran while one was open for 8% of the time, Pallas kernels for 0%

profile of v1, /device:TPU:1, one launch (start us, length us, event | category | flops | bytes accessed | tf_op | source)
XLA Modules:
  0.0 63.1 jit_solution(5453691370660003131)
XLA Ops:
  0.0 0.7 %copy-done = bf16[8,128]{1,0:T(8,128)(2,1)S(1)} copy-done((bf16[8,128]{1,0:T(8,128)(2,1)S(1)}, bf16[8,128]{1,0:T(8,128)(2,1)}, u32[]{:S(2)}) %copy-start) | copy-done | bytes 2072
  0.7 0.8 %fusion.9 = bf16[8,64]{1,0:T(8,128)(2,1)S(1)} fusion(bf16[8,128]{1,0:T(8,128)(2,1)S(1)} %copy-done, bf16[128,32]{0,1:T(8,128)(2,1)} %param.8, bf16[128,32]{0,1:T(8,128)(2,1)} %param.7), kind=kOutput, calls=%fused_computation.27 | convolution fusion | flops 164352 | bytes 19456 | tf_op jit(solution)/shard_map/dot_general | solution.py:131
  1.6 0.9 %reshape.200 = bf16[128,2,256]{2,1,0:T(2,128)(2,1)} reshape(bf16[128,8,64]{2,1,0:T(8,128)(2,1)S(1)} %broadcast_in_dim.10) | data formatting | bytes 262144
  2.4 11.5 %all-to-all-start = ((bf16[128,2,256]{2,1,0:T(2,128)(2,1)}), bf16[128,2,256]{2,1,0:T(2,128)(2,1)S(1)}, u32[]{:S(2)}, u32[]{:S(2)}) async-start(bf16[128,2,256]{2,1,0:T(2,128)(2,1)} %reshape.200), calls=%async_computation | async-start | bytes 262144 | tf_op jit(solution)/shard_map/all_to_all | solution.py:14
  13.9 0.8 %slice_bitcast_fusion.2 = (f32[64]{0:T(128)S(1)}, f32[64]{0:T(128)S(1)}) fusion(f32[2,64]{1,0:T(2,128)} %param.10), kind=kLoop, calls=%fused_computation.93 | loop fusion | bytes 1024 | tf_op jit(solution)/shard_map/add | solution.py:155
  14.7 1.4 %fusion.37 = (s32[1]{0:T(128)}, s32[1]{0:T(128)}) fusion(s32[2]{0:T(128)} %param.11), kind=kLoop, calls=%fused_computation.102 | loop fusion | bytes 16 | tf_op jit(solution)/shard_map/slice | solution.py:152
  16.7 0.6 and_convert_fusion.1
  17.4 0.6 and_convert_fusion
  18.0 1.0 %fusion.36 = (bf16[1,9,64,64]{3,2,1,0:T(8,128)(2,1)S(1)}, bf16[1,9,64,64]{3,2,1,0:T(8,128)(2,1)S(1)}) fusion(bf16[2,9,64,64]{3,2,1,0:T(8,128)(2,1)} %param.9), kind=kLoop, calls=%fused_computation.101 | loop fusion | bytes 294912 | tf_op jit(solution)/shard_map/slice | solution.py:142
  24.6 0.6 convolution_bitcast_fusion
  25.3 0.8 %fusion.14 = (f32[1,1032,64]{1,2,0:T(8,128)S(1)}, f32[1,1032,64]{1,2,0:T(8,128)S(1)}, f32[1,1032,64]{1,2,0:T(8,128)S(1)}) fusion(f32[9,1040,64]{1,2,0:T(8,128)S(1)} %convolution_bitcast_fusion, f32[1,1040,64]{1,2,0:T(8,128)S(1)} %get-tuple-element.26, s32[]{:T(128)S(6)} %select_n.19, f32[1,1040,64]{1,2,0:T(8,128)S(1)} %get-tuple-element.21, ...), kind=kLoop, calls=%fused_computation.37 | loop fusion | flops 396288 | bytes 3170312 | tf_op jit(solution)/shard_map/add | solution.py:75
  26.3 0.6 convolution_bitcast_fusion.1
  27.0 0.8 %fusion.15 = (f32[1,1032,64]{1,2,0:T(8,128)S(1)}, f32[1,1032,64]{1,2,0:T(8,128)S(1)}, f32[1,1032,64]{1,2,0:T(8,128)S(1)}) fusion(f32[9,1040,64]{1,2,0:T(8,128)S(1)} %convolution_bitcast_fusion.1, f32[1,1040,64]{1,2,0:T(8,128)S(1)} %get-tuple-element.17, s32[]{:T(128)S(6)} %select_n.19, f32[1,1040,64]{1,2,0:T(8,128)S(1)} %get-tuple-element.12, ...), kind=kLoop, calls=%fused_computation.39 | loop fusion | flops 396288 | bytes 3170312 | tf_op jit(solution)/shard_map/add | solution.py:74
  29.4 8.3 %maximum_multiply_fusion = (bf16[64,72,136]{2,1,0:T(8,128)(2,1)S(1)}, bf16[64,72,136]{2,1,0:T(8,128)(2,1)S(1)}) fusion(bf16[72,136]{1,0:T(8,128)(2,1)S(1)} %multiply_convert_fusion.2, f32[64,72]{1,0:T(8,128)S(1)} %get-tuple-element.55, f32[64,136]{1,0:T(8,128)S(1)} %get-tuple-element.61, f32[64,72]{1,0:T(8,128)S(1)} %get-tuple-element.56, ...), kind=kLoop, calls=%fused_computation.17 | loop fusion | flops 24440832 | bytes 5355328 | tf_op jit(solution)/shard_map/mul | solution.py:152
  37.8 13.4 %constant_dynamic-slice_fusion.5 = (bf16[64,64,128]{2,1,0:T(8,128)(2,1)S(1)}, bf16[64,64,128]{2,1,0:T(8,128)(2,1)S(1)}, bf16[64,64,128]{2,1,0:T(8,128)(2,1)S(1)}...) fusion(bf16[64,72,136]{2,1,0:T(8,128)(2,1)S(1)} %get-tuple-elem, ...), kind=kLoop, calls=%fused_computation.83 | loop fusion | bytes 18874384 | tf_op jit(solution)/shard_map/dynamic_slice | solution.py:36
  51.2 0.4 pad_maximum_fusion
  51.6 2.2 %fusion.4 = f32[128,8192]{1,0:T(8,128)S(1)} fusion(bf16[128,192]{0,1:T(8,128)(2,1)S(1)} %bitcast.141, bf16[24,8,64,128]{3,2,1,0:T(8,128)(2,1)S(1)} %bitcast.128), kind=kOutput, calls=%fused_computation.11 | convolution fusion | flops 402653184 | bytes 7389184 | tf_op jit(solution)/shard_map/dot_general | solution.py:44
  53.8 0.4 pad_maximum_fusion.2
  54.2 0.6 pad_maximum_fusion.1
  54.8 2.3 %convolution_add_fusion.1 = f32[128,8192]{1,0:T(8,128)S(1)} fusion(f32[128,8192]{1,0:T(8,128)S(1)} %fusion.4, bf16[128,192]{0,1:T(8,128)(2,1)S(1)} %bitcast.140, bf16[24,8,64,128]{3,2,1,0:T(8,128)(2,1)S(1)} %bitcast.130), kind=kOutput, calls=%fused_computation.1 | convolution fusion | flops 403701760 | bytes 11583488 | tf_op jit(solution)/shard_map/dot_general | solution.py:44
  57.1 2.3 %convolution_add_fusion = f32[128,8192]{1,0:T(8,128)S(1)} fusion(f32[128,8192]{1,0:T(8,128)S(1)} %convolution_add_fusion.1, bf16[128,192]{0,1:T(8,128)(2,1)S(1)} %bitcast.139, bf16[24,8,64,128]{3,2,1,0:T(8,128)(2,1)S(1)} %bitcast.129), kind=kOutput, calls=%fused_computation | convolution fusion | flops 403701760 | bytes 11583488 | tf_op jit(solution)/shard_map/dot_general | solution.py:44
  59.8 0.4 copy.25
  60.2 0.4 copy.24
  60.6 2.5 %multiply_convert_fusion.1 = bf16[64,64,128]{2,1,0:T(8,128)(2,1)} fusion(f32[8,8,64,128]{3,2,1,0:T(8,128)S(1)} %copy.24, f32[8,8,64,128]{3,2,1,0:T(8,128)S(1)} %copy.25, bf16[64,72,136]{2,1,0:T(8,128)(2,1)S(1)} %get-tuple-element.6, f32[64]{0:T(128)S(1)} %get-tuple-element.45), kind=kLoop, calls=%fused_computation.24 | loop fusion | flops 5767168 | bytes 6291712 | tf_op jit(solution)/shard_map/convert_element_type | solution.py:158
  (32 shorter events, 4.0 us)
Async XLA Ops:
  0.0 0.7 %copy-start = (bf16[8,128]{1,0:T(8,128)(2,1)S(1)}, bf16[8,128]{1,0:T(8,128)(2,1)}, u32[]{:S(2)}) copy-start(bf16[8,128]{1,0:T(8,128)(2,1)} %param.6) | copy-start | bytes 6148
  2.4 21.6 %all-to-all-start = ((bf16[128,2,256]{2,1,0:T(2,128)(2,1)}), bf16[128,2,256]{2,1,0:T(2,128)(2,1)S(1)}, u32[]{:S(2)}, u32[]{:S(2)}) async-start(bf16[128,2,256]{2,1,0:T(2,128)(2,1)} %reshape.200), calls=%async_computation | async-start | bytes 262144 | tf_op jit(solution)/shard_map/all_to_all | solution.py:14

commit v2 on v1

--- a/solution.py
+++ b/solution.py
@@ -21,28 +21,21 @@
 def tap_groups(padded, weights, dilation):
     out_channels = weights.shape[1]
     in_channels = weights.shape[2]
-    row_count = padded.shape[1] - 2 * MAXDIL
-    col_count = padded.shape[2] - 2 * MAXDIL
+    row_count = padded.shape[0] - 2 * MAXDIL
+    col_count = padded.shape[1] - 2 * MAXDIL
     zero_index = jnp.zeros((), jnp.int32)
-    summed = jnp.zeros((out_channels, row_count * col_count), jnp.float32)
-    for group_index in range(3):
-        row_step = group_index - 1
-        pieces = []
-        for inner_index in range(3):
-            col_step = inner_index - 1
-            row_index = MAXDIL + row_step * dilation
-            col_index = MAXDIL + col_step * dilation
-            pieces.append(
-                lax.dynamic_slice(
-                    padded, (zero_index, row_index, col_index), (in_channels, row_count, col_count)
-                )
-            )
-        stacked = jnp.concatenate(pieces, axis=0).reshape(3 * in_channels, row_count * col_count)
-        group_weight = jnp.transpose(
-            weights[3 * group_index : 3 * group_index + 3], (1, 0, 2)
-        ).reshape(out_channels, 3 * in_channels)
-        summed = summed + jnp.dot(group_weight, stacked, preferred_element_type=jnp.float32)
-    return summed.reshape(out_channels, row_count, col_count)
+    pieces = []
+    for tap in range(9):
+        row_index = MAXDIL + (tap // 3 - 1) * dilation
+        col_index = MAXDIL + (tap % 3 - 1) * dilation
+        piece = lax.dynamic_slice(
+            padded, (row_index, col_index, zero_index), (row_count, col_count, in_channels)
+        )
+        pieces.append(piece.reshape(row_count * col_count, in_channels))
+    stacked = jnp.concatenate(pieces, axis=1)
+    flat_weight = jnp.transpose(weights, (0, 2, 1)).reshape(9 * in_channels, out_channels)
+    summed = jnp.dot(stacked, flat_weight, preferred_element_type=jnp.float32)
+    return summed.reshape(row_count, col_count, out_channels)
 
 
 def mirrored_taps(weights):
@@ -87,15 +80,15 @@
         for step in range(3):
             q_in = inside(q_places + (step - 1) * dilation, bins_total)
             p_in = inside(p_places + (step - 1) * dilation, bins_total)
-            term_p = at(by_col[step], p_start, p_count).T
-            term_q = at(by_row[step], q_start, q_count).T
-            if p_axis == 1:
-                piece = term_p[:, :, None] * q_in[None, None, :] + term_q[:, None, :] * p_in[
-                    None, :, None
+            term_p = at(by_col[step], p_start, p_count)
+            term_q = at(by_row[step], q_start, q_count)
+            if p_axis == 0:
+                piece = term_p[:, None, :] * q_in[None, :, None] + term_q[None, :, :] * p_in[
+                    :, None, None
                 ]
             else:
-                piece = term_p[:, None, :] * q_in[None, :, None] + term_q[:, :, None] * p_in[
-                    None, None, :
+                piece = term_p[None, :, :] * q_in[:, None, None] + term_q[:, None, :] * p_in[
+                    None, :, None
                 ]
             total = piece if total is None else total + piece
         return total
@@ -103,24 +96,12 @@
     padded = jnp.pad(every, ((MAXDIL, MAXDIL), (0, 0)))
     rows_here = at(padded, row_start, rows)
     cols_here = at(padded, col_start, cols)
-    shape = (half, rows, cols)
-    map0 = jnp.concatenate(
-        [
-            jnp.broadcast_to(rows_here[:, :half].T[:, :, None], shape),
-            jnp.broadcast_to(cols_here[:, half:].T[:, None, :], shape),
-        ],
-        axis=0,
-    )
-    map0_mirror = jnp.concatenate(
-        [
-            jnp.broadcast_to(cols_here[:, :half].T[:, None, :], shape),
-            jnp.broadcast_to(rows_here[:, half:].T[:, :, None], shape),
-        ],
-        axis=0,
-    )
-    bias = shift_bias[:, None, None]
-    conv = conv_at(row_start, row_places, col_start, col_places, rows, cols, 1)
-    conv_mirror = conv_at(col_start, col_places, row_start, row_places, cols, rows, 2)
+    lower = jnp.arange(every.shape[1]) < half
+    map0 = jnp.where(lower, rows_here[:, None, :], cols_here[None, :, :])
+    map0_mirror = jnp.where(lower, cols_here[None, :, :], rows_here[:, None, :])
+    bias = shift_bias[None, None, :]
+    conv = conv_at(row_start, row_places, col_start, col_places, rows, cols, 0)
+    conv_mirror = conv_at(col_start, col_places, row_start, row_places, cols, rows, 1)
     mixed = (map0.astype(jnp.float32) + bias + conv).astype(jnp.bfloat16)
     mixed_mirror = (map0_mirror.astype(jnp.float32) + bias + conv_mirror).astype(jnp.bfloat16)
     return mixed, mixed_mirror, row_places, col_places
@@ -146,18 +127,19 @@
     )
 
     mask1 = (
-        inside(row_places, bins_total)[:, None] * inside(col_places, bins_total)[None, :]
+        inside(row_places, bins_total)[:, None, None] * inside(col_places, bins_total)[None, :, None]
     ).astype(jnp.bfloat16)
     taps1 = jnp.concatenate([conv_weight[1], mirrored_taps(conv_weight[1])], axis=1)
     conv1 = tap_groups(jax.nn.relu(map1) * mask1, taps1, dilations[1])
     channels = conv_weight.shape[2]
-    core = (slice(None), slice(MAXDIL, MAXDIL + row_size), slice(MAXDIL, MAXDIL + col_size))
-    base1 = map1[core].astype(jnp.float32) + conv_bias[1][:, None, None]
-    mixed1 = (base1 + conv1[:channels]).astype(jnp.bfloat16)
-    mixed1_mirror = (base1 + conv1[channels:]).astype(jnp.bfloat16)
-    return (0.5 * (mixed1.astype(jnp.float32) + mixed1_mirror.astype(jnp.float32))).astype(
+    core = (slice(MAXDIL, MAXDIL + row_size), slice(MAXDIL, MAXDIL + col_size), slice(None))
+    base1 = map1[core].astype(jnp.float32) + conv_bias[1][None, None, :]
+    mixed1 = (base1 + conv1[:, :, :channels]).astype(jnp.bfloat16)
+    mixed1_mirror = (base1 + conv1[:, :, channels:]).astype(jnp.bfloat16)
+    pair = (0.5 * (mixed1.astype(jnp.float32) + mixed1_mirror.astype(jnp.float32))).astype(
         jnp.bfloat16
     )
+    return jnp.transpose(pair, (2, 0, 1))
 
 
 def solution(mesh):

time: 63.4 us -> 46.8 us (0.74)
  local copies, waits for them, and re-layouts: 22.4 us -> 14.8 us
  matrix products: 8.77 us -> 3.85 us
  other arithmetic: 15.2 us -> 11 us
    dynamic_slice x1 -> x15, local copies, waits for them, and re-layouts: 13.4 us -> 1.2 us  [at(): return lax.dynamic_slice_in_dim(table, start, count, 0)]
    dot_general x3 -> x1, matrix products: 6.78 us -> 1.85 us  [tap_groups(): summed = jnp.dot(stacked, flat_weight, preferred_element_type=jnp.float32)]
    unnamed x9 -> x13, local copies, waits for them, and re-layouts: 3.2 us -> 7.52 us
    convert_element_type x2 -> x1, other arithmetic: 2.55 us -> 0.08 us  [local(): mask1 = (inside(row_places, bins_total)[:, None, None] * inside(col_place...]
    concatenate x4 -> x0, other arithmetic: 1.51 us -> none  [the longest x3 1.4 us: tap_groups(): jnp.concatenate(pieces, axis=0)]
    mul x1, other arithmetic: 8.35 us -> 7.18 us  [local(): conv1 = tap_groups(jax.nn.relu(map1) * mask1, taps1, dilations[1])]
    squeeze x0 -> x1, local copies, waits for them, and re-layouts: none -> 1.06 us  [local(): conv_weight[1]]
    slice x1 -> x0, local copies, waits for them, and re-layouts: 1 us -> none  [local(): conv_weight[0]]
  transfers between devices with their start and end apart: 1 -> 1, of which waited for: 1 -> 1; matrix products, arithmetic and copies ran while one was open for 8% -> 11% of each run, Pallas kernels for 0% -> 0%
where the time goes in v2:
time: 46.8 us; the launch traced here: 46.4 us
  local copies, waits for them, and re-layouts  14.8 us (32%)
  starting transfers between devices  11.5 us (25%)
  other arithmetic  11 us (24%)
  between operations  4.68 us (10%)
  matrix products  3.85 us (8%)
  waiting for transfers between devices  0.62 us (1%)
    all_to_all x1, starting transfers between devices, gather_projections(): lax.all_to_all(copies, axes, 0, 0, tiled=True).reshape(-1, proj.shape[1])  11.5 us
    unnamed x13, local copies, waits for them, and re-layouts  7.52 us
    mul x1, other arithmetic, local(): conv1 = tap_groups(jax.nn.relu(map1) * mask1, taps1, dilations[1])  7.18 us
    dot_general x1, matrix products, tap_groups(): summed = jnp.dot(stacked, flat_weight, preferred_element_type=jnp.float32)  1.85 us
    transpose x1, local copies, waits for them, and re-layouts, local(): return jnp.transpose(pair, (2, 0, 1))  1.65 us
    convert_element_type x4, other arithmetic, inside(): return ((places >= 0) & (places < bins_total)).astype(jnp.float32)  1.4 us
    slice x1, local copies, waits for them, and re-layouts, local(): conv1 = tap_groups(jax.nn.relu(map1) * mask1, taps1, dilations[1])  1.32 us
    dynamic_slice x15, local copies, waits for them, and re-layouts, at(): return lax.dynamic_slice_in_dim(table, start, count, 0)  1.2 us
  transfers between devices with their start and end apart: 1, of which 1 were waited for; matrix products, arithmetic and copies ran while one was open for 11% of the time, Pallas kernels for 0%

profile of v2, /device:TPU:1, one launch (start us, length us, event | category | flops | bytes accessed | tf_op | source)
XLA Modules:
  0.0 46.4 jit_solution(10786741189769103846)
XLA Ops:
  0.0 0.7 %copy-done = bf16[8,128]{1,0:T(8,128)(2,1)S(1)} copy-done((bf16[8,128]{1,0:T(8,128)(2,1)S(1)}, bf16[8,128]{1,0:T(8,128)(2,1)}, u32[]{:S(2)}) %copy-start) | copy-done | bytes 2072
  0.7 0.8 %fusion.2 = bf16[8,64]{1,0:T(8,128)(2,1)S(1)} fusion(bf16[8,128]{1,0:T(8,128)(2,1)S(1)} %copy-done, bf16[128,32]{0,1:T(8,128)(2,1)} %param.8, bf16[128,32]{0,1:T(8,128)(2,1)} %param.7), kind=kOutput, calls=%fused_computation.13 | convolution fusion | flops 164352 | bytes 19456 | tf_op jit(solution)/shard_map/dot_general | solution.py:112
  1.6 0.9 %reshape.179 = bf16[128,2,256]{2,1,0:T(2,128)(2,1)} reshape(bf16[128,8,64]{2,1,0:T(8,128)(2,1)S(1)} %broadcast_in_dim.39) | data formatting | bytes 262144
  2.4 11.5 %all-to-all-start = ((bf16[128,2,256]{2,1,0:T(2,128)(2,1)}), bf16[128,2,256]{2,1,0:T(2,128)(2,1)S(1)}, u32[]{:S(2)}, u32[]{:S(2)}) async-start(bf16[128,2,256]{2,1,0:T(2,128)(2,1)} %reshape.179), calls=%async_computation | async-start | bytes 262144 | tf_op jit(solution)/shard_map/all_to_all | solution.py:14
  14.0 0.8 %slice_bitcast_fusion = (f32[64]{0:T(128)S(1)}, f32[64]{0:T(128)S(1)}) fusion(f32[2,64]{1,0:T(2,128)} %param.10), kind=kLoop, calls=%fused_computation.69 | loop fusion | bytes 1024 | tf_op jit(solution)/shard_map/add | solution.py:136
  14.7 1.3 %fusion.24 = (s32[1]{0:T(128)}, s32[1]{0:T(128)}) fusion(s32[2]{0:T(128)} %param.11), kind=kLoop, calls=%fused_computation.79 | loop fusion | bytes 16 | tf_op jit(solution)/shard_map/slice | solution.py:133
  16.7 0.7 %and_convert_fusion = (f32[72]{0:T(128)S(1)}, f32[72]{0:T(128)S(1)}) fusion(s32[]{:T(128)} %bitcast.6, s32[]{:T(128)S(6)} %sub.7), kind=kLoop, calls=%fused_computation.62 | loop fusion | flops 720 | bytes 584 | tf_op jit(solution)/shard_map/convert_element_type | solution.py:18
  17.4 0.7 %and_convert_fusion.1 = (f32[136]{0:T(256)S(1)}, f32[136]{0:T(256)S(1)}) fusion(s32[]{:T(128)} %bitcast.6, s32[]{:T(128)S(6)} %sub.6), kind=kLoop, calls=%fused_computation.63 | loop fusion | flops 1360 | bytes 1096 | tf_op jit(solution)/shard_map/convert_element_type | solution.py:18
  18.1 1.1 %slice_bitcast_fusion.2 = (bf16[9,64,64]{2,1,0:T(8,128)(2,1)S(1)}, bf16[1,9,64,64]{3,2,1,0:T(8,128)(2,1)S(1)}, bf16[1,9,64,64]{3,2,1,0:T(8,128)(2,1)S(1)}) fusion(bf16[2,9,64,64]{3,2,1,0:T(8,128)(2,1)} %param.9), kind=kLoop, calls=%fused_computation.76 | loop fusion | bytes 368640 | tf_op jit(solution)/shard_map/squeeze | solution.py:132
  23.4 0.6 %all-to-all-done = bf16[128,2,256]{2,1,0:T(2,128)(2,1)S(1)} async-done(((bf16[128,2,256]{2,1,0:T(2,128)(2,1)}), bf16[128,2,256]{2,1,0:T(2,128)(2,1)S(1)}, u32[]{:S(2)}, u32[]{:S(2)}) %all-to-all-start) | async-done | bytes 131104 | tf_op jit(solution)/shard_map/all_to_all | solution.py:14
  25.2 0.8 %fusion.8 = (f32[1,1032,64]{1,2,0:T(8,128)S(1)}, f32[1,1032,64]{1,2,0:T(8,128)S(1)}, f32[1,1032,64]{1,2,0:T(8,128)S(1)}) fusion(f32[9,1040,64]{1,2,0:T(8,128)S(1)} %convolution_bitcast_fusion, f32[1,1040,64]{1,2,0:T(8,128)S(1)} %get-tuple-element.24, s32[]{:T(128)S(6)} %select_n.28, f32[1,1040,64]{1,2,0:T(8,128)S(1)} %get-tuple-element.19, s32[]{:T(128)S(6)} %select_n.27, ...), kind=kLoop, calls=%fused_computation.33 | loop fusion | flops 396288 | bytes 3170312 | tf_op jit(solution)/shard_map/add | solution.py:68
  26.9 0.8 %fusion.9 = (f32[1,1032,64]{1,2,0:T(8,128)S(1)}, f32[1,1032,64]{1,2,0:T(8,128)S(1)}, f32[1,1032,64]{1,2,0:T(8,128)S(1)}) fusion(f32[9,1040,64]{1,2,0:T(8,128)S(1)} %convolution_bitcast_fusion.1, f32[1,1040,64]{1,2,0:T(8,128)S(1)} %get-tuple-element.15, s32[]{:T(128)S(6)} %select_n.28, f32[1,1040,64]{1,2,0:T(8,128)S(1)} %get-tuple-element.10, ...), kind=kLoop, calls=%fused_computation.35 | loop fusion | flops 396288 | bytes 3170312 | tf_op jit(solution)/shard_map/add | solution.py:67
  28.6 7.2 %maximum_multiply_fusion = (bf16[72,136,64]{1,2,0:T(8,128)(2,1)S(1)}, bf16[72,136,64]{1,2,0:T(8,128)(2,1)S(1)}) fusion(bf16[72,136]{1,0:T(8,128)(2,1)S(1)} %multiply_convert_fusion.2, f32[72,64]{1,0:T(8,128)S(1)} %copy.21, f32[136,64]{0,1:T(8,128)S(1)} %get-tuple-element.44, f32[72,64]{1,0:T(8,128)S(1)} %copy.20, f32[136,64]{0,1:T(8,128)S(1)} %get-tuple-element.45, ...), kind=kLoop, calls=%fused_computation.5 | loop fusion | flops 24440832 | bytes 2875264 | tf_op jit(solution)/shard_map/mul | solution.py:133
  36.3 0.7 %dynamic-slice_dynamic-update-slice_fusion.6 = bf16[64,128,576]{1,2,0:T(8,128)(2,1)S(1)} fusion(bf16[64,128,576]{1,2,0:T(8,128)(2,1)S(1)} %dynamic-slice_dynamic-update-slice_fusion.7, bf16[72,136,64]{1,2,0:T(8,128)(2,1)S(1)} %get-tuple-element.5, s32[]{:T(128)S(6)} %select_n.30), kind=kLoop, calls=%fused_computation.22 | loop fusion | bytes 2097156
  37.0 0.7 %dynamic-slice_dynamic-update-slice_fusion.5 = bf16[64,128,576]{1,2,0:T(8,128)(2,1)S(1)} fusion(bf16[64,128,576]{1,2,0:T(8,128)(2,1)S(1)} %dynamic-slice_dynamic-update-slice_fusion.6, bf16[72,136,64]{1,2,0:T(8,128)(2,1)S(1)} %get-tuple-element.5, s32[]{:T(128)S(6)} %select_n.30, s32[]{:T(128)S(6)} %select_n.32), kind=kLoop, calls=%fused_computation.21 | loop fusion | bytes 2097160
  37.8 0.8 %dynamic-slice_dynamic-update-slice_fusion.4 = bf16[64,128,576]{1,2,0:T(8,128)(2,1)S(1)} fusion(bf16[64,128,576]{1,2,0:T(8,128)(2,1)S(1)} %dynamic-slice_dynamic-update-slice_fusion.5, bf16[72,136,64]{1,2,0:T(8,128)(2,1)S(1)} %get-tuple-element.5, s32[]{:T(128)S(6)} %select_n.31), kind=kLoop, calls=%fused_computation.20 | loop fusion | bytes 2097156
  38.5 0.7 %slice_dynamic-update-slice_fusion = bf16[64,128,576]{1,2,0:T(8,128)(2,1)S(1)} fusion(bf16[64,128,576]{1,2,0:T(8,128)(2,1)S(1)} %dynamic-slice_dynamic-update-slice_fusion.4, bf16[72,136,64]{1,2,0:T(8,128)(2,1)S(1)} %get-tuple-element.5), kind=kLoop, calls=%fused_computation.15 | loop fusion | bytes 2097152
  39.2 0.8 %dynamic-slice_dynamic-update-slice_fusion.3 = bf16[64,128,576]{1,2,0:T(8,128)(2,1)S(1)} fusion(bf16[64,128,576]{1,2,0:T(8,128)(2,1)S(1)} %slice_dynamic-update-slice_fusion, bf16[72,136,64]{1,2,0:T(8,128)(2,1)S(1)} %get-tuple-element.5, s32[]{:T(128)S(6)} %select_n.32), kind=kLoop, calls=%fused_computation.19 | loop fusion | bytes 2097156
  40.0 0.7 %dynamic-slice_dynamic-update-slice_fusion.2 = bf16[64,128,576]{1,2,0:T(8,128)(2,1)S(1)} fusion(bf16[64,128,576]{1,2,0:T(8,128)(2,1)S(1)} %dynamic-slice_dynamic-update-slice_fusion.3, bf16[72,136,64]{1,2,0:T(8,128)(2,1)S(1)} %get-tuple-element.5, s32[]{:T(128)S(6)} %select_n.33, s32[]{:T(128)S(6)} %select_n.31), kind=kLoop, calls=%fused_computation.18 | loop fusion | bytes 2097160
  40.7 0.7 %dynamic-slice_dynamic-update-slice_fusion.1 = bf16[64,128,576]{1,2,0:T(8,128)(2,1)S(1)} fusion(bf16[64,128,576]{1,2,0:T(8,128)(2,1)S(1)} %dynamic-slice_dynamic-update-slice_fusion.2, bf16[72,136,64]{1,2,0:T(8,128)(2,1)S(1)} %get-tuple-element.5, s32[]{:T(128)S(6)} %select_n.33), kind=kLoop, calls=%fused_computation.17 | loop fusion | bytes 2097156
  41.5 0.7 %dynamic-slice_dynamic-update-slice_fusion = bf16[64,128,576]{1,2,0:T(8,128)(2,1)S(1)} fusion(bf16[64,128,576]{1,2,0:T(8,128)(2,1)S(1)} %dynamic-slice_dynamic-update-slice_fusion.1, bf16[72,136,64]{1,2,0:T(8,128)(2,1)S(1)} %get-tuple-element.5, s32[]{:T(128)S(6)} %select_n.33, s32[]{:T(128)S(6)} %select_n.32), kind=kLoop, calls=%fused_computation.16 | loop fusion | bytes 2097160 | tf_op jit(solution)/shard_map/concatenate | solution.py:35
  42.2 1.9 %fusion.25 = f32[64,128,128]{1,2,0:T(8,128)S(1)} fusion(bf16[64,128,576]{1,2,0:T(8,128)(2,1)S(1)} %dynamic-slice_dynamic-update-slice_fusion, bf16[576,128,1]{1,0,2:T(8,128)(2,1)S(1)} %bitcast.68), kind=kOutput, calls=%fused_computation.80 | convolution fusion | flops 1207959552 | bytes 13778944 | tf_op jit(solution)/shard_map/dot_general | solution.py:37
  44.1 0.7 %fusion.3 = bf16[64,64,128]{2,0,1:T(8,128)(2,1)S(1)} fusion(f32[64,128,128]{1,2,0:T(8,128)S(1)} %fusion.25, bf16[72,136,64]{1,2,0:T(8,128)(2,1)S(1)} %get-tuple-element.6, f32[64]{0:T(128)S(1)} %get-tuple-element.28), kind=kLoop, calls=%fused_computation.14 | loop fusion | flops 5767168 | bytes 6291712 | tf_op jit(solution)/shard_map/transpose | solution.py:142
  44.8 1.6 %copy.24 = bf16[64,64,128]{2,1,0:T(8,128)(2,1)} copy(bf16[64,64,128]{2,0,1:T(8,128)(2,1)S(1)} %fusion.3) | data formatting | bytes 2097152 | tf_op jit(solution)/shard_map/transpose | solution.py:142
  (33 shorter events, 4.0 us)
Async XLA Ops:
  0.0 0.7 %copy-start = (bf16[8,128]{1,0:T(8,128)(2,1)S(1)}, bf16[8,128]{1,0:T(8,128)(2,1)}, u32[]{:S(2)}) copy-start(bf16[8,128]{1,0:T(8,128)(2,1)} %param.6) | copy-start | bytes 6148
  2.4 21.6 %all-to-all-start = ((bf16[128,2,256]{2,1,0:T(2,128)(2,1)}), bf16[128,2,256]{2,1,0:T(2,128)(2,1)S(1)}, u32[]{:S(2)}, u32[]{:S(2)}) async-start(bf16[128,2,256]{2,1,0:T(2,128)(2,1)} %reshape.179), calls=%async_computation | async-start | bytes 262144 | tf_op jit(solution)/shard_map/all_to_all | solution.py:14

commit v3 on v2

--- a/solution.py
+++ b/solution.py
@@ -21,20 +21,33 @@
 def tap_groups(padded, weights, dilation):
     out_channels = weights.shape[1]
     in_channels = weights.shape[2]
-    row_count = padded.shape[0] - 2 * MAXDIL
+    row_ext = padded.shape[0]
+    row_count = row_ext - 2 * MAXDIL
     col_count = padded.shape[1] - 2 * MAXDIL
     zero_index = jnp.zeros((), jnp.int32)
-    pieces = []
-    for tap in range(9):
-        row_index = MAXDIL + (tap // 3 - 1) * dilation
-        col_index = MAXDIL + (tap % 3 - 1) * dilation
-        piece = lax.dynamic_slice(
-            padded, (row_index, col_index, zero_index), (row_count, col_count, in_channels)
+    shifted = jnp.concatenate(
+        [
+            lax.dynamic_slice(
+                padded,
+                (zero_index, MAXDIL + (inner - 1) * dilation, zero_index),
+                (row_ext, col_count, in_channels),
+            )
+            for inner in range(3)
+        ],
+        axis=2,
+    )
+    summed = None
+    for outer in range(3):
+        rows_now = lax.dynamic_slice_in_dim(shifted, MAXDIL + (outer - 1) * dilation, row_count, 0)
+        group_weight = jnp.transpose(weights[3 * outer : 3 * outer + 3], (0, 2, 1)).reshape(
+            3 * in_channels, out_channels
         )
-        pieces.append(piece.reshape(row_count * col_count, in_channels))
-    stacked = jnp.concatenate(pieces, axis=1)
-    flat_weight = jnp.transpose(weights, (0, 2, 1)).reshape(9 * in_channels, out_channels)
-    summed = jnp.dot(stacked, flat_weight, preferred_element_type=jnp.float32)
+        part = jnp.dot(
+            rows_now.reshape(row_count * col_count, 3 * in_channels),
+            group_weight,
+            preferred_element_type=jnp.float32,
+        )
+        summed = part if summed is None else summed + part
     return summed.reshape(row_count, col_count, out_channels)
 
 
@@ -75,35 +88,39 @@
     row_places = row_start - MAXDIL + jnp.arange(rows)
     col_places = col_start - MAXDIL + jnp.arange(cols)
 
-    def conv_at(p_start, p_places, q_start, q_places, p_count, q_count, p_axis):
-        total = None
-        for step in range(3):
-            q_in = inside(q_places + (step - 1) * dilation, bins_total)
-            p_in = inside(p_places + (step - 1) * dilation, bins_total)
-            term_p = at(by_col[step], p_start, p_count)
-            term_q = at(by_row[step], q_start, q_count)
-            if p_axis == 0:
-                piece = term_p[:, None, :] * q_in[None, :, None] + term_q[None, :, :] * p_in[
-                    :, None, None
-                ]
-            else:
-                piece = term_p[None, :, :] * q_in[:, None, None] + term_q[:, None, :] * p_in[
-                    None, :, None
-                ]
-            total = piece if total is None else total + piece
-        return total
+    padded = jnp.pad(every, ((MAXDIL, MAXDIL), (0, 0)))
+    lower = jnp.arange(every.shape[1]) < half
+    own_row = jnp.where(lower, padded, 0.0) + shift_bias[None, :]
+    own_col = jnp.where(lower, 0.0, padded)
+    row_tables = [
+        own_row + by_col[1] + by_col[2],
+        own_row + by_col[0] + by_col[1] + by_col[2],
+        own_row + by_col[0] + by_col[1],
+    ]
+    col_tables = [
+        own_col + by_row[1] + by_row[2],
+        own_col + by_row[0] + by_row[1] + by_row[2],
+        own_col + by_row[0] + by_row[1],
+    ]
 
-    padded = jnp.pad(every, ((MAXDIL, MAXDIL), (0, 0)))
-    rows_here = at(padded, row_start, rows)
-    cols_here = at(padded, col_start, cols)
-    lower = jnp.arange(every.shape[1]) < half
-    map0 = jnp.where(lower, rows_here[:, None, :], cols_here[None, :, :])
-    map0_mirror = jnp.where(lower, cols_here[None, :, :], rows_here[:, None, :])
-    bias = shift_bias[None, None, :]
-    conv = conv_at(row_start, row_places, col_start, col_places, rows, cols, 0)
-    conv_mirror = conv_at(col_start, col_places, row_start, row_places, cols, rows, 1)
-    mixed = (map0.astype(jnp.float32) + bias + conv).astype(jnp.bfloat16)
-    mixed_mirror = (map0_mirror.astype(jnp.float32) + bias + conv_mirror).astype(jnp.bfloat16)
+    def pick(tables, start, count, places, axis):
+        low, mid, high = (at(table, start, count) for table in tables)
+        shape = [1, 1, 1]
+        shape[axis] = -1
+        near_low = (places < dilation).reshape(shape)
+        near_high = (places >= bins_total - dilation).reshape(shape)
+        return jnp.where(near_low, low[:, None, :], jnp.where(near_high, high[:, None, :], mid[:, None, :])) if axis == 1 else jnp.where(
+            near_low, low[None, :, :], jnp.where(near_high, high[None, :, :], mid[None, :, :])
+        )
+
+    mixed = (
+        pick(row_tables, row_start, rows, col_places, 1)
+        + pick(col_tables, col_start, cols, row_places, 0)
+    ).astype(jnp.bfloat16)
+    mixed_mirror = (
+        pick(row_tables, col_start, cols, row_places, 0)
+        + pick(col_tables, row_start, rows, col_places, 1)
+    ).astype(jnp.bfloat16)
     return mixed, mixed_mirror, row_places, col_places
 
 

time: 46.8 us -> 77 us (1.65)
  local copies, waits for them, and re-layouts: 14.8 us -> 27.5 us
  matrix products: 3.85 us -> 15 us
  other arithmetic: 11 us -> 17.3 us
    dot_general x1 -> x3, matrix products: 1.85 us -> 13 us  [tap_groups(): jnp.dot(rows_now.reshape(row_count * col_count, 3 * in_channels), group_w...]
    dynamic_slice x0 -> x2, local copies, waits for them, and re-layouts: none -> 8.52 us  [the longest x1 7.33 us: tap_groups(): lax.dynamic_slice_in_dim(shifted, MAXDIL + (outer - 1) * dilation, row_co...]
    slice x0 -> x2, local copies, waits for them, and re-layouts: none -> 5.83 us  [the longest x1 4.83 us: local(): mixed1 = (base1 + conv1[:, :, :channels]).astype(jnp.bfloat16)]
    transpose x1, other arithmetic: 0.7 us -> 4.81 us  [local(): return jnp.transpose(pair, (2, 0, 1))]
    concatenate x0 -> x2, other arithmetic: none -> 2.96 us  [the longest x1 2.21 us: tap_groups(): jnp.concatenate([lax.dynamic_slice(padded, (zero_index, MAXDIL + (inner -...]
    unnamed x13 -> x14, local copies, waits for them, and re-layouts: 7.52 us -> 9.83 us
    transpose x3 -> x0, local copies, waits for them, and re-layouts: 1.84 us -> none  [the longest x1 1.65 us: local(): return jnp.transpose(pair, (2, 0, 1))]
    convert_element_type x4 -> x2, other arithmetic: 1.4 us -> 0.02 us  [inside(): return ((places >= 0) & (places < bins_total)).astype(jnp.float32)]
  transfers between devices with their start and end apart: 1 -> 1, of which waited for: 1 -> 0; matrix products, arithmetic and copies ran while one was open for 11% -> 7% of each run, Pallas kernels for 0% -> 0%
where the time goes in v3:
time: 77 us; the launch traced here: 76.6 us
  local copies, waits for them, and re-layouts  27.5 us (36%)
  other arithmetic  17.3 us (22%)
  matrix products  15 us (19%)
  starting transfers between devices  11.5 us (15%)
  between operations  5.32 us (7%)
    dot_general x3, matrix products, tap_groups(): jnp.dot(rows_now.reshape(row_count * col_count, 3 * in_channels), group_w...  13 us
    all_to_all x1, starting transfers between devices, gather_projections(): lax.all_to_all(copies, axes, 0, 0, tiled=True).reshape(-1, proj.shape[1])  11.5 us
    unnamed x14, local copies, waits for them, and re-layouts  9.83 us
    dynamic_slice x1, local copies, waits for them, and re-layouts, tap_groups(): lax.dynamic_slice_in_dim(shifted, MAXDIL + (outer - 1) * dilation, row_co...  7.33 us
    mul x1, other arithmetic, local(): conv1 = tap_groups(jax.nn.relu(map1) * mask1, taps1, dilations[1])  5.99 us
    slice x1, local copies, waits for them, and re-layouts, local(): mixed1 = (base1 + conv1[:, :, :channels]).astype(jnp.bfloat16)  4.83 us
    transpose x1, other arithmetic, local(): return jnp.transpose(pair, (2, 0, 1))  4.81 us
    concatenate x1, other arithmetic, tap_groups(): jnp.concatenate([lax.dynamic_slice(padded, (zero_index, MAXDIL + (inner -...  2.21 us
  transfers between devices with their start and end apart: 1, of which 0 were waited for; matrix products, arithmetic and copies ran while one was open for 7% of the time, Pallas kernels for 0%

profile of v3, /device:TPU:1, one launch (start us, length us, event | category | flops | bytes accessed | tf_op | source)
XLA Modules:
  0.0 76.6 jit_solution(6027358704675482639)
XLA Ops:
  0.0 0.7 copy-done
  0.7 0.8 %fusion.7 = bf16[8,64]{1,0:T(8,128)(2,1)S(1)} fusion(bf16[8,128]{1,0:T(8,128)(2,1)S(1)} %copy-done, bf16[128,32]{0,1:T(8,128)(2,1)} %param.8, bf16[128,32]{0,1:T(8,128)(2,1)} %param.7), kind=kOutput, calls=%fused_computation.21 | convolution fusion | flops 164352 | bytes 19456 | tf_op jit(solution)/shard_map/dot_general | solution.py:129
  1.6 0.9 %reshape.166 = bf16[128,2,256]{2,1,0:T(2,128)(2,1)} reshape(bf16[128,8,64]{2,1,0:T(8,128)(2,1)S(1)} %broadcast_in_dim.158) | data formatting | bytes 262144
  2.5 11.5 %all-to-all-start = ((bf16[128,2,256]{2,1,0:T(2,128)(2,1)}), bf16[128,2,256]{2,1,0:T(2,128)(2,1)S(1)}, u32[]{:S(2)}, u32[]{:S(2)}) async-start(bf16[128,2,256]{2,1,0:T(2,128)(2,1)} %reshape.166), calls=%async_computation | async-start | bytes 262144 | tf_op jit(solution)/shard_map/all_to_all | solution.py:14
  14.0 0.8 slice_bitcast_fusion
  14.7 1.4 %fusion.53 = (s32[1]{0:T(128)}, s32[1]{0:T(128)}) fusion(s32[2]{0:T(128)} %param.11), kind=kLoop, calls=%fused_computation.105 | loop fusion | bytes 16 | tf_op jit(solution)/shard_map/slice | solution.py:150
  17.3 1.0 %fusion.52 = (bf16[1,9,64,64]{3,2,1,0:T(8,128)(2,1)S(1)}, bf16[1,9,64,64]{3,2,1,0:T(8,128)(2,1)S(1)}) fusion(bf16[2,9,64,64]{3,2,1,0:T(8,128)(2,1)} %param.9), kind=kLoop, calls=%fused_computation.104 | loop fusion | bytes 294912 | tf_op jit(solution)/shard_map/slice | solution.py:140
  23.9 0.7 pad_maximum_fusion.1
  25.1 0.6 convolution_bitcast_fusion
  25.7 0.6 convolution_bitcast_fusion.1
  26.5 0.6 add_add_fusion
  27.1 1.0 %fusion.44 = (f32[1032,64]{0,1:T(8,128)S(1)}, f32[1032,64]{0,1:T(8,128)S(1)}, f32[1032,64]{0,1:T(8,128)S(1)}, f32[1032,64]{0,1:T(8,128)S(1)}) fusion(f32[1032,64]{0,1:T(8,128)S(1)} %get-tuple-element.8, f32[1,1040,64]{1,2,0:T(8,128)S(1)} %get-tuple-element.24, s32[]{:T(128)S(6)} %select_n.82, f32[9,1040,64]{1,2,0:T(8,128)S(1)} %convolution_bitcast_fusion.1, ...), kind=kLoop, calls=%fused_computation.99 | loop fusion | flops 1188864 | bytes 4622664 | tf_op jit(solution)/shard_map/add | solution.py:97
  28.2 0.6 fusion.47
  29.4 6.0 %maximum_multiply_fusion = (bf16[72,136,64]{1,0,2:T(8,128)(2,1)S(1)}, bf16[72,136,64]{1,0,2:T(8,128)(2,1)}) fusion(bf16[72,136]{1,0:T(8,128)(2,1)S(1)} %multiply_convert_fusion.2, f32[72,64]{0,1:T(8,128)S(1)} %get-tuple-element.54, f32[72,64]{0,1:T(8,128)S(1)} %get-tuple-element.55, f32[72,64]{0,1:T(8,128)S(1)} %get-tuple-element.50, ...), kind=kLoop, calls=%fused_computation.15 | loop fusion | flops 11907072 | bytes 2846240 | tf_op jit(solution)/shard_map/mul | solution.py:150
  35.4 1.2 %constant_dynamic-slice_fusion.15 = (bf16[72,128,64]{1,0,2:T(8,128)(2,1)S(1)}, bf16[72,128,64]{1,0,2:T(8,128)(2,1)S(1)}, bf16[72,128,64]{1,0,2:T(8,128)(2,1)S(1)}) fusion(bf16[72,136,64]{1,0,2:T(8,128)(2,1)S(1)} %get-tuple-element.5, s32[]{:T(128)S(6)} %select_n.94, s32[]{:T(128)S(6)} %select_n.95), kind=kLoop, calls=%fused_computation.84 | loop fusion | bytes 7077896 | tf_op jit(solution)/shard_map/dynamic_slice | solution.py:30
  36.5 2.2 %pad_maximum_fusion = bf16[72,128,192]{1,0,2:T(8,128)(2,1)S(1)} fusion(bf16[72,128,64]{1,0,2:T(8,128)(2,1)S(1)} %get-tuple-element.33, bf16[72,128,64]{1,0,2:T(8,128)(2,1)S(1)} %get-tuple-element.34, bf16[72,128,64]{1,0,2:T(8,128)(2,1)S(1)} %get-tuple-element.32), kind=kLoop, calls=%fused_computation.5 | loop fusion | flops 3538944 | bytes 7077888 | tf_op jit(solution)/shard_map/concatenate | solution.py:28
  38.8 7.3 %constant_dynamic-slice_fusion.8 = (bf16[64,128,192]{1,0,2:T(8,128)(2,1)S(1)}, bf16[64,128,192]{1,0,2:T(8,128)(2,1)}, bf16[64,128,192]{1,0,2:T(8,128)(2,1)S(1)}) fusion(bf16[72,128,192]{1,0,2:T(8,128)(2,1)S(1)} %pad_maximum_fusion, s32[]{:T(128)S(6)} %select_n.97, s32[]{:T(128)S(6)} %select_n.96), kind=kLoop, calls=%fused_computation.77 | loop fusion | bytes 18874376 | tf_op jit(solution)/shard_map/dynamic_slice | solution.py:41
  46.1 4.3 %fusion.4 = f32[8192,128]{1,0:T(8,128)S(1)} fusion(bf16[192,128]{1,0:T(8,128)(2,1)S(1)} %bitcast.107, bf16[24,8,64,128]{3,2,1,0:T(8,128)(2,1)S(1)} %bitcast.100), kind=kOutput, calls=%fused_computation.12 | convolution fusion | flops 402653184 | bytes 7389184 | tf_op jit(solution)/shard_map/dot_general | solution.py:45
  50.4 4.4 %convolution_add_fusion.1 = f32[8192,128]{1,0:T(8,128)S(1)} fusion(f32[8192,128]{1,0:T(8,128)S(1)} %fusion.4, bf16[192,128]{1,0:T(8,128)(2,1)S(1)} %bitcast.109, bf16[24,8,64,128]{3,2,1,0:T(8,128)(2,1)S(1)} %bitcast.99), kind=kOutput, calls=%fused_computation.1 | convolution fusion | flops 403701760 | bytes 11583488 | tf_op jit(solution)/shard_map/dot_general | solution.py:45
  54.8 4.4 %convolution_add_fusion = f32[8192,128]{1,0:T(8,128)S(1)} fusion(f32[8192,128]{1,0:T(8,128)S(1)} %convolution_add_fusion.1, bf16[192,128]{1,0:T(8,128)(2,1)S(1)} %bitcast.108, bf16[24,8,64,128]{3,2,1,0:T(8,128)(2,1)S(1)} %bitcast.98), kind=kOutput, calls=%fused_computation | convolution fusion | flops 403701760 | bytes 11583488 | tf_op jit(solution)/shard_map/dot_general | solution.py:45
  59.2 4.8 %fusion.49 = (f32[64,128,64]{2,1,0:T(8,128)}, f32[64,128,64]{2,1,0:T(8,128)}) fusion(f32[64,128,128]{2,1,0:T(8,128)S(1)} %bitcast.97), kind=kLoop, calls=%fused_computation.101 | loop fusion | bytes 8388608 | tf_op jit(solution)/shard_map/slice | solution.py:154
  64.0 3.5 %copy.21 = f32[64,128,64]{1,0,2:T(8,128)S(1)} copy(f32[64,128,64]{2,1,0:T(8,128)} %get-tuple-element.15) | data formatting | bytes 4194304
  67.6 4.2 %copy.22 = f32[64,128,64]{1,0,2:T(8,128)} copy(f32[64,128,64]{2,1,0:T(8,128)} %get-tuple-element.16) | data formatting | bytes 4194304
  71.8 4.8 %fusion.8 = bf16[64,64,128]{2,1,0:T(8,128)(2,1)} fusion(f32[64,128,64]{1,0,2:T(8,128)} %copy.22, f32[64,128,64]{1,0,2:T(8,128)S(1)} %copy.21, bf16[72,136,64]{1,0,2:T(8,128)(2,1)} %get-tuple-element.6, f32[64]{0:T(128)S(1)} %get-tuple-element.42), kind=kLoop, calls=%fused_computation.22 | loop fusion | flops 5767168 | bytes 6291712 | tf_op jit(solution)/shard_map/transpose | solution.py:159
  (29 shorter events, 2.9 us)
Async XLA Ops:
  0.0 0.7 copy-start
  2.5 22.2 %all-to-all-start = ((bf16[128,2,256]{2,1,0:T(2,128)(2,1)}), bf16[128,2,256]{2,1,0:T(2,128)(2,1)S(1)}, u32[]{:S(2)}, u32[]{:S(2)}) async-start(bf16[128,2,256]{2,1,0:T(2,128)(2,1)} %reshape.166), calls=%async_computation | async-start | bytes 262144 | tf_op jit(solution)/shard_map/all_to_all | solution.py:14
  46.1 4.3 %copy-start.1 = (bf16[64,128,192]{1,0,2:T(8,128)(2,1)S(1)}, bf16[64,128,192]{1,0,2:T(8,128)(2,1)}, u32[]{:S(2)}) copy-start(bf16[64,128,192]{1,0,2:T(8,128)(2,1)} %get-tuple-element.18) | copy-start | bytes 9437188
  46.1 4.3 %copy-start.3 = (bf16[3,128,64]{1,2,0:T(8,128)(2,1)S(1)}, bf16[3,128,64]{1,2,0:T(8,128)(2,1)}, u32[]{:S(2)}) copy-start(bf16[3,128,64]{1,2,0:T(8,128)(2,1)} %get-tuple-element.37) | copy-start | bytes 147460
  50.4 4.4 %copy-start.2 = (bf16[3,128,64]{1,2,0:T(8,128)(2,1)S(1)}, bf16[3,128,64]{1,2,0:T(8,128)(2,1)}, u32[]{:S(2)}) copy-start(bf16[3,128,64]{1,2,0:T(8,128)(2,1)} %get-tuple-element.35) | copy-start | bytes 147460

commit v4 on v3

--- a/solution.py
+++ b/solution.py
@@ -21,33 +21,20 @@
 def tap_groups(padded, weights, dilation):
     out_channels = weights.shape[1]
     in_channels = weights.shape[2]
-    row_ext = padded.shape[0]
-    row_count = row_ext - 2 * MAXDIL
+    row_count = padded.shape[0] - 2 * MAXDIL
     col_count = padded.shape[1] - 2 * MAXDIL
     zero_index = jnp.zeros((), jnp.int32)
-    shifted = jnp.concatenate(
-        [
-            lax.dynamic_slice(
-                padded,
-                (zero_index, MAXDIL + (inner - 1) * dilation, zero_index),
-                (row_ext, col_count, in_channels),
-            )
-            for inner in range(3)
-        ],
-        axis=2,
-    )
-    summed = None
-    for outer in range(3):
-        rows_now = lax.dynamic_slice_in_dim(shifted, MAXDIL + (outer - 1) * dilation, row_count, 0)
-        group_weight = jnp.transpose(weights[3 * outer : 3 * outer + 3], (0, 2, 1)).reshape(
-            3 * in_channels, out_channels
+    pieces = []
+    for tap in range(9):
+        row_index = MAXDIL + (tap // 3 - 1) * dilation
+        col_index = MAXDIL + (tap % 3 - 1) * dilation
+        piece = lax.dynamic_slice(
+            padded, (row_index, col_index, zero_index), (row_count, col_count, in_channels)
         )
-        part = jnp.dot(
-            rows_now.reshape(row_count * col_count, 3 * in_channels),
-            group_weight,
-            preferred_element_type=jnp.float32,
-        )
-        summed = part if summed is None else summed + part
+        pieces.append(piece.reshape(row_count * col_count, in_channels))
+    stacked = jnp.concatenate(pieces, axis=1)
+    flat_weight = jnp.transpose(weights, (0, 2, 1)).reshape(9 * in_channels, out_channels)
+    summed = jnp.dot(stacked, flat_weight, preferred_element_type=jnp.float32)
     return summed.reshape(row_count, col_count, out_channels)
 
 

time: 77 us -> 46.6 us (0.61)
  local copies, waits for them, and re-layouts: 27.5 us -> 14.9 us
  matrix products: 15 us -> 3.84 us
  other arithmetic: 17.3 us -> 10.4 us
    dot_general x3 -> x1, matrix products: 13 us -> 1.85 us  [tap_groups(): summed = jnp.dot(stacked, flat_weight, preferred_element_type=jnp.float32)]
    dynamic_slice x2 -> x0, local copies, waits for them, and re-layouts: 8.52 us -> none  [the longest x1 7.33 us: tap_groups(): lax.dynamic_slice_in_dim(shifted, MAXDIL + (outer - 1) * dilation, row_co...]
    slice x2 -> x0, local copies, waits for them, and re-layouts: 5.83 us -> none  [the longest x1 4.83 us: local(): mixed1 = (base1 + conv1[:, :, :channels]).astype(jnp.bfloat16)]
    transpose x1, other arithmetic: 4.81 us -> 0.7 us  [local(): return jnp.transpose(pair, (2, 0, 1))]
    concatenate x2 -> x0, other arithmetic: 2.96 us -> none  [the longest x1 2.21 us: tap_groups(): jnp.concatenate([lax.dynamic_slice(padded, (zero_index, MAXDIL + (inner -...]
    unnamed x14 -> x13, local copies, waits for them, and re-layouts: 9.83 us -> 7.63 us
    transpose x0 -> x3, local copies, waits for them, and re-layouts: none -> 1.84 us  [the longest x1 1.65 us: local(): return jnp.transpose(pair, (2, 0, 1))]
    squeeze x0 -> x1, local copies, waits for them, and re-layouts: none -> 1.06 us  [local(): conv_weight[1]]
  transfers between devices with their start and end apart: 1 -> 1, of which waited for: 0 -> 0; matrix products, arithmetic and copies ran while one was open for 7% -> 11% of each run, Pallas kernels for 0% -> 0%
where the time goes in v4:
time: 46.6 us; the launch traced here: 46.3 us
  local copies, waits for them, and re-layouts  14.9 us (32%)
  starting transfers between devices  11.5 us (25%)
  other arithmetic  10.4 us (22%)
  between operations  5.64 us (12%)
  matrix products  3.84 us (8%)
    all_to_all x1, starting transfers between devices, gather_projections(): lax.all_to_all(copies, axes, 0, 0, tiled=True).reshape(-1, proj.shape[1])  11.5 us
    unnamed x13, local copies, waits for them, and re-layouts  7.63 us
    mul x1, other arithmetic, local(): conv1 = tap_groups(jax.nn.relu(map1) * mask1, taps1, dilations[1])  5.91 us
    dot_general x1, matrix products, tap_groups(): summed = jnp.dot(stacked, flat_weight, preferred_element_type=jnp.float32)  1.85 us
    transpose x1, local copies, waits for them, and re-layouts, local(): return jnp.transpose(pair, (2, 0, 1))  1.65 us
    lt x2, other arithmetic, pick(): near_low = (places < dilation).reshape(shape)  1.39 us
    slice x1, local copies, waits for them, and re-layouts, local(): conv1 = tap_groups(jax.nn.relu(map1) * mask1, taps1, dilations[1])  1.35 us
    squeeze x1, local copies, waits for them, and re-layouts, local(): conv_weight[1]  1.06 us
  transfers between devices with their start and end apart: 1, of which 0 were waited for; matrix products, arithmetic and copies ran while one was open for 11% of the time, Pallas kernels for 0%

profile of v4, /device:TPU:1, one launch (start us, length us, event | category | flops | bytes accessed | tf_op | source)
XLA Modules:
  0.0 46.3 jit_solution(3219818798493901346)
XLA Ops:
  0.0 0.7 %copy-done = bf16[8,128]{1,0:T(8,128)(2,1)S(1)} copy-done((bf16[8,128]{1,0:T(8,128)(2,1)S(1)}, bf16[8,128]{1,0:T(8,128)(2,1)}, u32[]{:S(2)}) %copy-start) | copy-done | bytes 2072
  0.7 0.8 %fusion.2 = bf16[8,64]{1,0:T(8,128)(2,1)S(1)} fusion(bf16[8,128]{1,0:T(8,128)(2,1)S(1)} %copy-done, bf16[128,32]{0,1:T(8,128)(2,1)} %param.8, bf16[128,32]{0,1:T(8,128)(2,1)} %param.7), kind=kOutput, calls=%fused_computation.13 | convolution fusion | flops 164352 | bytes 19456 | tf_op jit(solution)/shard_map/dot_general | solution.py:116
  1.6 0.9 %reshape.172 = bf16[128,2,256]{2,1,0:T(2,128)(2,1)} reshape(bf16[128,8,64]{2,1,0:T(8,128)(2,1)S(1)} %broadcast_in_dim.158) | data formatting | bytes 262144
  2.4 11.5 %all-to-all-start = ((bf16[128,2,256]{2,1,0:T(2,128)(2,1)}), bf16[128,2,256]{2,1,0:T(2,128)(2,1)S(1)}, u32[]{:S(2)}, u32[]{:S(2)}) async-start(bf16[128,2,256]{2,1,0:T(2,128)(2,1)} %reshape.172), calls=%async_computation | async-start | bytes 262144 | tf_op jit(solution)/shard_map/all_to_all | solution.py:14
  14.0 0.8 %slice_bitcast_fusion = (f32[64]{0:T(128)S(1)}, f32[64]{0:T(128)S(1)}) fusion(f32[2,64]{1,0:T(2,128)} %param.10), kind=kLoop, calls=%fused_computation.81 | loop fusion | bytes 1024 | tf_op jit(solution)/shard_map/add | solution.py:140
  14.7 1.3 %fusion.44 = (s32[1]{0:T(128)}, s32[1]{0:T(128)}) fusion(s32[2]{0:T(128)} %param.11), kind=kLoop, calls=%fused_computation.95 | loop fusion | bytes 16 | tf_op jit(solution)/shard_map/slice | solution.py:137
  16.8 1.1 %slice_bitcast_fusion.2 = (bf16[9,64,64]{2,1,0:T(8,128)(2,1)S(1)}, bf16[1,9,64,64]{3,2,1,0:T(8,128)(2,1)S(1)}, bf16[1,9,64,64]{3,2,1,0:T(8,128)(2,1)S(1)}) fusion(bf16[2,9,64,64]{3,2,1,0:T(8,128)(2,1)} %param.9), kind=kLoop, calls=%fused_computation.90 | loop fusion | bytes 368640 | tf_op jit(solution)/shard_map/squeeze | solution.py:136
  18.0 0.7 %fusion.32 = pred[72]{0:T(512)(128)(4,1)S(1)} fusion(s32[]{:T(128)} %bitcast, s32[]{:T(128)S(6)} %sub.14), kind=kLoop, calls=%fused_computation.84 | loop fusion | flops 144 | bytes 80 | tf_op jit(solution)/shard_map/lt | solution.py:97
  23.7 0.7 %fusion.30 = pred[136]{0:T(512)(128)(4,1)S(1)} fusion(s32[]{:T(128)} %bitcast, s32[]{:T(128)S(6)} %sub.12), kind=kLoop, calls=%fused_computation.80 | loop fusion | flops 272 | bytes 144 | tf_op jit(solution)/shard_map/lt | solution.py:97
  26.2 0.6 %add_add_fusion = (f32[1032,64]{0,1:T(8,128)S(1)}, f32[1032,64]{0,1:T(8,128)S(1)}) fusion(f32[64]{0:T(128)S(1)} %get-tuple-element.33, bf16[1024,64]{0,1:T(8,128)(2,1)S(1)} %copy.18, pred[64]{0:T(512)(128)(4,1)S(1)} %iota_compare_fusion, f32[1,1040,64]{1,2,0:T(8,128)S(1)} %get-tuple-element.19, s32[]{:T(128)S(6)} %select_n.90, ...), kind=kLoop, calls=%fused_computation.49 | loop fusion | flops 594432 | bytes 2244936 | tf_op jit(solution)/shard_map/add | solution.py:83
  26.8 1.0 %fusion.37 = (f32[1032,64]{0,1:T(8,128)S(1)}, f32[1032,64]{0,1:T(8,128)S(1)}, f32[1032,64]{0,1:T(8,128)S(1)}, f32[1032,64]{0,1:T(8,128)S(1)}) fusion(f32[1032,64]{0,1:T(8,128)S(1)} %get-tuple-element.8, f32[1,1040,64]{1,2,0:T(8,128)S(1)} %get-tuple-element.19, s32[]{:T(128)S(6)} %select_n.90, f32[9,1040,64]{1,2,0:T(8,128)S(1)} %convolution_bitcast_fusion.1, ...), kind=kLoop, calls=%fused_computation.91 | loop fusion | flops 1188864 | bytes 4622664 | tf_op jit(solution)/shard_map/add | solution.py:84
  27.9 0.6 %fusion.40 = (f32[1032,64]{0,1:T(8,128)S(1)}, f32[1032,64]{0,1:T(8,128)S(1)}) fusion(f32[1032,64]{0,1:T(8,128)S(1)} %get-tuple-element.31, f32[1,1040,64]{1,2,0:T(8,128)S(1)} %get-tuple-element.25, s32[]{:T(128)S(6)} %select_n.90, f32[9,1040,64]{1,2,0:T(8,128)S(1)} %convolution_bitcast_fusion, f32[1,1040,64]{1,2,0:T(8,128)S(1)} %get-tuple-element.26, ...), kind=kLoop, calls=%fused_computation.92 | loop fusion | flops 594432 | bytes 2508872 | tf_op jit(solution)/shard_map/add | solution.py:89
  29.6 5.9 %maximum_multiply_fusion = (bf16[72,136,64]{1,2,0:T(8,128)(2,1)S(1)}, bf16[72,136,64]{1,2,0:T(8,128)(2,1)S(1)}) fusion(bf16[72,136]{1,0:T(8,128)(2,1)S(1)} %multiply_convert_fusion.2, f32[72,64]{1,0:T(8,128)S(1)} %copy.26, f32[72,64]{1,0:T(8,128)S(1)} %copy.25, f32[72,64]{1,0:T(8,128)S(1)} %copy.24, f32[136,64]{0,1:T(8,128)S(1)} %get-tuple-element.42, ...), kind=kLoop, calls=%fused_computation.5 | loop fusion | flops 11907072 | bytes 2846240 | tf_op jit(solution)/shard_map/mul | solution.py:137
  36.0 0.7 %dynamic-slice_dynamic-update-slice_fusion.6 = bf16[64,128,576]{1,2,0:T(8,128)(2,1)S(1)} fusion(bf16[64,128,576]{1,2,0:T(8,128)(2,1)S(1)} %dynamic-slice_dynamic-update-slice_fusion.7, bf16[72,136,64]{1,2,0:T(8,128)(2,1)S(1)} %get-tuple-element.5, s32[]{:T(128)S(6)} %select_n.102), kind=kLoop, calls=%fused_computation.22 | loop fusion | bytes 2097156
  36.7 0.8 %dynamic-slice_dynamic-update-slice_fusion.5 = bf16[64,128,576]{1,2,0:T(8,128)(2,1)S(1)} fusion(bf16[64,128,576]{1,2,0:T(8,128)(2,1)S(1)} %dynamic-slice_dynamic-update-slice_fusion.6, bf16[72,136,64]{1,2,0:T(8,128)(2,1)S(1)} %get-tuple-element.5, s32[]{:T(128)S(6)} %select_n.102, s32[]{:T(128)S(6)} %select_n.104), kind=kLoop, calls=%fused_computation.21 | loop fusion | bytes 2097160
  37.5 0.8 %dynamic-slice_dynamic-update-slice_fusion.4 = bf16[64,128,576]{1,2,0:T(8,128)(2,1)S(1)} fusion(bf16[64,128,576]{1,2,0:T(8,128)(2,1)S(1)} %dynamic-slice_dynamic-update-slice_fusion.5, bf16[72,136,64]{1,2,0:T(8,128)(2,1)S(1)} %get-tuple-element.5, s32[]{:T(128)S(6)} %select_n.103), kind=kLoop, calls=%fused_computation.20 | loop fusion | bytes 2097156
  38.3 0.7 %slice_dynamic-update-slice_fusion = bf16[64,128,576]{1,2,0:T(8,128)(2,1)S(1)} fusion(bf16[64,128,576]{1,2,0:T(8,128)(2,1)S(1)} %dynamic-slice_dynamic-update-slice_fusion.4, bf16[72,136,64]{1,2,0:T(8,128)(2,1)S(1)} %get-tuple-element.5), kind=kLoop, calls=%fused_computation.15 | loop fusion | bytes 2097152
  39.0 0.8 %dynamic-slice_dynamic-update-slice_fusion.3 = bf16[64,128,576]{1,2,0:T(8,128)(2,1)S(1)} fusion(bf16[64,128,576]{1,2,0:T(8,128)(2,1)S(1)} %slice_dynamic-update-slice_fusion, bf16[72,136,64]{1,2,0:T(8,128)(2,1)S(1)} %get-tuple-element.5, s32[]{:T(128)S(6)} %select_n.104), kind=kLoop, calls=%fused_computation.19 | loop fusion | bytes 2097156
  39.8 0.8 %dynamic-slice_dynamic-update-slice_fusion.2 = bf16[64,128,576]{1,2,0:T(8,128)(2,1)S(1)} fusion(bf16[64,128,576]{1,2,0:T(8,128)(2,1)S(1)} %dynamic-slice_dynamic-update-slice_fusion.3, bf16[72,136,64]{1,2,0:T(8,128)(2,1)S(1)} %get-tuple-element.5, s32[]{:T(128)S(6)} %select_n.105, s32[]{:T(128)S(6)} %select_n.103), kind=kLoop, calls=%fused_computation.18 | loop fusion | bytes 2097160
  40.5 0.7 %dynamic-slice_dynamic-update-slice_fusion.1 = bf16[64,128,576]{1,2,0:T(8,128)(2,1)S(1)} fusion(bf16[64,128,576]{1,2,0:T(8,128)(2,1)S(1)} %dynamic-slice_dynamic-update-slice_fusion.2, bf16[72,136,64]{1,2,0:T(8,128)(2,1)S(1)} %get-tuple-element.5, s32[]{:T(128)S(6)} %select_n.105), kind=kLoop, calls=%fused_computation.17 | loop fusion | bytes 2097156
  41.3 0.8 %dynamic-slice_dynamic-update-slice_fusion = bf16[64,128,576]{1,2,0:T(8,128)(2,1)S(1)} fusion(bf16[64,128,576]{1,2,0:T(8,128)(2,1)S(1)} %dynamic-slice_dynamic-update-slice_fusion.1, bf16[72,136,64]{1,2,0:T(8,128)(2,1)S(1)} %get-tuple-element.5, s32[]{:T(128)S(6)} %select_n.105, s32[]{:T(128)S(6)} %select_n.104), kind=kLoop, calls=%fused_computation.16 | loop fusion | bytes 2097160 | tf_op jit(solution)/shard_map/concatenate | solution.py:35
  42.0 1.9 %fusion.45 = f32[64,128,128]{1,2,0:T(8,128)S(1)} fusion(bf16[64,128,576]{1,2,0:T(8,128)(2,1)S(1)} %dynamic-slice_dynamic-update-slice_fusion, bf16[576,128,1]{1,0,2:T(8,128)(2,1)S(1)} %bitcast.74), kind=kOutput, calls=%fused_computation.96 | convolution fusion | flops 1207959552 | bytes 13778944 | tf_op jit(solution)/shard_map/dot_general | solution.py:37
  43.9 0.7 %fusion.3 = bf16[64,64,128]{2,0,1:T(8,128)(2,1)S(1)} fusion(f32[64,128,128]{1,2,0:T(8,128)S(1)} %fusion.45, bf16[72,136,64]{1,2,0:T(8,128)(2,1)S(1)} %get-tuple-element.6, f32[64]{0:T(128)S(1)} %get-tuple-element.32), kind=kLoop, calls=%fused_computation.14 | loop fusion | flops 5767168 | bytes 6291712 | tf_op jit(solution)/shard_map/transpose | solution.py:146
  44.6 1.6 %copy.29 = bf16[64,64,128]{2,1,0:T(8,128)(2,1)} copy(bf16[64,64,128]{2,0,1:T(8,128)(2,1)S(1)} %fusion.3) | data formatting | bytes 2097152 | tf_op jit(solution)/shard_map/transpose | solution.py:146
  (31 shorter events, 3.9 us)
Async XLA Ops:
  0.0 0.7 %copy-start = (bf16[8,128]{1,0:T(8,128)(2,1)S(1)}, bf16[8,128]{1,0:T(8,128)(2,1)}, u32[]{:S(2)}) copy-start(bf16[8,128]{1,0:T(8,128)(2,1)} %param.6) | copy-start | bytes 6148
  2.4 22.0 %all-to-all-start = ((bf16[128,2,256]{2,1,0:T(2,128)(2,1)}), bf16[128,2,256]{2,1,0:T(2,128)(2,1)S(1)}, u32[]{:S(2)}, u32[]{:S(2)}) async-start(bf16[128,2,256]{2,1,0:T(2,128)(2,1)} %reshape.172), calls=%async_computation | async-start | bytes 262144 | tf_op jit(solution)/shard_map/all_to_all | solution.py:14

commit v5 on v4

--- a/solution.py
+++ b/solution.py
@@ -45,68 +45,70 @@
 def first_layer(every, taps, shift_bias, dilation, row_start, rows, col_start, cols):
     bins_total = every.shape[0]
     half = every.shape[1] // 2
+    lower = jnp.arange(every.shape[1]) < half
     active = jnp.pad(jax.nn.relu(every), ((REACH, REACH), (0, 0)))
-    row_part = jnp.einsum(
-        "nk,tok->tno", active[:, :half], taps[:, :, :half], preferred_element_type=jnp.float32
-    )
-    col_part = jnp.einsum(
-        "nk,tok->tno", active[:, half:], taps[:, :, half:], preferred_element_type=jnp.float32
-    )
-    span = bins_total + 2 * MAXDIL
-    by_col, by_row = [], []
-    for outer in range(3):
-        along_rows = None
-        along_cols = None
-        for inner in range(3):
-            piece_r = lax.dynamic_slice_in_dim(
-                row_part[3 * inner + outer], MAXDIL + (inner - 1) * dilation, span, 0
-            )
-            piece_c = lax.dynamic_slice_in_dim(
-                col_part[3 * outer + inner], MAXDIL + (inner - 1) * dilation, span, 0
-            )
-            along_rows = piece_r if along_rows is None else along_rows + piece_r
-            along_cols = piece_c if along_cols is None else along_cols + piece_c
-        by_col.append(along_rows)
-        by_row.append(along_cols)
+    padded = jnp.pad(every, ((MAXDIL, MAXDIL), (0, 0)))
 
-    def at(table, start, count):
-        return lax.dynamic_slice_in_dim(table, start, count, 0)
+    def tables(start, count):
+        window = lax.dynamic_slice_in_dim(active, start, count + 2 * MAXDIL, 0)
+        row_part = jnp.einsum(
+            "nk,tok->tno", window[:, :half], taps[:, :, :half], preferred_element_type=jnp.float32
+        )
+        col_part = jnp.einsum(
+            "nk,tok->tno", window[:, half:], taps[:, :, half:], preferred_element_type=jnp.float32
+        )
+        by_col, by_row = [], []
+        for outer in range(3):
+            along_rows = None
+            along_cols = None
+            for inner in range(3):
+                piece_r = lax.dynamic_slice_in_dim(
+                    row_part[3 * inner + outer], MAXDIL + (inner - 1) * dilation, count, 0
+                )
+                piece_c = lax.dynamic_slice_in_dim(
+                    col_part[3 * outer + inner], MAXDIL + (inner - 1) * dilation, count, 0
+                )
+                along_rows = piece_r if along_rows is None else along_rows + piece_r
+                along_cols = piece_c if along_cols is None else along_cols + piece_c
+            by_col.append(along_rows)
+            by_row.append(along_cols)
+        own = lax.dynamic_slice_in_dim(padded, start, count, 0)
+        own_row = jnp.where(lower, own, 0.0) + shift_bias[None, :]
+        own_col = jnp.where(lower, 0.0, own)
+        row_tables = [
+            own_row + by_col[1] + by_col[2],
+            own_row + by_col[0] + by_col[1] + by_col[2],
+            own_row + by_col[0] + by_col[1],
+        ]
+        col_tables = [
+            own_col + by_row[1] + by_row[2],
+            own_col + by_row[0] + by_row[1] + by_row[2],
+            own_col + by_row[0] + by_row[1],
+        ]
+        return row_tables, col_tables
 
     row_places = row_start - MAXDIL + jnp.arange(rows)
     col_places = col_start - MAXDIL + jnp.arange(cols)
+    rows_row_tables, rows_col_tables = tables(row_start, rows)
+    cols_row_tables, cols_col_tables = tables(col_start, cols)
 
-    padded = jnp.pad(every, ((MAXDIL, MAXDIL), (0, 0)))
-    lower = jnp.arange(every.shape[1]) < half
-    own_row = jnp.where(lower, padded, 0.0) + shift_bias[None, :]
-    own_col = jnp.where(lower, 0.0, padded)
-    row_tables = [
-        own_row + by_col[1] + by_col[2],
-        own_row + by_col[0] + by_col[1] + by_col[2],
-        own_row + by_col[0] + by_col[1],
-    ]
-    col_tables = [
-        own_col + by_row[1] + by_row[2],
-        own_col + by_row[0] + by_row[1] + by_row[2],
-        own_col + by_row[0] + by_row[1],
-    ]
-
-    def pick(tables, start, count, places, axis):
-        low, mid, high = (at(table, start, count) for table in tables)
+    def pick(tables_here, places, axis):
+        low, mid, high = tables_here
         shape = [1, 1, 1]
         shape[axis] = -1
         near_low = (places < dilation).reshape(shape)
         near_high = (places >= bins_total - dilation).reshape(shape)
-        return jnp.where(near_low, low[:, None, :], jnp.where(near_high, high[:, None, :], mid[:, None, :])) if axis == 1 else jnp.where(
-            near_low, low[None, :, :], jnp.where(near_high, high[None, :, :], mid[None, :, :])
-        )
+        if axis == 1:
+            low, mid, high = low[:, None, :], mid[:, None, :], high[:, None, :]
+        else:
+            low, mid, high = low[None, :, :], mid[None, :, :], high[None, :, :]
+        return jnp.where(near_low, low, jnp.where(near_high, high, mid))
 
     mixed = (
-        pick(row_tables, row_start, rows, col_places, 1)
-        + pick(col_tables, col_start, cols, row_places, 0)
+        pick(rows_row_tables, col_places, 1) + pick(cols_col_tables, row_places, 0)
     ).astype(jnp.bfloat16)
     mixed_mirror = (
-        pick(row_tables, col_start, cols, row_places, 0)
-        + pick(col_tables, row_start, rows, col_places, 1)
+        pick(cols_row_tables, row_places, 0) + pick(rows_col_tables, col_places, 1)
     ).astype(jnp.bfloat16)
     return mixed, mixed_mirror, row_places, col_places
 

time: 46.6 us -> 45.5 us (0.976)
  other arithmetic: 10.4 us -> 9.31 us
  local copies, waits for them, and re-layouts: 14.9 us -> 14.2 us
  between operations: 5.64 us -> 6.29 us
    dynamic_slice x12 -> x0, local copies, waits for them, and re-layouts: 1.05 us -> none  [at(): return lax.dynamic_slice_in_dim(table, start, count, 0)]
    add x3 -> x6, other arithmetic: 2.24 us -> 1.25 us  [the longest x2 0.37 us: tables(): own_row + by_col[0] + by_col[1] + by_col[2]]
    add x0 -> x6, local copies, waits for them, and re-layouts: none -> 0.47 us  [the longest x1 0.08 us: tables(): own_col + by_row[1] + by_row[2]]
    dot_general x2 -> x4, matrix products: 1.16 us -> 1.19 us  [the longest x2 0.6 us: tables(): jnp.einsum('nk,tok->tno', window[:, half:], taps[:, :, half:], preferred_...]
where the time goes in v5:
time: 45.5 us; the launch traced here: 45.1 us
  local copies, waits for them, and re-layouts  14.2 us (31%)
  starting transfers between devices  11.5 us (25%)
  other arithmetic  9.31 us (20%)
  between operations  6.29 us (14%)
  matrix products  3.88 us (9%)
    all_to_all x1, starting transfers between devices, gather_projections(): lax.all_to_all(copies, axes, 0, 0, tiled=True).reshape(-1, proj.shape[1])  11.5 us
    unnamed x13, local copies, waits for them, and re-layouts  7.63 us
    mul x1, other arithmetic, local(): conv1 = tap_groups(jax.nn.relu(map1) * mask1, taps1, dilations[1])  5.89 us
    dot_general x1, matrix products, tap_groups(): summed = jnp.dot(stacked, flat_weight, preferred_element_type=jnp.float32)  1.85 us
    transpose x1, local copies, waits for them, and re-layouts, local(): return jnp.transpose(pair, (2, 0, 1))  1.65 us
    slice x1, local copies, waits for them, and re-layouts, local(): conv1 = tap_groups(jax.nn.relu(map1) * mask1, taps1, dilations[1])  1.39 us
    lt x2, other arithmetic, pick(): near_low = (places < dilation).reshape(shape)  1.29 us
    squeeze x1, local copies, waits for them, and re-layouts, local(): conv_weight[1]  1.06 us
  transfers between devices with their start and end apart: 1, of which 0 were waited for; matrix products, arithmetic and copies ran while one was open for 11% of the time, Pallas kernels for 0%

profile of v5, /device:TPU:1, one launch (start us, length us, event | category | flops | bytes accessed | tf_op | source)
XLA Modules:
  0.0 45.1 jit_solution(11104116395500832103)
XLA Ops:
  0.0 0.7 %copy-done = bf16[8,128]{1,0:T(8,128)(2,1)S(1)} copy-done((bf16[8,128]{1,0:T(8,128)(2,1)S(1)}, bf16[8,128]{1,0:T(8,128)(2,1)}, u32[]{:S(2)}) %copy-start) | copy-done | bytes 2072
  0.7 0.8 %fusion.2 = bf16[8,64]{1,0:T(8,128)(2,1)S(1)} fusion(bf16[8,128]{1,0:T(8,128)(2,1)S(1)} %copy-done, bf16[128,32]{0,1:T(8,128)(2,1)} %param.8, bf16[128,32]{0,1:T(8,128)(2,1)} %param.7), kind=kOutput, calls=%fused_computation.15 | convolution fusion | flops 164352 | bytes 19456 | tf_op jit(solution)/shard_map/dot_general | solution.py:118
  1.6 0.9 %reshape.204 = bf16[128,2,256]{2,1,0:T(2,128)(2,1)} reshape(bf16[128,8,64]{2,1,0:T(8,128)(2,1)S(1)} %broadcast_in_dim.172) | data formatting | bytes 262144
  2.4 11.5 %all-to-all-start = ((bf16[128,2,256]{2,1,0:T(2,128)(2,1)}), bf16[128,2,256]{2,1,0:T(2,128)(2,1)S(1)}, u32[]{:S(2)}, u32[]{:S(2)}) async-start(bf16[128,2,256]{2,1,0:T(2,128)(2,1)} %reshape.204), calls=%async_computation | async-start | bytes 262144 | tf_op jit(solution)/shard_map/all_to_all | solution.py:14
  14.0 0.8 %slice_bitcast_fusion = (f32[64]{0:T(128)S(1)}, f32[64]{0:T(128)S(1)}) fusion(f32[2,64]{1,0:T(2,128)} %param.10), kind=kLoop, calls=%fused_computation.108 | loop fusion | bytes 1024 | tf_op jit(solution)/shard_map/add | solution.py:142
  14.7 1.4 %fusion.73 = (s32[1]{0:T(128)}, s32[1]{0:T(128)}) fusion(s32[2]{0:T(128)} %param.11), kind=kLoop, calls=%fused_computation.128 | loop fusion | bytes 16 | tf_op jit(solution)/shard_map/slice | solution.py:139
  16.8 1.1 %slice_bitcast_fusion.2 = (bf16[9,64,64]{2,1,0:T(8,128)(2,1)S(1)}, bf16[1,9,64,64]{3,2,1,0:T(8,128)(2,1)S(1)}, bf16[1,9,64,64]{3,2,1,0:T(8,128)(2,1)S(1)}) fusion(bf16[2,9,64,64]{3,2,1,0:T(8,128)(2,1)} %param.9), kind=kLoop, calls=%fused_computation.119 | loop fusion | bytes 368640 | tf_op jit(solution)/shard_map/squeeze | solution.py:138
  18.0 0.6 %fusion.51 = pred[72]{0:T(512)(128)(4,1)S(1)} fusion(s32[]{:T(128)} %bitcast, s32[]{:T(128)S(6)} %sub.14), kind=kLoop, calls=%fused_computation.111 | loop fusion | flops 144 | bytes 80 | tf_op jit(solution)/shard_map/lt | solution.py:99
  24.4 0.7 %fusion.49 = pred[136]{0:T(512)(128)(4,1)S(1)} fusion(s32[]{:T(128)} %bitcast, s32[]{:T(128)S(6)} %sub.12), kind=kLoop, calls=%fused_computation.107 | loop fusion | flops 272 | bytes 144 | tf_op jit(solution)/shard_map/lt | solution.py:99
  25.9 0.3 convolution_bitcast_fusion.1
  26.3 0.3 convolution_bitcast_fusion
  28.5 5.9 %maximum_multiply_fusion = (bf16[72,136,64]{1,2,0:T(8,128)(2,1)S(1)}, bf16[72,136,64]{1,2,0:T(8,128)(2,1)S(1)}) fusion(bf16[72,136]{1,0:T(8,128)(2,1)S(1)} %multiply_convert_fusion.2, f32[72,64]{1,0:T(8,128)S(1)} %copy.26, f32[72,64]{1,0:T(8,128)S(1)} %copy.25, f32[72,64]{1,0:T(8,128)S(1)} %copy.24, f32[136,64]{0,1:T(8,128)S(1)} %get-tuple-element.17, ...), kind=kLoop, calls=%fused_computation.3 | loop fusion | flops 11907072 | bytes 2846240 | tf_op jit(solution)/shard_map/mul | solution.py:139
  34.4 0.5 %dynamic-slice_dynamic-update-slice_fusion.7 = bf16[64,128,576]{1,2,0:T(8,128)(2,1)S(1)} fusion(bf16[72,136,64]{1,2,0:T(8,128)(2,1)S(1)} %get-tuple-element.5, s32[]{:T(128)S(6)} %select_n.128, s32[]{:T(128)S(6)} %select_n.129), kind=kLoop, calls=%fused_computation.25 | loop fusion | bytes 2097160
  34.9 0.7 %dynamic-slice_dynamic-update-slice_fusion.6 = bf16[64,128,576]{1,2,0:T(8,128)(2,1)S(1)} fusion(bf16[64,128,576]{1,2,0:T(8,128)(2,1)S(1)} %dynamic-slice_dynamic-update-slice_fusion.7, bf16[72,136,64]{1,2,0:T(8,128)(2,1)S(1)} %get-tuple-element.5, s32[]{:T(128)S(6)} %select_n.128), kind=kLoop, calls=%fused_computation.24 | loop fusion | bytes 2097156
  35.6 0.8 %dynamic-slice_dynamic-update-slice_fusion.5 = bf16[64,128,576]{1,2,0:T(8,128)(2,1)S(1)} fusion(bf16[64,128,576]{1,2,0:T(8,128)(2,1)S(1)} %dynamic-slice_dynamic-update-slice_fusion.6, bf16[72,136,64]{1,2,0:T(8,128)(2,1)S(1)} %get-tuple-element.5, s32[]{:T(128)S(6)} %select_n.128, s32[]{:T(128)S(6)} %select_n.130), kind=kLoop, calls=%fused_computation.23 | loop fusion | bytes 2097160
  36.4 0.8 %dynamic-slice_dynamic-update-slice_fusion.4 = bf16[64,128,576]{1,2,0:T(8,128)(2,1)S(1)} fusion(bf16[64,128,576]{1,2,0:T(8,128)(2,1)S(1)} %dynamic-slice_dynamic-update-slice_fusion.5, bf16[72,136,64]{1,2,0:T(8,128)(2,1)S(1)} %get-tuple-element.5, s32[]{:T(128)S(6)} %select_n.129), kind=kLoop, calls=%fused_computation.22 | loop fusion | bytes 2097156
  37.2 0.7 %slice_dynamic-update-slice_fusion = bf16[64,128,576]{1,2,0:T(8,128)(2,1)S(1)} fusion(bf16[64,128,576]{1,2,0:T(8,128)(2,1)S(1)} %dynamic-slice_dynamic-update-slice_fusion.4, bf16[72,136,64]{1,2,0:T(8,128)(2,1)S(1)} %get-tuple-element.5), kind=kLoop, calls=%fused_computation.17 | loop fusion | bytes 2097152
  37.9 0.8 %dynamic-slice_dynamic-update-slice_fusion.3 = bf16[64,128,576]{1,2,0:T(8,128)(2,1)S(1)} fusion(bf16[64,128,576]{1,2,0:T(8,128)(2,1)S(1)} %slice_dynamic-update-slice_fusion, bf16[72,136,64]{1,2,0:T(8,128)(2,1)S(1)} %get-tuple-element.5, s32[]{:T(128)S(6)} %select_n.130), kind=kLoop, calls=%fused_computation.21 | loop fusion | bytes 2097156
  38.7 0.8 %dynamic-slice_dynamic-update-slice_fusion.2 = bf16[64,128,576]{1,2,0:T(8,128)(2,1)S(1)} fusion(bf16[64,128,576]{1,2,0:T(8,128)(2,1)S(1)} %dynamic-slice_dynamic-update-slice_fusion.3, bf16[72,136,64]{1,2,0:T(8,128)(2,1)S(1)} %get-tuple-element.5, s32[]{:T(128)S(6)} %select_n.131, s32[]{:T(128)S(6)} %select_n.129), kind=kLoop, calls=%fused_computation.20 | loop fusion | bytes 2097160
  39.4 0.7 %dynamic-slice_dynamic-update-slice_fusion.1 = bf16[64,128,576]{1,2,0:T(8,128)(2,1)S(1)} fusion(bf16[64,128,576]{1,2,0:T(8,128)(2,1)S(1)} %dynamic-slice_dynamic-update-slice_fusion.2, bf16[72,136,64]{1,2,0:T(8,128)(2,1)S(1)} %get-tuple-element.5, s32[]{:T(128)S(6)} %select_n.131), kind=kLoop, calls=%fused_computation.19 | loop fusion | bytes 2097156
  40.2 0.8 %dynamic-slice_dynamic-update-slice_fusion = bf16[64,128,576]{1,2,0:T(8,128)(2,1)S(1)} fusion(bf16[64,128,576]{1,2,0:T(8,128)(2,1)S(1)} %dynamic-slice_dynamic-update-slice_fusion.1, bf16[72,136,64]{1,2,0:T(8,128)(2,1)S(1)} %get-tuple-element.5, s32[]{:T(128)S(6)} %select_n.131, s32[]{:T(128)S(6)} %select_n.130), kind=kLoop, calls=%fused_computation.18 | loop fusion | bytes 2097160 | tf_op jit(solution)/shard_map/concatenate | solution.py:35
  40.9 1.9 %fusion.74 = f32[64,128,128]{1,2,0:T(8,128)S(1)} fusion(bf16[64,128,576]{1,2,0:T(8,128)(2,1)S(1)} %dynamic-slice_dynamic-update-slice_fusion, bf16[576,128,1]{1,0,2:T(8,128)(2,1)S(1)} %bitcast.120), kind=kOutput, calls=%fused_computation.129 | convolution fusion | flops 1207959552 | bytes 13778944 | tf_op jit(solution)/shard_map/dot_general | solution.py:37
  42.8 0.7 %fusion.3 = bf16[64,64,128]{2,0,1:T(8,128)(2,1)S(1)} fusion(f32[64,128,128]{1,2,0:T(8,128)S(1)} %fusion.74, bf16[72,136,64]{1,2,0:T(8,128)(2,1)S(1)} %get-tuple-element.6, f32[64]{0:T(128)S(1)} %get-tuple-element.54), kind=kLoop, calls=%fused_computation.16 | loop fusion | flops 5767168 | bytes 6291712 | tf_op jit(solution)/shard_map/transpose | solution.py:148
  43.5 1.6 %copy.29 = bf16[64,64,128]{2,1,0:T(8,128)(2,1)} copy(bf16[64,64,128]{2,0,1:T(8,128)(2,1)S(1)} %fusion.3) | data formatting | bytes 2097152 | tf_op jit(solution)/shard_map/transpose | solution.py:148
  (30 shorter events, 3.3 us)
Async XLA Ops:
  0.0 0.7 %copy-start = (bf16[8,128]{1,0:T(8,128)(2,1)S(1)}, bf16[8,128]{1,0:T(8,128)(2,1)}, u32[]{:S(2)}) copy-start(bf16[8,128]{1,0:T(8,128)(2,1)} %param.6) | copy-start | bytes 6148
  2.4 22.6 %all-to-all-start = ((bf16[128,2,256]{2,1,0:T(2,128)(2,1)}), bf16[128,2,256]{2,1,0:T(2,128)(2,1)S(1)}, u32[]{:S(2)}, u32[]{:S(2)}) async-start(bf16[128,2,256]{2,1,0:T(2,128)(2,1)} %reshape.204), calls=%async_computation | async-start | bytes 262144 | tf_op jit(solution)/shard_map/all_to_all | solution.py:14

commit v6 on v5

--- a/solution.py
+++ b/solution.py
@@ -40,6 +40,16 @@
 
 def mirrored_taps(weights):
     return weights.reshape(3, 3, *weights.shape[1:]).swapaxes(0, 1).reshape(weights.shape)
+
+
+def packed_rows(places, channels):
+    return jnp.repeat(places.reshape(-1, 2), channels, axis=1)[:, None, :]
+
+
+def unpack(packed, channels):
+    halves, cols = packed.shape[0], packed.shape[1]
+    split = packed.reshape(halves, cols, 2, channels)
+    return jnp.transpose(split, (0, 2, 1, 3)).reshape(2 * halves, cols, channels)
 
 
 def first_layer(every, taps, shift_bias, dilation, row_start, rows, col_start, cols):
@@ -92,23 +102,27 @@
     rows_row_tables, rows_col_tables = tables(row_start, rows)
     cols_row_tables, cols_col_tables = tables(col_start, cols)
 
-    def pick(tables_here, places, axis):
-        low, mid, high = tables_here
-        shape = [1, 1, 1]
-        shape[axis] = -1
-        near_low = (places < dilation).reshape(shape)
-        near_high = (places >= bins_total - dilation).reshape(shape)
-        if axis == 1:
-            low, mid, high = low[:, None, :], mid[:, None, :], high[:, None, :]
-        else:
-            low, mid, high = low[None, :, :], mid[None, :, :], high[None, :, :]
-        return jnp.where(near_low, low, jnp.where(near_high, high, mid))
+    def over_rows(table):
+        return table.reshape(rows // 2, 1, 2 * table.shape[1])
 
+    def over_cols(table):
+        return jnp.concatenate([table, table], axis=1)[None]
+
+    def pick(tables_here, along_rows, class_places):
+        low, mid, high = (over_rows(t) if along_rows else over_cols(t) for t in tables_here)
+        return jnp.where(
+            class_places < dilation,
+            low,
+            jnp.where(class_places >= bins_total - dilation, high, mid),
+        )
+
+    row_class = packed_rows(row_places, every.shape[1])
+    col_class = col_places[None, :, None]
     mixed = (
-        pick(rows_row_tables, col_places, 1) + pick(cols_col_tables, row_places, 0)
+        pick(rows_row_tables, True, col_class) + pick(cols_col_tables, False, row_class)
     ).astype(jnp.bfloat16)
     mixed_mirror = (
-        pick(cols_row_tables, row_places, 0) + pick(rows_col_tables, col_places, 1)
+        pick(cols_row_tables, False, row_class) + pick(rows_col_tables, True, col_class)
     ).astype(jnp.bfloat16)
     return mixed, mixed_mirror, row_places, col_places
 
@@ -132,14 +146,15 @@
         jnp.bfloat16
     )
 
+    channels = conv_weight.shape[2]
     mask1 = (
-        inside(row_places, bins_total)[:, None, None] * inside(col_places, bins_total)[None, :, None]
+        inside(packed_rows(row_places, channels), bins_total)
+        * inside(col_places, bins_total)[None, :, None]
     ).astype(jnp.bfloat16)
     taps1 = jnp.concatenate([conv_weight[1], mirrored_taps(conv_weight[1])], axis=1)
-    conv1 = tap_groups(jax.nn.relu(map1) * mask1, taps1, dilations[1])
-    channels = conv_weight.shape[2]
+    conv1 = tap_groups(unpack(jax.nn.relu(map1) * mask1, channels), taps1, dilations[1])
     core = (slice(MAXDIL, MAXDIL + row_size), slice(MAXDIL, MAXDIL + col_size), slice(None))
-    base1 = map1[core].astype(jnp.float32) + conv_bias[1][None, None, :]
+    base1 = unpack(map1, channels)[core].astype(jnp.float32) + conv_bias[1][None, None, :]
     mixed1 = (base1 + conv1[:, :, :channels]).astype(jnp.bfloat16)
     mixed1_mirror = (base1 + conv1[:, :, channels:]).astype(jnp.bfloat16)
     pair = (0.5 * (mixed1.astype(jnp.float32) + mixed1_mirror.astype(jnp.float32))).astype(

time: 45.5 us -> 80 us (1.76)
  local copies, waits for them, and re-layouts: 14.2 us -> 41.7 us
  other arithmetic: 9.31 us -> 16.1 us
    dynamic_slice x0 -> x1, local copies, waits for them, and re-layouts: none -> 13.7 us  [tap_groups(): lax.dynamic_slice(padded, (row_index, col_index, zero_index), (row_count,...]
    reshape x0 -> x2, local copies, waits for them, and re-layouts: none -> 7.64 us  [unpack(): jnp.transpose(split, (0, 2, 1, 3)).reshape(2 * halves, cols, channels)]
    slice x1 -> x2, local copies, waits for them, and re-layouts: 1.39 us -> 4.31 us  [the longest x1 2.92 us: local(): unpack(map1, channels)[core].astype(jnp.float32)]
    mul x1, other arithmetic: 5.89 us -> 8.38 us  [local(): jax.nn.relu(map1) * mask1]
    concatenate x0 -> x4, other arithmetic: none -> 2.09 us
    another operation x0 -> x1, other arithmetic: none -> 2.06 us
    another operation x0 -> x2, local copies, waits for them, and re-layouts: none -> 2.05 us
    broadcast_in_dim x0 -> x15, local copies, waits for them, and re-layouts: none -> 1.12 us  [the longest x8 0.73 us: pick(): jnp.where(class_places >= bins_total - dilation, high, mid)]
  transfers between devices with their start and end apart: 1 -> 1, of which waited for: 0 -> 0; matrix products, arithmetic and copies ran while one was open for 11% -> 6% of each run, Pallas kernels for 0% -> 0%
where the time goes in v6:
time: 80 us; the launch traced here: 79.4 us
  local copies, waits for them, and re-layouts  41.7 us (52%)
  other arithmetic  16.1 us (20%)
  starting transfers between devices  11.5 us (14%)
  between operations  6.28 us (8%)
  matrix products  3.88 us (5%)
    dynamic_slice x1, local copies, waits for them, and re-layouts, tap_groups(): lax.dynamic_slice(padded, (row_index, col_index, zero_index), (row_count,...  13.7 us
    all_to_all x1, starting transfers between devices, gather_projections(): lax.all_to_all(copies, axes, 0, 0, tiled=True).reshape(-1, proj.shape[1])  11.5 us
    mul x1, other arithmetic, local(): jax.nn.relu(map1) * mask1  8.38 us
    unnamed x13, local copies, waits for them, and re-layouts  7.81 us
    reshape x2, local copies, waits for them, and re-layouts, unpack(): jnp.transpose(split, (0, 2, 1, 3)).reshape(2 * halves, cols, channels)  7.64 us
    slice x1, local copies, waits for them, and re-layouts, local(): unpack(map1, channels)[core].astype(jnp.float32)  2.92 us
    another operation x1, other arithmetic  2.06 us
    another operation x2, local copies, waits for them, and re-layouts  2.05 us
  transfers between devices with their start and end apart: 1, of which 0 were waited for; matrix products, arithmetic and copies ran while one was open for 6% of the time, Pallas kernels for 0%

profile of v6, /device:TPU:1, one launch (start us, length us, event | category | flops | bytes accessed | tf_op | source)
XLA Modules:
  0.0 79.4 jit_solution(12563964876282522173)
XLA Ops:
  0.7 0.8 %fusion.3 = bf16[8,64]{1,0:T(8,128)(2,1)S(1)} fusion(bf16[8,128]{1,0:T(8,128)(2,1)S(1)} %copy-done, bf16[128,32]{0,1:T(8,128)(2,1)} %param.8, bf16[128,32]{0,1:T(8,128)(2,1)} %param.7), kind=kOutput, calls=%fused_computation.18 | convolution fusion | flops 164352 | bytes 19456 | tf_op jit(solution)/shard_map/dot_general | solution.py:132
  1.6 0.9 %reshape.211 = bf16[128,2,256]{2,1,0:T(2,128)(2,1)} reshape(bf16[128,8,64]{2,1,0:T(8,128)(2,1)S(1)} %broadcast_in_dim.186) | data formatting | bytes 262144
  2.5 11.5 %all-to-all-start = ((bf16[128,2,256]{2,1,0:T(2,128)(2,1)}), bf16[128,2,256]{2,1,0:T(2,128)(2,1)S(1)}, u32[]{:S(2)}, u32[]{:S(2)}) async-start(bf16[128,2,256]{2,1,0:T(2,128)(2,1)} %reshape.211), calls=%async_computation | async-start | bytes 262144 | tf_op jit(solution)/shard_map/all_to_all | solution.py:14
  14.0 0.8 slice_bitcast_fusion
  14.7 1.4 %fusion.76 = (s32[1]{0:T(128)}, s32[1]{0:T(128)}) fusion(s32[2]{0:T(128)} %param.11), kind=kLoop, calls=%fused_computation.146 | loop fusion | bytes 16 | tf_op jit(solution)/shard_map/slice | solution.py:155
  17.4 1.0 %slice_bitcast_fusion.2 = (bf16[9,64,64]{2,1,0:T(8,128)(2,1)S(1)}, bf16[1,9,64,64]{3,2,1,0:T(8,128)(2,1)S(1)}, bf16[1,9,64,64]{3,2,1,0:T(8,128)(2,1)S(1)}) fusion(bf16[2,9,64,64]{3,2,1,0:T(8,128)(2,1)} %param.9), kind=kLoop, calls=%fused_computation.135 | loop fusion | bytes 368640 | tf_op jit(solution)/shard_map/squeeze | solution.py:154
  29.5 8.4 %fusion = (bf16[36,136,128]{1,0,2:T(8,128)(2,1)S(1)}, bf16[36,136,128]{1,0,2:T(8,128)(2,1)}) fusion(f32[136]{0:T(256)S(1)} %get-tuple-element.71, f32[36,128]{0,1:T(8,128)S(1)} %bitcast.130, f32[36,128]{0,1:T(8,128)S(1)} %copy.67, f32[36,128]{0,1:T(8,128)S(1)} %copy.65, f32[36,128]{0,1:T(8,128)S(1)} %copy.63, f32[136,128]{0,1:T(8,128)S(1)} %get-tuple-element.84, ...), kind=kLoop, calls=%fused_computation.4 | loop fusion | flops 13160448 | bytes 3063600 | tf_op jit(solution)/shard_map/mul | solution.py:155
  38.1 2.1 %pad_maximum_fusion.1 = bf16[36,272,64]{1,0,2:T(8,128)(2,1)} fusion(bf16[36,136,64]{1,0,2:T(8,128)(2,1)S(1)} %get-tuple-element.26, bf16[36,136,64]{1,0,2:T(8,128)(2,1)S(1)} %get-tuple-element.25), kind=kLoop, calls=%fused_computation.12 | loop fusion | flops 2506752 | bytes 2506752 | tf_op jit(solution)/shard_map/concatenate.1
  40.1 3.2 %reshape.203 = bf16[72,136,64]{1,0,2:T(8,128)(2,1)S(1)} reshape(bf16[36,272,64]{1,0,2:T(8,128)(2,1)} %pad_maximum_fusion.1) | data formatting | bytes 2506752 | tf_op jit(solution)/shard_map/reshape | solution.py:52
  43.3 1.9 %fusion.70 = (bf16[36,136,64]{1,0,2:T(8,128)(2,1)S(1)}, bf16[36,136,64]{1,0,2:T(8,128)(2,1)S(1)}) fusion(bf16[36,136,128]{1,0,2:T(8,128)(2,1)} %get-tuple-element.6), kind=kLoop, calls=%fused_computation.140 | loop fusion | bytes 2506752 | tf_op jit(solution)/shard_map/slice.12
  45.2 2.0 %pad_maximum_fusion = bf16[36,272,64]{1,0,2:T(8,128)(2,1)} fusion(bf16[36,136,64]{1,0,2:T(8,128)(2,1)S(1)} %get-tuple-element.24, bf16[36,136,64]{1,0,2:T(8,128)(2,1)S(1)} %get-tuple-element.23), kind=kLoop, calls=%fused_computation.11 | loop fusion | flops 2506752 | bytes 2506752 | tf_op jit(solution)/shard_map/concatenate
  47.2 4.5 %reshape.202 = bf16[72,136,64]{1,0,2:T(8,128)(2,1)} reshape(bf16[36,272,64]{1,0,2:T(8,128)(2,1)} %pad_maximum_fusion) | data formatting | bytes 2506752 | tf_op jit(solution)/shard_map/reshape | solution.py:52
  51.7 2.9 %slice.239 = bf16[64,128,64]{1,0,2:T(8,128)(2,1)S(1)} slice(bf16[72,136,64]{1,0,2:T(8,128)(2,1)} %reshape.202), slice={[4:68], [4:132], [0:64]} | slice | bytes 2097152 | tf_op jit(solution)/shard_map/slice | solution.py:157
  54.6 13.7 %constant_dynamic-slice_fusion.2 = (bf16[64,128,64]{1,0,2:T(8,128)(2,1)S(1)}, bf16[64,128,64]{1,0,2:T(8,128)(2,1)S(1)}, bf16[64,128,64]{1,0,2:T(8,128)(2,1)S(1)}...) fusion(bf16[72,136,64]{1,0,2:T(8,128)(2,1)S(1)} %reshape.203, ...), kind=kLoop, calls=%fused_computation.110 | loop fusion | bytes 18874384 | tf_op jit(solution)/shard_map/dynamic_slice | solution.py:31
  69.0 0.7 copy_dynamic-update-slice_fusion.7
  69.8 0.7 copy_dynamic-update-slice_fusion.6
  70.5 0.7 copy_dynamic-update-slice_fusion.5
  71.3 0.7 copy_dynamic-update-slice_fusion.4
  72.0 0.7 copy_dynamic-update-slice_fusion.3
  72.8 0.7 copy_dynamic-update-slice_fusion.2
  73.5 0.7 copy_dynamic-update-slice_fusion.1
  75.0 1.8 %fusion.77 = f32[64,128,128]{1,2,0:T(8,128)S(1)} fusion(bf16[64,128,576]{1,2,0:T(8,128)(2,1)S(1)} %copy_dynamic-update-slice_fusion, bf16[576,128,1]{1,0,2:T(8,128)(2,1)S(1)} %bitcast.127), kind=kOutput, calls=%fused_computation.147 | convolution fusion | flops 1207959552 | bytes 13778944 | tf_op jit(solution)/shard_map/dot_general | solution.py:37
  76.9 0.9 %fusion.4 = bf16[64,64,128]{2,0,1:T(8,128)(2,1)S(1)} fusion(f32[64,128,128]{1,2,0:T(8,128)S(1)} %fusion.77, bf16[64,128,64]{1,0,2:T(8,128)(2,1)S(1)} %slice.239, f32[64]{0:T(128)S(1)} %get-tuple-element.67), kind=kLoop, calls=%fused_computation.19 | loop fusion | flops 5767168 | bytes 6291712 | tf_op jit(solution)/shard_map/transpose | solution.py:163
  77.8 1.6 %copy.80 = bf16[64,64,128]{2,1,0:T(8,128)(2,1)} copy(bf16[64,64,128]{2,0,1:T(8,128)(2,1)S(1)} %fusion.4) | data formatting | bytes 2097152 | tf_op jit(solution)/shard_map/transpose | solution.py:163
  (56 shorter events, 8.6 us)
Async XLA Ops:
  0.0 0.7 copy-start
  2.5 22.3 %all-to-all-start = ((bf16[128,2,256]{2,1,0:T(2,128)(2,1)}), bf16[128,2,256]{2,1,0:T(2,128)(2,1)S(1)}, u32[]{:S(2)}, u32[]{:S(2)}) async-start(bf16[128,2,256]{2,1,0:T(2,128)(2,1)} %reshape.211), calls=%async_computation | async-start | bytes 262144 | tf_op jit(solution)/shard_map/all_to_all | solution.py:14

commit v7 on v5

--- a/solution.py
+++ b/solution.py
@@ -10,7 +10,8 @@
 def gather_projections(proj):
     axes = ("row", "col")
     count = lax.axis_size("row") * lax.axis_size("col")
-    copies = jnp.broadcast_to(proj[None], (count,) + proj.shape)
+    flat = proj.reshape(2, -1)
+    copies = jnp.broadcast_to(flat[None], (count,) + flat.shape)
     return lax.all_to_all(copies, axes, 0, 0, tiled=True).reshape(-1, proj.shape[1])
 
 

time: 45.5 us -> 45.4 us (level)
    unnamed x13 -> x11, local copies, waits for them, and re-layouts: 7.63 us -> 6.54 us
    broadcast_in_dim x1 -> x2, local copies, waits for them, and re-layouts: 0.05 us -> 0.83 us  [gather_projections(): copies = jnp.broadcast_to(flat[None], (count,) + flat.shape)]
where the time goes in v7:
time: 45.4 us; the launch traced here: 45 us
  local copies, waits for them, and re-layouts  14.1 us (31%)
  starting transfers between devices  11.5 us (25%)
  other arithmetic  9.31 us (21%)
  between operations  6.28 us (14%)
  matrix products  3.88 us (9%)
    all_to_all x1, starting transfers between devices, gather_projections(): lax.all_to_all(copies, axes, 0, 0, tiled=True).reshape(-1, proj.shape[1])  11.5 us
    unnamed x11, local copies, waits for them, and re-layouts  6.54 us
    mul x1, other arithmetic, local(): conv1 = tap_groups(jax.nn.relu(map1) * mask1, taps1, dilations[1])  5.89 us
    dot_general x1, matrix products, tap_groups(): summed = jnp.dot(stacked, flat_weight, preferred_element_type=jnp.float32)  1.85 us
    transpose x1, local copies, waits for them, and re-layouts, local(): return jnp.transpose(pair, (2, 0, 1))  1.65 us
    slice x1, local copies, waits for them, and re-layouts, local(): conv1 = tap_groups(jax.nn.relu(map1) * mask1, taps1, dilations[1])  1.39 us
    lt x2, other arithmetic, pick(): near_low = (places < dilation).reshape(shape)  1.29 us
    squeeze x1, local copies, waits for them, and re-layouts, local(): conv_weight[1]  1.06 us
  transfers between devices with their start and end apart: 1, of which 0 were waited for; matrix products, arithmetic and copies ran while one was open for 11% of the time, Pallas kernels for 0%

profile of v7, /device:TPU:1, one launch (start us, length us, event | category | flops | bytes accessed | tf_op | source)
XLA Modules:
  0.0 45.0 jit_solution(15243077488144467447)
XLA Ops:
  0.0 0.7 %copy-done = bf16[8,128]{1,0:T(8,128)(2,1)S(1)} copy-done((bf16[8,128]{1,0:T(8,128)(2,1)S(1)}, bf16[8,128]{1,0:T(8,128)(2,1)}, u32[]{:S(2)}) %copy-start) | copy-done | bytes 2072
  0.7 0.8 %fusion.2 = bf16[8,64]{1,0:T(8,128)(2,1)S(1)} fusion(bf16[8,128]{1,0:T(8,128)(2,1)S(1)} %copy-done, bf16[128,32]{0,1:T(8,128)(2,1)} %param.8, bf16[128,32]{0,1:T(8,128)(2,1)} %param.7), kind=kOutput, calls=%fused_computation.15 | convolution fusion | flops 164352 | bytes 19456 | tf_op jit(solution)/shard_map/dot_general | solution.py:119
  1.6 0.7 %broadcast_in_dim.174 = bf16[128,2,256]{2,1,0:T(2,128)(2,1)} broadcast(bf16[2,256]{1,0:T(2,128)(2,1)S(1)} %broadcast_in_dim.173), dimensions={1,2} | broadcast | bytes 132096 | tf_op jit(solution)/shard_map/broadcast_in_dim | solution.py:14
  2.3 11.5 %all-to-all-start = ((bf16[128,2,256]{2,1,0:T(2,128)(2,1)}), bf16[128,2,256]{2,1,0:T(2,128)(2,1)S(1)}, u32[]{:S(2)}, u32[]{:S(2)}) async-start(bf16[128,2,256]{2,1,0:T(2,128)(2,1)} %broadcast_in_dim.174), calls=%async_computation | async-start | bytes 262144 | tf_op jit(solution)/shard_map/all_to_all | solution.py:15
  13.9 0.8 %slice_bitcast_fusion = (f32[64]{0:T(128)S(1)}, f32[64]{0:T(128)S(1)}) fusion(f32[2,64]{1,0:T(2,128)} %param.10), kind=kLoop, calls=%fused_computation.108 | loop fusion | bytes 1024 | tf_op jit(solution)/shard_map/add | solution.py:143
  14.6 1.4 %fusion.73 = (s32[1]{0:T(128)}, s32[1]{0:T(128)}) fusion(s32[2]{0:T(128)} %param.11), kind=kLoop, calls=%fused_computation.128 | loop fusion | bytes 16 | tf_op jit(solution)/shard_map/slice | solution.py:140
  16.7 1.1 %slice_bitcast_fusion.2 = (bf16[9,64,64]{2,1,0:T(8,128)(2,1)S(1)}, bf16[1,9,64,64]{3,2,1,0:T(8,128)(2,1)S(1)}, bf16[1,9,64,64]{3,2,1,0:T(8,128)(2,1)S(1)}) fusion(bf16[2,9,64,64]{3,2,1,0:T(8,128)(2,1)} %param.9), kind=kLoop, calls=%fused_computation.119 | loop fusion | bytes 368640 | tf_op jit(solution)/shard_map/squeeze | solution.py:139
  17.9 0.6 %fusion.51 = pred[72]{0:T(512)(128)(4,1)S(1)} fusion(s32[]{:T(128)} %bitcast, s32[]{:T(128)S(6)} %sub.14), kind=kLoop, calls=%fused_computation.111 | loop fusion | flops 144 | bytes 80 | tf_op jit(solution)/shard_map/lt | solution.py:100
  24.2 0.7 %fusion.49 = pred[136]{0:T(512)(128)(4,1)S(1)} fusion(s32[]{:T(128)} %bitcast, s32[]{:T(128)S(6)} %sub.12), kind=kLoop, calls=%fused_computation.107 | loop fusion | flops 272 | bytes 144 | tf_op jit(solution)/shard_map/lt | solution.py:100
  25.8 0.3 convolution_bitcast_fusion.1
  26.2 0.3 convolution_bitcast_fusion
  28.4 5.9 %maximum_multiply_fusion = (bf16[72,136,64]{1,2,0:T(8,128)(2,1)S(1)}, bf16[72,136,64]{1,2,0:T(8,128)(2,1)S(1)}) fusion(bf16[72,136]{1,0:T(8,128)(2,1)S(1)} %multiply_convert_fusion.2, f32[72,64]{1,0:T(8,128)S(1)} %copy.25, f32[72,64]{1,0:T(8,128)S(1)} %copy.24, f32[72,64]{1,0:T(8,128)S(1)} %copy.23, f32[136,64]{0,1:T(8,128)S(1)} %get-tuple-element.17, ...), kind=kLoop, calls=%fused_computation.3 | loop fusion | flops 11907072 | bytes 2846240 | tf_op jit(solution)/shard_map/mul | solution.py:140
  34.3 0.5 %dynamic-slice_dynamic-update-slice_fusion.7 = bf16[64,128,576]{1,2,0:T(8,128)(2,1)S(1)} fusion(bf16[72,136,64]{1,2,0:T(8,128)(2,1)S(1)} %get-tuple-element.5, s32[]{:T(128)S(6)} %select_n.128, s32[]{:T(128)S(6)} %select_n.129), kind=kLoop, calls=%fused_computation.25 | loop fusion | bytes 2097160
  34.8 0.7 %dynamic-slice_dynamic-update-slice_fusion.6 = bf16[64,128,576]{1,2,0:T(8,128)(2,1)S(1)} fusion(bf16[64,128,576]{1,2,0:T(8,128)(2,1)S(1)} %dynamic-slice_dynamic-update-slice_fusion.7, bf16[72,136,64]{1,2,0:T(8,128)(2,1)S(1)} %get-tuple-element.5, s32[]{:T(128)S(6)} %select_n.128), kind=kLoop, calls=%fused_computation.24 | loop fusion | bytes 2097156
  35.5 0.8 %dynamic-slice_dynamic-update-slice_fusion.5 = bf16[64,128,576]{1,2,0:T(8,128)(2,1)S(1)} fusion(bf16[64,128,576]{1,2,0:T(8,128)(2,1)S(1)} %dynamic-slice_dynamic-update-slice_fusion.6, bf16[72,136,64]{1,2,0:T(8,128)(2,1)S(1)} %get-tuple-element.5, s32[]{:T(128)S(6)} %select_n.128, s32[]{:T(128)S(6)} %select_n.130), kind=kLoop, calls=%fused_computation.23 | loop fusion | bytes 2097160
  36.3 0.8 %dynamic-slice_dynamic-update-slice_fusion.4 = bf16[64,128,576]{1,2,0:T(8,128)(2,1)S(1)} fusion(bf16[64,128,576]{1,2,0:T(8,128)(2,1)S(1)} %dynamic-slice_dynamic-update-slice_fusion.5, bf16[72,136,64]{1,2,0:T(8,128)(2,1)S(1)} %get-tuple-element.5, s32[]{:T(128)S(6)} %select_n.129), kind=kLoop, calls=%fused_computation.22 | loop fusion | bytes 2097156
  37.1 0.7 %slice_dynamic-update-slice_fusion = bf16[64,128,576]{1,2,0:T(8,128)(2,1)S(1)} fusion(bf16[64,128,576]{1,2,0:T(8,128)(2,1)S(1)} %dynamic-slice_dynamic-update-slice_fusion.4, bf16[72,136,64]{1,2,0:T(8,128)(2,1)S(1)} %get-tuple-element.5), kind=kLoop, calls=%fused_computation.17 | loop fusion | bytes 2097152
  37.8 0.8 %dynamic-slice_dynamic-update-slice_fusion.3 = bf16[64,128,576]{1,2,0:T(8,128)(2,1)S(1)} fusion(bf16[64,128,576]{1,2,0:T(8,128)(2,1)S(1)} %slice_dynamic-update-slice_fusion, bf16[72,136,64]{1,2,0:T(8,128)(2,1)S(1)} %get-tuple-element.5, s32[]{:T(128)S(6)} %select_n.130), kind=kLoop, calls=%fused_computation.21 | loop fusion | bytes 2097156
  38.5 0.8 %dynamic-slice_dynamic-update-slice_fusion.2 = bf16[64,128,576]{1,2,0:T(8,128)(2,1)S(1)} fusion(bf16[64,128,576]{1,2,0:T(8,128)(2,1)S(1)} %dynamic-slice_dynamic-update-slice_fusion.3, bf16[72,136,64]{1,2,0:T(8,128)(2,1)S(1)} %get-tuple-element.5, s32[]{:T(128)S(6)} %select_n.131, s32[]{:T(128)S(6)} %select_n.129), kind=kLoop, calls=%fused_computation.20 | loop fusion | bytes 2097160
  39.3 0.7 %dynamic-slice_dynamic-update-slice_fusion.1 = bf16[64,128,576]{1,2,0:T(8,128)(2,1)S(1)} fusion(bf16[64,128,576]{1,2,0:T(8,128)(2,1)S(1)} %dynamic-slice_dynamic-update-slice_fusion.2, bf16[72,136,64]{1,2,0:T(8,128)(2,1)S(1)} %get-tuple-element.5, s32[]{:T(128)S(6)} %select_n.131), kind=kLoop, calls=%fused_computation.19 | loop fusion | bytes 2097156
  40.0 0.8 %dynamic-slice_dynamic-update-slice_fusion = bf16[64,128,576]{1,2,0:T(8,128)(2,1)S(1)} fusion(bf16[64,128,576]{1,2,0:T(8,128)(2,1)S(1)} %dynamic-slice_dynamic-update-slice_fusion.1, bf16[72,136,64]{1,2,0:T(8,128)(2,1)S(1)} %get-tuple-element.5, s32[]{:T(128)S(6)} %select_n.131, s32[]{:T(128)S(6)} %select_n.130), kind=kLoop, calls=%fused_computation.18 | loop fusion | bytes 2097160 | tf_op jit(solution)/shard_map/concatenate | solution.py:36
  40.8 1.9 %fusion.74 = f32[64,128,128]{1,2,0:T(8,128)S(1)} fusion(bf16[64,128,576]{1,2,0:T(8,128)(2,1)S(1)} %dynamic-slice_dynamic-update-slice_fusion, bf16[576,128,1]{1,0,2:T(8,128)(2,1)S(1)} %bitcast.118), kind=kOutput, calls=%fused_computation.129 | convolution fusion | flops 1207959552 | bytes 13778944 | tf_op jit(solution)/shard_map/dot_general | solution.py:38
  42.7 0.7 %fusion.3 = bf16[64,64,128]{2,0,1:T(8,128)(2,1)S(1)} fusion(f32[64,128,128]{1,2,0:T(8,128)S(1)} %fusion.74, bf16[72,136,64]{1,2,0:T(8,128)(2,1)S(1)} %get-tuple-element.6, f32[64]{0:T(128)S(1)} %get-tuple-element.54), kind=kLoop, calls=%fused_computation.16 | loop fusion | flops 5767168 | bytes 6291712 | tf_op jit(solution)/shard_map/transpose | solution.py:149
  43.4 1.6 %copy.28 = bf16[64,64,128]{2,1,0:T(8,128)(2,1)} copy(bf16[64,64,128]{2,0,1:T(8,128)(2,1)S(1)} %fusion.3) | data formatting | bytes 2097152 | tf_op jit(solution)/shard_map/transpose | solution.py:149
  (30 shorter events, 3.3 us)
Async XLA Ops:
  0.0 0.7 %copy-start = (bf16[8,128]{1,0:T(8,128)(2,1)S(1)}, bf16[8,128]{1,0:T(8,128)(2,1)}, u32[]{:S(2)}) copy-start(bf16[8,128]{1,0:T(8,128)(2,1)} %param.6) | copy-start | bytes 6148
  2.3 22.6 %all-to-all-start = ((bf16[128,2,256]{2,1,0:T(2,128)(2,1)}), bf16[128,2,256]{2,1,0:T(2,128)(2,1)S(1)}, u32[]{:S(2)}, u32[]{:S(2)}) async-start(bf16[128,2,256]{2,1,0:T(2,128)(2,1)} %broadcast_in_dim.174), calls=%async_computation | async-start | bytes 262144 | tf_op jit(solution)/shard_map/all_to_all | solution.py:15

commit v8 on v7

--- a/solution.py
+++ b/solution.py
@@ -1,6 +1,8 @@
 import jax
 import jax.numpy as jnp
 from jax import lax
+from jax.experimental import pallas as pl
+from jax.experimental.pallas import tpu as pltpu
 from jax.sharding import PartitionSpec as P
 
 MAXDIL = 4
@@ -19,24 +21,56 @@
     return ((places >= 0) & (places < bins_total)).astype(jnp.float32)
 
 
+CHUNK = 8
+
+
+def row_group_kernel(dilation_ref, shifted_ref, weight_ref, out_ref):
+    first = pl.program_id(0) * CHUNK + MAXDIL
+    dilation = dilation_ref[0]
+    cols, width = shifted_ref.shape[1], shifted_ref.shape[2]
+    summed = None
+    for outer in range(3):
+        cells = shifted_ref[pl.ds(first + (outer - 1) * dilation, CHUNK), :, :]
+        part = jnp.dot(
+            cells.reshape(CHUNK * cols, width), weight_ref[outer], preferred_element_type=jnp.float32
+        )
+        summed = part if summed is None else summed + part
+    out_ref[...] = summed.reshape(out_ref.shape)
+
+
 def tap_groups(padded, weights, dilation):
     out_channels = weights.shape[1]
     in_channels = weights.shape[2]
-    row_count = padded.shape[0] - 2 * MAXDIL
+    row_ext = padded.shape[0]
+    row_count = row_ext - 2 * MAXDIL
     col_count = padded.shape[1] - 2 * MAXDIL
     zero_index = jnp.zeros((), jnp.int32)
-    pieces = []
-    for tap in range(9):
-        row_index = MAXDIL + (tap // 3 - 1) * dilation
-        col_index = MAXDIL + (tap % 3 - 1) * dilation
-        piece = lax.dynamic_slice(
-            padded, (row_index, col_index, zero_index), (row_count, col_count, in_channels)
-        )
-        pieces.append(piece.reshape(row_count * col_count, in_channels))
-    stacked = jnp.concatenate(pieces, axis=1)
-    flat_weight = jnp.transpose(weights, (0, 2, 1)).reshape(9 * in_channels, out_channels)
-    summed = jnp.dot(stacked, flat_weight, preferred_element_type=jnp.float32)
-    return summed.reshape(row_count, col_count, out_channels)
+    shifted = jnp.concatenate(
+        [
+            lax.dynamic_slice(
+                padded,
+                (zero_index, MAXDIL + (inner - 1) * dilation, zero_index),
+                (row_ext, col_count, in_channels),
+            )
+            for inner in range(3)
+        ],
+        axis=2,
+    )
+    group_weight = jnp.transpose(weights, (0, 2, 1)).reshape(3, 3 * in_channels, out_channels)
+    width = 3 * in_channels
+    return pl.pallas_call(
+        row_group_kernel,
+        out_shape=jax.ShapeDtypeStruct((row_count, col_count, out_channels), jnp.float32),
+        grid_spec=pltpu.PrefetchScalarGridSpec(
+            num_scalar_prefetch=1,
+            grid=(row_count // CHUNK,),
+            in_specs=[
+                pl.BlockSpec((row_ext, col_count, width), lambda g, d: (0, 0, 0)),
+                pl.BlockSpec((3, width, out_channels), lambda g, d: (0, 0, 0)),
+            ],
+            out_specs=pl.BlockSpec((CHUNK, col_count, out_channels), lambda g, d: (g, 0, 0)),
+        ),
+    )(jnp.reshape(dilation, (1,)).astype(jnp.int32), shifted, group_weight)
 
 
 def mirrored_taps(weights):

time: 45.4 us -> 63.5 us (1.40)
  other arithmetic: 9.31 us -> 19.9 us
  Pallas kernels: 0 us -> 9.15 us
  matrix products: 3.88 us -> 2.02 us
    pallas_call x0 -> x1, Pallas kernels: none -> 9.15 us  [tap_groups(): pl.pallas_call(row_group_kernel, out_shape=jax.ShapeDtypeStruct((row_coun...]
    transpose x1, other arithmetic: 0.7 us -> 6.55 us  [local(): return jnp.transpose(pair, (2, 0, 1))]
    unnamed x11 -> x3, local copies, waits for them, and re-layouts: 6.54 us -> 0.83 us
    dynamic_slice x0 -> x1, local copies, waits for them, and re-layouts: none -> 4.15 us  [tap_groups(): lax.dynamic_slice(padded, (zero_index, MAXDIL + (inner - 1) * dilation, z...]
    concatenate x0 -> x1, other arithmetic: none -> 3.61 us  [tap_groups(): jnp.concatenate([lax.dynamic_slice(padded, (zero_index, MAXDIL + (inner -...]
    dot_general x1 -> x0, matrix products: 1.85 us -> none  [tap_groups(): summed = jnp.dot(stacked, flat_weight, preferred_element_type=jnp.float32)]
    transpose x1, local copies, waits for them, and re-layouts: 1.65 us -> 3.41 us  [local(): return jnp.transpose(pair, (2, 0, 1))]
    mul x1, other arithmetic: 5.89 us -> 6.94 us  [local(): conv1 = tap_groups(jax.nn.relu(map1) * mask1, taps1, dilations[1])]
  transfers between devices with their start and end apart: 1 -> 1, of which waited for: 0 -> 0; matrix products, arithmetic and copies ran while one was open for 11% -> 9% of each run, Pallas kernels for 0% -> 0%
where the time goes in v8:
time: 63.5 us; the launch traced here: 63.1 us
  other arithmetic  19.9 us (31%)
  local copies, waits for them, and re-layouts  14.7 us (23%)
  starting transfers between devices  11.5 us (18%)
  Pallas kernels  9.15 us (14%)
  between operations  5.83 us (9%)
  matrix products  2.02 us (3%)
    all_to_all x1, starting transfers between devices, gather_projections(): lax.all_to_all(copies, axes, 0, 0, tiled=True).reshape(-1, proj.shape[1])  11.5 us
    pallas_call x1, Pallas kernels, tap_groups(): pl.pallas_call(row_group_kernel, out_shape=jax.ShapeDtypeStruct((row_coun...  9.15 us
    mul x1, other arithmetic, local(): conv1 = tap_groups(jax.nn.relu(map1) * mask1, taps1, dilations[1])  6.94 us
    transpose x1, other arithmetic, local(): return jnp.transpose(pair, (2, 0, 1))  6.55 us
    dynamic_slice x1, local copies, waits for them, and re-layouts, tap_groups(): lax.dynamic_slice(padded, (zero_index, MAXDIL + (inner - 1) * dilation, z...  4.15 us
    concatenate x1, other arithmetic, tap_groups(): jnp.concatenate([lax.dynamic_slice(padded, (zero_index, MAXDIL + (inner -...  3.61 us
    transpose x1, local copies, waits for them, and re-layouts, local(): return jnp.transpose(pair, (2, 0, 1))  3.41 us
    lt x2, other arithmetic, pick(): near_low = (places < dilation).reshape(shape)  1.39 us
  transfers between devices with their start and end apart: 1, of which 0 were waited for; matrix products, arithmetic and copies ran while one was open for 9% of the time, Pallas kernels for 0%

profile of v8, /device:TPU:1, one launch (start us, length us, event | category | flops | bytes accessed | tf_op | source)
XLA Modules:
  0.0 63.1 jit_solution(5885624713641498902)
XLA Ops:
  0.0 0.7 %copy-done = bf16[8,128]{1,0:T(8,128)(2,1)S(1)} copy-done((bf16[8,128]{1,0:T(8,128)(2,1)S(1)}, bf16[8,128]{1,0:T(8,128)(2,1)}, u32[]{:S(2)}) %copy-start) | copy-done | bytes 2072
  0.7 0.8 %fusion.3 = bf16[8,64]{1,0:T(8,128)(2,1)S(1)} fusion(bf16[8,128]{1,0:T(8,128)(2,1)S(1)} %copy-done, bf16[128,32]{0,1:T(8,128)(2,1)} %param.8, bf16[128,32]{0,1:T(8,128)(2,1)} %param.7), kind=kOutput, calls=%fused_computation.17 | convolution fusion | flops 164352 | bytes 19456 | tf_op jit(solution)/shard_map/dot_general | solution.py:153
  1.6 0.7 %broadcast_in_dim.174 = bf16[128,2,256]{2,1,0:T(2,128)(2,1)} broadcast(bf16[2,256]{1,0:T(2,128)(2,1)S(1)} %broadcast_in_dim.173), dimensions={1,2} | broadcast | bytes 132096 | tf_op jit(solution)/shard_map/broadcast_in_dim | solution.py:16
  2.3 11.5 %all-to-all-start = ((bf16[128,2,256]{2,1,0:T(2,128)(2,1)}), bf16[128,2,256]{2,1,0:T(2,128)(2,1)S(1)}, u32[]{:S(2)}, u32[]{:S(2)}) async-start(bf16[128,2,256]{2,1,0:T(2,128)(2,1)} %broadcast_in_dim.174), calls=%async_computation | async-start | bytes 262144 | tf_op jit(solution)/shard_map/all_to_all | solution.py:17
  13.9 0.8 %slice_bitcast_fusion = (f32[64]{0:T(128)S(1)}, f32[64]{0:T(128)S(1)}) fusion(f32[2,64]{1,0:T(2,128)} %param.10), kind=kLoop, calls=%fused_computation.103 | loop fusion | bytes 1024 | tf_op jit(solution)/shard_map/add | solution.py:177
  14.6 1.4 %fusion.74 = (s32[1]{0:T(128)}, s32[1]{0:T(128)}) fusion(s32[2]{0:T(128)} %param.11), kind=kLoop, calls=%fused_computation.123 | loop fusion | bytes 16 | tf_op jit(solution)/shard_map/slice | solution.py:164
  16.7 1.0 %slice_bitcast_fusion.2 = (bf16[9,64,64]{2,1,0:T(8,128)(2,1)S(1)}, bf16[1,9,64,64]{3,2,1,0:T(8,128)(2,1)S(1)}, bf16[1,9,64,64]{3,2,1,0:T(8,128)(2,1)S(1)}) fusion(bf16[2,9,64,64]{3,2,1,0:T(8,128)(2,1)} %param.9), kind=kLoop, calls=%fused_computation.114 | loop fusion | bytes 368640 | tf_op jit(solution)/shard_map/squeeze | solution.py:173
  18.0 0.7 %fusion.52 = pred[72]{0:T(512)(128)(4,1)S(1)} fusion(s32[]{:T(128)} %bitcast, s32[]{:T(128)S(6)} %sub.14), kind=kLoop, calls=%fused_computation.106 | loop fusion | flops 144 | bytes 80 | tf_op jit(solution)/shard_map/lt | solution.py:134
  23.5 0.8 %copy.39 = bf16[9,64,128]{2,1,0:T(8,128)(2,1)} copy(bf16[9,64,128]{1,2,0:T(8,128)(2,1)S(1)} %maximum_bitcast_fusion) | data formatting | bytes 294912 | tf_op jit(solution)/shard_map/transpose | solution.py:59
  24.5 0.7 %fusion.50 = pred[136]{0:T(512)(128)(4,1)S(1)} fusion(s32[]{:T(128)} %bitcast, s32[]{:T(128)S(6)} %sub.12), kind=kLoop, calls=%fused_computation.102 | loop fusion | flops 272 | bytes 144 | tf_op jit(solution)/shard_map/lt | solution.py:134
  25.2 0.2 reshape.163
  25.6 0.3 convolution_bitcast_fusion.3
  25.9 0.3 convolution_bitcast_fusion.2
  26.1 0.3 convolution_bitcast_fusion.1
  26.5 0.3 convolution_bitcast_fusion
  26.8 0.2 add_add_fusion.1
  27.9 0.3 fusion.4
  28.7 0.2 fusion.65
  29.3 6.9 %maximum_multiply_fusion = (bf16[72,136,64]{2,1,0:T(8,128)(2,1)S(1)}, bf16[72,136,64]{2,1,0:T(8,128)(2,1)S(1)}) fusion(bf16[72,136]{1,0:T(8,128)(2,1)S(1)} %multiply_convert_fusion.2, f32[72,64]{1,0:T(8,128)S(1)} %copy.37, f32[72,64]{1,0:T(8,128)S(1)} %copy.36, f32[72,64]{1,0:T(8,128)S(1)} %copy.35, f32[136,64]{1,0:T(8,128)S(1)} %copy.34, ...), kind=kLoop, calls=%fused_computation.10 | loop fusion | flops 11907072 | bytes 2846240 | tf_op jit(solution)/shard_map/mul | solution.py:174
  36.2 4.2 %constant_dynamic-slice_fusion.1 = (bf16[72,128,64]{2,1,0:T(8,128)(2,1)S(1)}, bf16[72,128,64]{2,1,0:T(8,128)(2,1)S(1)}, bf16[72,128,64]{2,1,0:T(8,128)(2,1)S(1)}) fusion(bf16[72,136,64]{2,1,0:T(8,128)(2,1)S(1)} %get-tuple-element.5, s32[]{:T(128)S(6)} %select_n.114, s32[]{:T(128)S(6)} %select_n.115), kind=kLoop, calls=%fused_computation.96 | loop fusion | bytes 7077896 | tf_op jit(solution)/shard_map/dynamic_slice | solution.py:50
  40.4 3.6 %pad_maximum_fusion.shifted_ref = bf16[72,128,192]{2,1,0:T(8,128)(2,1)} fusion(bf16[72,128,64]{2,1,0:T(8,128)(2,1)S(1)} %get-tuple-element.24, bf16[72,128,64]{2,1,0:T(8,128)(2,1)S(1)} %get-tuple-element.25, bf16[72,128,64]{2,1,0:T(8,128)(2,1)S(1)} %get-tuple-element.23), kind=kLoop, calls=%fused_computation.3 | loop fusion | flops 10616832 | bytes 7077888 | tf_op jit(solution)/shard_map/concatenate | solution.py:48
  44.0 9.2 %shard_map.64 = f32[64,128,128]{2,1,0:T(8,128)} custom-call(s32[1]{0:T(128)} %get-tuple-element.60.dilation_ref, bf16[72,128,192]{2,1,0:T(8,128)(2,1)} %pad_maximum_fusion.shifted_ref, bf16[3,192,128]{2,1,0:T(8,128)(2,1)} %bitcast.114), custom_call_target="tpu_custom_call" | custom-call | tf_op jit(solution)/shard_map/pallas_call | solution.py:61
  53.2 6.5 %fusion.2 = bf16[64,64,128]{0,2,1:T(8,128)(2,1)} fusion(f32[64,128,128]{2,1,0:T(8,128)} %shard_map.64, bf16[72,136,64]{2,1,0:T(8,128)(2,1)S(1)} %get-tuple-element.6, f32[64]{0:T(128)S(1)} %get-tuple-element.57), kind=kLoop, calls=%fused_computation.11 | loop fusion | flops 5767168 | bytes 6291712 | tf_op jit(solution)/shard_map/transpose | solution.py:183
  59.7 3.4 %copy.40 = bf16[64,64,128]{2,1,0:T(8,128)(2,1)} copy(bf16[64,64,128]{0,2,1:T(8,128)(2,1)} %fusion.2) | data formatting | bytes 2097152 | tf_op jit(solution)/shard_map/transpose | solution.py:183
  (29 shorter events, 2.2 us)
Async XLA Ops:
  0.0 0.7 %copy-start = (bf16[8,128]{1,0:T(8,128)(2,1)S(1)}, bf16[8,128]{1,0:T(8,128)(2,1)}, u32[]{:S(2)}) copy-start(bf16[8,128]{1,0:T(8,128)(2,1)} %param.6) | copy-start | bytes 6148
  2.3 22.9 %all-to-all-start = ((bf16[128,2,256]{2,1,0:T(2,128)(2,1)}), bf16[128,2,256]{2,1,0:T(2,128)(2,1)S(1)}, u32[]{:S(2)}, u32[]{:S(2)}) async-start(bf16[128,2,256]{2,1,0:T(2,128)(2,1)} %broadcast_in_dim.174), calls=%async_computation | async-start | bytes 262144 | tf_op jit(solution)/shard_map/all_to_all | solution.py:17

commit v9 on v7

--- a/solution.py
+++ b/solution.py
@@ -146,7 +146,11 @@
     pair = (0.5 * (mixed1.astype(jnp.float32) + mixed1_mirror.astype(jnp.float32))).astype(
         jnp.bfloat16
     )
-    return jnp.transpose(pair, (2, 0, 1))
+    flat = pair.reshape(row_size * col_size, channels)
+    turned = jnp.einsum(
+        "ck,nk->cn", jnp.eye(channels, dtype=pair.dtype), flat, preferred_element_type=jnp.float32
+    )
+    return turned.astype(jnp.bfloat16).reshape(channels, row_size, col_size)
 
 
 def solution(mesh):

time: 45.4 us -> 45 us (level)
  other arithmetic: 9.31 us -> 8.42 us
  matrix products: 3.88 us -> 4.77 us
    transpose x1 -> x0, local copies, waits for them, and re-layouts: 1.65 us -> none  [local(): return jnp.transpose(pair, (2, 0, 1))]
    unnamed x11 -> x12, local copies, waits for them, and re-layouts: 6.54 us -> 7.8 us
    dot_general x0 -> x1, matrix products: none -> 0.89 us  [local(): jnp.einsum('ck,nk->cn', jnp.eye(channels, dtype=pair.dtype), flat, prefer...]
    transpose x1 -> x0, other arithmetic: 0.7 us -> none  [local(): return jnp.transpose(pair, (2, 0, 1))]
where the time goes in v9:
time: 45 us; the launch traced here: 44.6 us
  local copies, waits for them, and re-layouts  13.7 us (30%)
  starting transfers between devices  11.5 us (26%)
  other arithmetic  8.42 us (19%)
  between operations  6.28 us (14%)
  matrix products  4.77 us (11%)
    all_to_all x1, starting transfers between devices, gather_projections(): lax.all_to_all(copies, axes, 0, 0, tiled=True).reshape(-1, proj.shape[1])  11.5 us
    unnamed x12, local copies, waits for them, and re-layouts  7.8 us
    mul x1, other arithmetic, local(): conv1 = tap_groups(jax.nn.relu(map1) * mask1, taps1, dilations[1])  5.71 us
    dot_general x1, matrix products, tap_groups(): summed = jnp.dot(stacked, flat_weight, preferred_element_type=jnp.float32)  1.85 us
    slice x1, local copies, waits for them, and re-layouts, local(): conv1 = tap_groups(jax.nn.relu(map1) * mask1, taps1, dilations[1])  1.39 us
    lt x2, other arithmetic, pick(): near_low = (places < dilation).reshape(shape)  1.29 us
    squeeze x1, local copies, waits for them, and re-layouts, local(): conv_weight[1]  1.06 us
  transfers between devices with their start and end apart: 1, of which 0 were waited for; matrix products, arithmetic and copies ran while one was open for 11% of the time, Pallas kernels for 0%

profile of v9, /device:TPU:1, one launch (start us, length us, event | category | flops | bytes accessed | tf_op | source)
XLA Modules:
  0.0 44.6 jit_solution(14940277043563486855)
XLA Ops:
  0.0 0.7 %copy-done = bf16[8,128]{1,0:T(8,128)(2,1)S(1)} copy-done((bf16[8,128]{1,0:T(8,128)(2,1)S(1)}, bf16[8,128]{1,0:T(8,128)(2,1)}, u32[]{:S(2)}) %copy-start) | copy-done | bytes 2072
  0.7 0.8 %fusion.3 = bf16[8,64]{1,0:T(8,128)(2,1)S(1)} fusion(bf16[8,128]{1,0:T(8,128)(2,1)S(1)} %copy-done, bf16[128,32]{0,1:T(8,128)(2,1)} %param.8, bf16[128,32]{0,1:T(8,128)(2,1)} %param.7), kind=kOutput, calls=%fused_computation.17 | convolution fusion | flops 164352 | bytes 19456 | tf_op jit(solution)/shard_map/dot_general | solution.py:119
  1.6 0.7 %broadcast_in_dim.174 = bf16[128,2,256]{2,1,0:T(2,128)(2,1)} broadcast(bf16[2,256]{1,0:T(2,128)(2,1)S(1)} %broadcast_in_dim.173), dimensions={1,2} | broadcast | bytes 132096 | tf_op jit(solution)/shard_map/broadcast_in_dim | solution.py:14
  2.3 11.5 %all-to-all-start = ((bf16[128,2,256]{2,1,0:T(2,128)(2,1)}), bf16[128,2,256]{2,1,0:T(2,128)(2,1)S(1)}, u32[]{:S(2)}, u32[]{:S(2)}) async-start(bf16[128,2,256]{2,1,0:T(2,128)(2,1)} %broadcast_in_dim.174), calls=%async_computation | async-start | bytes 262144 | tf_op jit(solution)/shard_map/all_to_all | solution.py:15
  13.9 0.8 %slice_bitcast_fusion = (f32[64]{0:T(128)S(1)}, f32[64]{0:T(128)S(1)}) fusion(f32[2,64]{1,0:T(2,128)} %param.10), kind=kLoop, calls=%fused_computation.113 | loop fusion | bytes 1024 | tf_op jit(solution)/shard_map/add | solution.py:143
  14.6 1.4 %fusion.76 = (s32[1]{0:T(128)}, s32[1]{0:T(128)}) fusion(s32[2]{0:T(128)} %param.11), kind=kLoop, calls=%fused_computation.133 | loop fusion | bytes 16 | tf_op jit(solution)/shard_map/slice | solution.py:140
  16.7 1.1 %slice_bitcast_fusion.2 = (bf16[9,64,64]{2,1,0:T(8,128)(2,1)S(1)}, bf16[1,9,64,64]{3,2,1,0:T(8,128)(2,1)S(1)}, bf16[1,9,64,64]{3,2,1,0:T(8,128)(2,1)S(1)}) fusion(bf16[2,9,64,64]{3,2,1,0:T(8,128)(2,1)} %param.9), kind=kLoop, calls=%fused_computation.124 | loop fusion | bytes 368640 | tf_op jit(solution)/shard_map/squeeze | solution.py:139
  17.9 0.6 %fusion.54 = pred[72]{0:T(512)(128)(4,1)S(1)} fusion(s32[]{:T(128)} %bitcast, s32[]{:T(128)S(6)} %sub.14), kind=kLoop, calls=%fused_computation.116 | loop fusion | flops 144 | bytes 80 | tf_op jit(solution)/shard_map/lt | solution.py:100
  24.2 0.7 %fusion.52 = pred[136]{0:T(512)(128)(4,1)S(1)} fusion(s32[]{:T(128)} %bitcast, s32[]{:T(128)S(6)} %sub.12), kind=kLoop, calls=%fused_computation.112 | loop fusion | flops 272 | bytes 144 | tf_op jit(solution)/shard_map/lt | solution.py:100
  25.8 0.3 convolution_bitcast_fusion.1
  26.2 0.3 convolution_bitcast_fusion
  28.4 5.7 %maximum_multiply_fusion = (bf16[72,136,64]{1,2,0:T(8,128)(2,1)S(1)}, bf16[72,136,64]{1,2,0:T(8,128)(2,1)S(1)}) fusion(bf16[72,136]{1,0:T(8,128)(2,1)S(1)} %multiply_convert_fusion.2, f32[72,64]{1,0:T(8,128)S(1)} %copy.24, f32[72,64]{1,0:T(8,128)S(1)} %copy.23, f32[72,64]{1,0:T(8,128)S(1)} %copy.22, f32[136,64]{0,1:T(8,128)S(1)} %get-tuple-element.17, ...), kind=kLoop, calls=%fused_computation.4 | loop fusion | flops 11907072 | bytes 2846240 | tf_op jit(solution)/shard_map/mul | solution.py:140
  34.1 0.5 %dynamic-slice_dynamic-update-slice_fusion.7 = bf16[64,128,576]{1,2,0:T(8,128)(2,1)S(1)} fusion(bf16[72,136,64]{1,2,0:T(8,128)(2,1)S(1)} %get-tuple-element.5, s32[]{:T(128)S(6)} %select_n.128, s32[]{:T(128)S(6)} %select_n.129), kind=kLoop, calls=%fused_computation.29 | loop fusion | bytes 2097160
  34.6 0.7 %dynamic-slice_dynamic-update-slice_fusion.6 = bf16[64,128,576]{1,2,0:T(8,128)(2,1)S(1)} fusion(bf16[64,128,576]{1,2,0:T(8,128)(2,1)S(1)} %dynamic-slice_dynamic-update-slice_fusion.7, bf16[72,136,64]{1,2,0:T(8,128)(2,1)S(1)} %get-tuple-element.5, s32[]{:T(128)S(6)} %select_n.128), kind=kLoop, calls=%fused_computation.28 | loop fusion | bytes 2097156
  35.3 0.8 %dynamic-slice_dynamic-update-slice_fusion.5 = bf16[64,128,576]{1,2,0:T(8,128)(2,1)S(1)} fusion(bf16[64,128,576]{1,2,0:T(8,128)(2,1)S(1)} %dynamic-slice_dynamic-update-slice_fusion.6, bf16[72,136,64]{1,2,0:T(8,128)(2,1)S(1)} %get-tuple-element.5, s32[]{:T(128)S(6)} %select_n.128, s32[]{:T(128)S(6)} %select_n.130), kind=kLoop, calls=%fused_computation.27 | loop fusion | bytes 2097160
  36.1 0.8 %dynamic-slice_dynamic-update-slice_fusion.4 = bf16[64,128,576]{1,2,0:T(8,128)(2,1)S(1)} fusion(bf16[64,128,576]{1,2,0:T(8,128)(2,1)S(1)} %dynamic-slice_dynamic-update-slice_fusion.5, bf16[72,136,64]{1,2,0:T(8,128)(2,1)S(1)} %get-tuple-element.5, s32[]{:T(128)S(6)} %select_n.129), kind=kLoop, calls=%fused_computation.26 | loop fusion | bytes 2097156
  36.9 0.7 %slice_dynamic-update-slice_fusion = bf16[64,128,576]{1,2,0:T(8,128)(2,1)S(1)} fusion(bf16[64,128,576]{1,2,0:T(8,128)(2,1)S(1)} %dynamic-slice_dynamic-update-slice_fusion.4, bf16[72,136,64]{1,2,0:T(8,128)(2,1)S(1)} %get-tuple-element.5), kind=kLoop, calls=%fused_computation.21 | loop fusion | bytes 2097152
  37.6 0.8 %dynamic-slice_dynamic-update-slice_fusion.3 = bf16[64,128,576]{1,2,0:T(8,128)(2,1)S(1)} fusion(bf16[64,128,576]{1,2,0:T(8,128)(2,1)S(1)} %slice_dynamic-update-slice_fusion, bf16[72,136,64]{1,2,0:T(8,128)(2,1)S(1)} %get-tuple-element.5, s32[]{:T(128)S(6)} %select_n.130), kind=kLoop, calls=%fused_computation.25 | loop fusion | bytes 2097156
  38.4 0.8 %dynamic-slice_dynamic-update-slice_fusion.2 = bf16[64,128,576]{1,2,0:T(8,128)(2,1)S(1)} fusion(bf16[64,128,576]{1,2,0:T(8,128)(2,1)S(1)} %dynamic-slice_dynamic-update-slice_fusion.3, bf16[72,136,64]{1,2,0:T(8,128)(2,1)S(1)} %get-tuple-element.5, s32[]{:T(128)S(6)} %select_n.131, s32[]{:T(128)S(6)} %select_n.129), kind=kLoop, calls=%fused_computation.24 | loop fusion | bytes 2097160
  39.1 0.7 %dynamic-slice_dynamic-update-slice_fusion.1 = bf16[64,128,576]{1,2,0:T(8,128)(2,1)S(1)} fusion(bf16[64,128,576]{1,2,0:T(8,128)(2,1)S(1)} %dynamic-slice_dynamic-update-slice_fusion.2, bf16[72,136,64]{1,2,0:T(8,128)(2,1)S(1)} %get-tuple-element.5, s32[]{:T(128)S(6)} %select_n.131), kind=kLoop, calls=%fused_computation.23 | loop fusion | bytes 2097156
  39.9 0.8 %dynamic-slice_dynamic-update-slice_fusion = bf16[64,128,576]{1,2,0:T(8,128)(2,1)S(1)} fusion(bf16[64,128,576]{1,2,0:T(8,128)(2,1)S(1)} %dynamic-slice_dynamic-update-slice_fusion.1, bf16[72,136,64]{1,2,0:T(8,128)(2,1)S(1)} %get-tuple-element.5, s32[]{:T(128)S(6)} %select_n.131, s32[]{:T(128)S(6)} %select_n.130), kind=kLoop, calls=%fused_computation.22 | loop fusion | bytes 2097160 | tf_op jit(solution)/shard_map/concatenate | solution.py:36
  40.6 1.9 %fusion.77 = f32[64,128,128]{1,2,0:T(8,128)S(1)} fusion(bf16[64,128,576]{1,2,0:T(8,128)(2,1)S(1)} %dynamic-slice_dynamic-update-slice_fusion, bf16[576,128,1]{1,0,2:T(8,128)(2,1)S(1)} %bitcast.126), kind=kOutput, calls=%fused_computation.134 | convolution fusion | flops 1207959552 | bytes 13778944 | tf_op jit(solution)/shard_map/dot_general | solution.py:38
  42.5 0.9 %fusion.2 = bf16[8,8,64,128]{3,1,2,0:T(8,128)(2,1)S(1)} fusion(f32[64,128,128]{1,2,0:T(8,128)S(1)} %fusion.77, bf16[72,136,64]{1,2,0:T(8,128)(2,1)S(1)} %get-tuple-element.6, f32[64]{0:T(128)S(1)} %get-tuple-element.54), kind=kOutput, calls=%fused_computation.11 | convolution fusion | flops 73404416 | bytes 6291968 | tf_op jit(solution)/shard_map/ck,nk->cn/dot_general | solution.py:150
  43.4 1.3 %copy.30 = bf16[8,8,64,128]{3,2,1,0:T(8,128)(2,1)} copy(bf16[8,8,64,128]{3,1,2,0:T(8,128)(2,1)S(1)} %fusion.2) | data formatting | bytes 2097152
  (30 shorter events, 3.3 us)
Async XLA Ops:
  0.0 0.7 %copy-start = (bf16[8,128]{1,0:T(8,128)(2,1)S(1)}, bf16[8,128]{1,0:T(8,128)(2,1)}, u32[]{:S(2)}) copy-start(bf16[8,128]{1,0:T(8,128)(2,1)} %param.6) | copy-start | bytes 6148
  2.3 22.6 %all-to-all-start = ((bf16[128,2,256]{2,1,0:T(2,128)(2,1)}), bf16[128,2,256]{2,1,0:T(2,128)(2,1)S(1)}, u32[]{:S(2)}, u32[]{:S(2)}) async-start(bf16[128,2,256]{2,1,0:T(2,128)(2,1)} %broadcast_in_dim.174), calls=%async_computation | async-start | bytes 262144 | tf_op jit(solution)/shard_map/all_to_all | solution.py:15

commit v10 on v9

--- a/solution.py
+++ b/solution.py
@@ -30,7 +30,9 @@
         row_index = MAXDIL + (tap // 3 - 1) * dilation
         col_index = MAXDIL + (tap % 3 - 1) * dilation
         piece = lax.dynamic_slice(
-            padded, (row_index, col_index, zero_index), (row_count, col_count, in_channels)
+            padded,
+            (row_index, col_index, zero_index + (tap % 2) * in_channels),
+            (row_count, col_count, in_channels),
         )
         pieces.append(piece.reshape(row_count * col_count, in_channels))
     stacked = jnp.concatenate(pieces, axis=1)
@@ -45,8 +47,11 @@
 
 def first_layer(every, taps, shift_bias, dilation, row_start, rows, col_start, cols):
     bins_total = every.shape[0]
-    half = every.shape[1] // 2
-    lower = jnp.arange(every.shape[1]) < half
+    channels = every.shape[1]
+    half = channels // 2
+    lower = (jnp.arange(2 * channels) % channels) < half
+    taps = jnp.concatenate([taps, taps], axis=1)
+    shift_bias = jnp.concatenate([shift_bias, shift_bias])
     active = jnp.pad(jax.nn.relu(every), ((REACH, REACH), (0, 0)))
     padded = jnp.pad(every, ((MAXDIL, MAXDIL), (0, 0)))
 
@@ -74,6 +79,7 @@
             by_col.append(along_rows)
             by_row.append(along_cols)
         own = lax.dynamic_slice_in_dim(padded, start, count, 0)
+        own = jnp.concatenate([own, own], axis=1)
         own_row = jnp.where(lower, own, 0.0) + shift_bias[None, :]
         own_col = jnp.where(lower, 0.0, own)
         row_tables = [
@@ -140,7 +146,7 @@
     conv1 = tap_groups(jax.nn.relu(map1) * mask1, taps1, dilations[1])
     channels = conv_weight.shape[2]
     core = (slice(MAXDIL, MAXDIL + row_size), slice(MAXDIL, MAXDIL + col_size), slice(None))
-    base1 = map1[core].astype(jnp.float32) + conv_bias[1][None, None, :]
+    base1 = map1[core][:, :, :channels].astype(jnp.float32) + conv_bias[1][None, None, :]
     mixed1 = (base1 + conv1[:, :, :channels]).astype(jnp.bfloat16)
     mixed1_mirror = (base1 + conv1[:, :, channels:]).astype(jnp.bfloat16)
     pair = (0.5 * (mixed1.astype(jnp.float32) + mixed1_mirror.astype(jnp.float32))).astype(

time: 45 us -> 52 us (1.16)
  other arithmetic: 8.42 us -> 15.5 us
  between operations: 6.28 us -> 5.7 us
    mul x1, other arithmetic: 5.71 us -> 13.4 us  [local(): conv1 = tap_groups(jax.nn.relu(map1) * mask1, taps1, dilations[1])]
    broadcast_in_dim x0 -> x6, local copies, waits for them, and re-layouts: none -> 0.57 us  [pick(): return jnp.where(near_low, low, jnp.where(near_high, high, mid))]
    add x7 -> x1, local copies, waits for them, and re-layouts: 1.23 us -> 0.76 us  [local(): map1[core][:, :, :channels].astype(jnp.float32)]
  transfers between devices with their start and end apart: 1 -> 1, of which waited for: 0 -> 0; matrix products, arithmetic and copies ran while one was open for 11% -> 9% of each run, Pallas kernels for 0% -> 0%
where the time goes in v10:
time: 52 us; the launch traced here: 51.6 us
  other arithmetic  15.5 us (30%)
  local copies, waits for them, and re-layouts  13.9 us (27%)
  starting transfers between devices  11.5 us (22%)
  between operations  5.7 us (11%)
  matrix products  5.03 us (10%)
    mul x1, other arithmetic, local(): conv1 = tap_groups(jax.nn.relu(map1) * mask1, taps1, dilations[1])  13.4 us
    all_to_all x1, starting transfers between devices, gather_projections(): lax.all_to_all(copies, axes, 0, 0, tiled=True).reshape(-1, proj.shape[1])  11.5 us
    unnamed x12, local copies, waits for them, and re-layouts  7.68 us
    dot_general x1, matrix products, tap_groups(): summed = jnp.dot(stacked, flat_weight, preferred_element_type=jnp.float32)  1.85 us
    slice x1, local copies, waits for them, and re-layouts, local(): conv1 = tap_groups(jax.nn.relu(map1) * mask1, taps1, dilations[1])  1.35 us
    lt x2, other arithmetic, pick(): near_low = (places < dilation).reshape(shape)  1.13 us
    squeeze x1, local copies, waits for them, and re-layouts, local(): conv_weight[1]  1.06 us
  transfers between devices with their start and end apart: 1, of which 0 were waited for; matrix products, arithmetic and copies ran while one was open for 9% of the time, Pallas kernels for 0%

profile of v10, /device:TPU:1, one launch (start us, length us, event | category | flops | bytes accessed | tf_op | source)
XLA Modules:
  0.0 51.6 jit_solution(15057301666340458253)
XLA Ops:
  0.0 0.7 %copy-done = bf16[8,128]{1,0:T(8,128)(2,1)S(1)} copy-done((bf16[8,128]{1,0:T(8,128)(2,1)S(1)}, bf16[8,128]{1,0:T(8,128)(2,1)}, u32[]{:S(2)}) %copy-start) | copy-done | bytes 2072
  0.7 0.8 %fusion.3 = bf16[8,64]{1,0:T(8,128)(2,1)S(1)} fusion(bf16[8,128]{1,0:T(8,128)(2,1)S(1)} %copy-done, bf16[128,32]{0,1:T(8,128)(2,1)} %param.8, bf16[128,32]{0,1:T(8,128)(2,1)} %param.7), kind=kOutput, calls=%fused_computation.17 | convolution fusion | flops 164352 | bytes 19456 | tf_op jit(solution)/shard_map/dot_general | solution.py:125
  1.6 0.7 %broadcast_in_dim.188 = bf16[128,2,256]{2,1,0:T(2,128)(2,1)} broadcast(bf16[2,256]{1,0:T(2,128)(2,1)S(1)} %broadcast_in_dim.187), dimensions={1,2} | broadcast | bytes 132096 | tf_op jit(solution)/shard_map/broadcast_in_dim | solution.py:14
  2.3 11.5 %all-to-all-start = ((bf16[128,2,256]{2,1,0:T(2,128)(2,1)}), bf16[128,2,256]{2,1,0:T(2,128)(2,1)S(1)}, u32[]{:S(2)}, u32[]{:S(2)}) async-start(bf16[128,2,256]{2,1,0:T(2,128)(2,1)} %broadcast_in_dim.188), calls=%async_computation | async-start | bytes 262144 | tf_op jit(solution)/shard_map/all_to_all | solution.py:15
  13.9 0.8 %slice_bitcast_fusion = (f32[64]{0:T(128)S(1)}, f32[64]{0:T(128)S(1)}) fusion(f32[2,64]{1,0:T(2,128)} %param.10), kind=kLoop, calls=%fused_computation.115 | loop fusion | bytes 1024 | tf_op jit(solution)/shard_map/add | solution.py:149
  14.6 1.3 %fusion.71 = (s32[1]{0:T(128)}, s32[1]{0:T(128)}) fusion(s32[2]{0:T(128)} %param.11), kind=kLoop, calls=%fused_computation.134 | loop fusion | bytes 16 | tf_op jit(solution)/shard_map/slice | solution.py:146
  16.5 0.6 %fusion.47 = pred[72]{0:T(512)(128)(4,1)S(1)} fusion(s32[]{:T(128)} %bitcast, s32[]{:T(128)S(6)} %sub.14), kind=kLoop, calls=%fused_computation.118 | loop fusion | flops 144 | bytes 80 | tf_op jit(solution)/shard_map/lt | solution.py:106
  17.1 1.1 %slice_bitcast_fusion.2 = (bf16[9,64,64]{2,1,0:T(8,128)(2,1)S(1)}, bf16[1,9,64,64]{3,2,1,0:T(8,128)(2,1)S(1)}, bf16[1,9,64,64]{3,2,1,0:T(8,128)(2,1)S(1)}) fusion(bf16[2,9,64,64]{3,2,1,0:T(8,128)(2,1)} %param.9), kind=kLoop, calls=%fused_computation.127 | loop fusion | bytes 368640 | tf_op jit(solution)/shard_map/squeeze | solution.py:145
  18.4 0.6 %fusion.44 = pred[136]{0:T(512)(128)(4,1)S(1)} fusion(s32[]{:T(128)} %bitcast, s32[]{:T(128)S(6)} %sub.12), kind=kLoop, calls=%fused_computation.112 | loop fusion | flops 272 | bytes 144 | tf_op jit(solution)/shard_map/lt | solution.py:106
  25.2 0.4 convolution_bitcast_fusion.1
  25.6 0.4 convolution_bitcast_fusion
  27.8 13.4 %maximum_multiply_fusion = (bf16[72,136,128]{1,2,0:T(8,128)(2,1)S(1)}, bf16[72,136,128]{1,2,0:T(8,128)(2,1)S(1)}) fusion(bf16[72,136]{1,0:T(8,128)(2,1)S(1)} %multiply_convert_fusion.2, f32[72,128]{1,0:T(8,128)S(1)} %get-tuple-element.21, f32[72,128]{1,0:T(8,128)S(1)} %get-tuple-element.22, f32[72,128]{1,0:T(8,128)S(1)} %get-tuple-element.19, ...), kind=kLoop, calls=%fused_computation.4 | loop fusion | flops 23814144 | bytes 5672480 | tf_op jit(solution)/shard_map/mul | solution.py:146
  41.2 0.5 dynamic-slice_dynamic-update-slice_fusion.7
  41.7 0.7 %dynamic-slice_dynamic-update-slice_fusion.6 = bf16[64,128,576]{1,2,0:T(8,128)(2,1)S(1)} fusion(bf16[64,128,576]{1,2,0:T(8,128)(2,1)S(1)} %dynamic-slice_dynamic-update-slice_fusion.7, bf16[72,136,128]{1,2,0:T(8,128)(2,1)S(1)} %get-tuple-element.5, s32[]{:T(128)S(6)} %select_n.180), kind=kLoop, calls=%fused_computation.28 | loop fusion | bytes 2097156
  42.4 0.7 %dynamic-slice_dynamic-update-slice_fusion.5 = bf16[64,128,576]{1,2,0:T(8,128)(2,1)S(1)} fusion(bf16[64,128,576]{1,2,0:T(8,128)(2,1)S(1)} %dynamic-slice_dynamic-update-slice_fusion.6, bf16[72,136,128]{1,2,0:T(8,128)(2,1)S(1)} %get-tuple-element.5, s32[]{:T(128)S(6)} %select_n.180, s32[]{:T(128)S(6)} %select_n.182), kind=kLoop, calls=%fused_computation.27 | loop fusion | bytes 2097160
  43.1 0.8 %dynamic-slice_dynamic-update-slice_fusion.4 = bf16[64,128,576]{1,2,0:T(8,128)(2,1)S(1)} fusion(bf16[64,128,576]{1,2,0:T(8,128)(2,1)S(1)} %dynamic-slice_dynamic-update-slice_fusion.5, bf16[72,136,128]{1,2,0:T(8,128)(2,1)S(1)} %get-tuple-element.5, s32[]{:T(128)S(6)} %select_n.181), kind=kLoop, calls=%fused_computation.26 | loop fusion | bytes 2097156
  43.9 0.7 %slice_dynamic-update-slice_fusion = bf16[64,128,576]{1,2,0:T(8,128)(2,1)S(1)} fusion(bf16[64,128,576]{1,2,0:T(8,128)(2,1)S(1)} %dynamic-slice_dynamic-update-slice_fusion.4, bf16[72,136,128]{1,2,0:T(8,128)(2,1)S(1)} %get-tuple-element.5), kind=kLoop, calls=%fused_computation.21 | loop fusion | bytes 2097152
  44.6 0.8 %dynamic-slice_dynamic-update-slice_fusion.3 = bf16[64,128,576]{1,2,0:T(8,128)(2,1)S(1)} fusion(bf16[64,128,576]{1,2,0:T(8,128)(2,1)S(1)} %slice_dynamic-update-slice_fusion, bf16[72,136,128]{1,2,0:T(8,128)(2,1)S(1)} %get-tuple-element.5, s32[]{:T(128)S(6)} %select_n.182), kind=kLoop, calls=%fused_computation.25 | loop fusion | bytes 2097156
  45.4 0.7 %dynamic-slice_dynamic-update-slice_fusion.2 = bf16[64,128,576]{1,2,0:T(8,128)(2,1)S(1)} fusion(bf16[64,128,576]{1,2,0:T(8,128)(2,1)S(1)} %dynamic-slice_dynamic-update-slice_fusion.3, bf16[72,136,128]{1,2,0:T(8,128)(2,1)S(1)} %get-tuple-element.5, s32[]{:T(128)S(6)} %select_n.183, s32[]{:T(128)S(6)} %select_n.181), kind=kLoop, calls=%fused_computation.24 | loop fusion | bytes 2097160
  46.1 0.7 %dynamic-slice_dynamic-update-slice_fusion.1 = bf16[64,128,576]{1,2,0:T(8,128)(2,1)S(1)} fusion(bf16[64,128,576]{1,2,0:T(8,128)(2,1)S(1)} %dynamic-slice_dynamic-update-slice_fusion.2, bf16[72,136,128]{1,2,0:T(8,128)(2,1)S(1)} %get-tuple-element.5, s32[]{:T(128)S(6)} %select_n.183), kind=kLoop, calls=%fused_computation.23 | loop fusion | bytes 2097156
  46.8 0.7 %dynamic-slice_dynamic-update-slice_fusion = bf16[64,128,576]{1,2,0:T(8,128)(2,1)S(1)} fusion(bf16[64,128,576]{1,2,0:T(8,128)(2,1)S(1)} %dynamic-slice_dynamic-update-slice_fusion.1, bf16[72,136,128]{1,2,0:T(8,128)(2,1)S(1)} %get-tuple-element.5, s32[]{:T(128)S(6)} %select_n.183, s32[]{:T(128)S(6)} %select_n.182), kind=kLoop, calls=%fused_computation.22 | loop fusion | bytes 2097160 | tf_op jit(solution)/shard_map/concatenate | solution.py:38
  47.6 1.9 %fusion.72 = f32[64,128,128]{1,2,0:T(8,128)S(1)} fusion(bf16[64,128,576]{1,2,0:T(8,128)(2,1)S(1)} %dynamic-slice_dynamic-update-slice_fusion, bf16[576,128,1]{1,0,2:T(8,128)(2,1)S(1)} %bitcast.105), kind=kOutput, calls=%fused_computation.135 | convolution fusion | flops 1207959552 | bytes 13778944 | tf_op jit(solution)/shard_map/dot_general | solution.py:40
  49.5 0.9 %fusion.2 = bf16[8,8,64,128]{3,1,2,0:T(8,128)(2,1)S(1)} fusion(f32[64,128,128]{1,2,0:T(8,128)S(1)} %fusion.72, bf16[72,136,128]{1,2,0:T(8,128)(2,1)S(1)} %get-tuple-element.6, f32[64]{0:T(128)S(1)} %get-tuple-element.50), kind=kOutput, calls=%fused_computation.11 | convolution fusion | flops 73404416 | bytes 6291968 | tf_op jit(solution)/shard_map/ck,nk->cn/dot_general | solution.py:156
  50.4 1.3 %copy.40 = bf16[8,8,64,128]{3,2,1,0:T(8,128)(2,1)} copy(bf16[8,8,64,128]{3,1,2,0:T(8,128)(2,1)S(1)} %fusion.2) | data formatting | bytes 2097152
  (39 shorter events, 3.4 us)
Async XLA Ops:
  0.0 0.7 %copy-start = (bf16[8,128]{1,0:T(8,128)(2,1)S(1)}, bf16[8,128]{1,0:T(8,128)(2,1)}, u32[]{:S(2)}) copy-start(bf16[8,128]{1,0:T(8,128)(2,1)} %param.6) | copy-start | bytes 6148
  2.3 21.8 %all-to-all-start = ((bf16[128,2,256]{2,1,0:T(2,128)(2,1)}), bf16[128,2,256]{2,1,0:T(2,128)(2,1)S(1)}, u32[]{:S(2)}, u32[]{:S(2)}) async-start(bf16[128,2,256]{2,1,0:T(2,128)(2,1)} %broadcast_in_dim.188), calls=%async_computation | async-start | bytes 262144 | tf_op jit(solution)/shard_map/all_to_all | solution.py:15

commit v11 on v9

--- a/solution.py
+++ b/solution.py
@@ -32,7 +32,7 @@
         piece = lax.dynamic_slice(
             padded, (row_index, col_index, zero_index), (row_count, col_count, in_channels)
         )
-        pieces.append(piece.reshape(row_count * col_count, in_channels))
+        pieces.append(piece.reshape(row_count * col_count, in_channels).astype(jnp.bfloat16))
     stacked = jnp.concatenate(pieces, axis=1)
     flat_weight = jnp.transpose(weights, (0, 2, 1)).reshape(9 * in_channels, out_channels)
     summed = jnp.dot(stacked, flat_weight, preferred_element_type=jnp.float32)
@@ -137,7 +137,8 @@
         inside(row_places, bins_total)[:, None, None] * inside(col_places, bins_total)[None, :, None]
     ).astype(jnp.bfloat16)
     taps1 = jnp.concatenate([conv_weight[1], mirrored_taps(conv_weight[1])], axis=1)
-    conv1 = tap_groups(jax.nn.relu(map1) * mask1, taps1, dilations[1])
+    active1 = jax.nn.relu(map1).astype(jnp.float32) * mask1.astype(jnp.float32)
+    conv1 = tap_groups(active1, taps1, dilations[1])
     channels = conv_weight.shape[2]
     core = (slice(MAXDIL, MAXDIL + row_size), slice(MAXDIL, MAXDIL + col_size), slice(None))
     base1 = map1[core].astype(jnp.float32) + conv_bias[1][None, None, :]

time: 45 us -> 45.4 us (level)
  no operation moved by 1% of the time
where the time goes in v11:
time: 45.4 us; the launch traced here: 45 us
  local copies, waits for them, and re-layouts  13.7 us (30%)
  starting transfers between devices  11.5 us (25%)
  other arithmetic  8.82 us (19%)
  between operations  6.27 us (14%)
  matrix products  4.77 us (11%)
    all_to_all x1, starting transfers between devices, gather_projections(): lax.all_to_all(copies, axes, 0, 0, tiled=True).reshape(-1, proj.shape[1])  11.5 us
    unnamed x12, local copies, waits for them, and re-layouts  7.8 us
    mul x1, other arithmetic, local(): active1 = jax.nn.relu(map1).astype(jnp.float32) * mask1.astype(jnp.float32)  6.1 us
    dot_general x1, matrix products, tap_groups(): summed = jnp.dot(stacked, flat_weight, preferred_element_type=jnp.float32)  1.85 us
    slice x1, local copies, waits for them, and re-layouts, local(): conv1 = tap_groups(active1, taps1, dilations[1])  1.39 us
    lt x2, other arithmetic, pick(): near_low = (places < dilation).reshape(shape)  1.29 us
    squeeze x1, local copies, waits for them, and re-layouts, local(): conv_weight[1]  1.06 us
  transfers between devices with their start and end apart: 1, of which 0 were waited for; matrix products, arithmetic and copies ran while one was open for 11% of the time, Pallas kernels for 0%

profile of v11, /device:TPU:1, one launch (start us, length us, event | category | flops | bytes accessed | tf_op | source)
XLA Modules:
  0.0 45.0 jit_solution(9210114147928222528)
XLA Ops:
  0.0 0.7 %copy-done = bf16[8,128]{1,0:T(8,128)(2,1)S(1)} copy-done((bf16[8,128]{1,0:T(8,128)(2,1)S(1)}, bf16[8,128]{1,0:T(8,128)(2,1)}, u32[]{:S(2)}) %copy-start) | copy-done | bytes 2072
  0.7 0.8 %fusion.3 = bf16[8,64]{1,0:T(8,128)(2,1)S(1)} fusion(bf16[8,128]{1,0:T(8,128)(2,1)S(1)} %copy-done, bf16[128,32]{0,1:T(8,128)(2,1)} %param.8, bf16[128,32]{0,1:T(8,128)(2,1)} %param.7), kind=kOutput, calls=%fused_computation.26 | convolution fusion | flops 164352 | bytes 19456 | tf_op jit(solution)/shard_map/dot_general | solution.py:119
  1.6 0.7 %broadcast_in_dim.174 = bf16[128,2,256]{2,1,0:T(2,128)(2,1)} broadcast(bf16[2,256]{1,0:T(2,128)(2,1)S(1)} %broadcast_in_dim.173), dimensions={1,2} | broadcast | bytes 132096 | tf_op jit(solution)/shard_map/broadcast_in_dim | solution.py:14
  2.3 11.5 %all-to-all-start = ((bf16[128,2,256]{2,1,0:T(2,128)(2,1)}), bf16[128,2,256]{2,1,0:T(2,128)(2,1)S(1)}, u32[]{:S(2)}, u32[]{:S(2)}) async-start(bf16[128,2,256]{2,1,0:T(2,128)(2,1)} %broadcast_in_dim.174), calls=%async_computation | async-start | bytes 262144 | tf_op jit(solution)/shard_map/all_to_all | solution.py:15
  13.9 0.8 %slice_bitcast_fusion = (f32[64]{0:T(128)S(1)}, f32[64]{0:T(128)S(1)}) fusion(f32[2,64]{1,0:T(2,128)} %param.10), kind=kLoop, calls=%fused_computation.123 | loop fusion | bytes 1024 | tf_op jit(solution)/shard_map/add | solution.py:144
  14.6 1.4 %fusion.86 = (s32[1]{0:T(128)}, s32[1]{0:T(128)}) fusion(s32[2]{0:T(128)} %param.11), kind=kLoop, calls=%fused_computation.143 | loop fusion | bytes 16 | tf_op jit(solution)/shard_map/slice | solution.py:141
  16.7 1.1 %slice_bitcast_fusion.2 = (bf16[9,64,64]{2,1,0:T(8,128)(2,1)S(1)}, bf16[1,9,64,64]{3,2,1,0:T(8,128)(2,1)S(1)}, bf16[1,9,64,64]{3,2,1,0:T(8,128)(2,1)S(1)}) fusion(bf16[2,9,64,64]{3,2,1,0:T(8,128)(2,1)} %param.9), kind=kLoop, calls=%fused_computation.134 | loop fusion | bytes 368640 | tf_op jit(solution)/shard_map/squeeze | solution.py:139
  17.9 0.6 %fusion.64 = pred[72]{0:T(512)(128)(4,1)S(1)} fusion(s32[]{:T(128)} %bitcast, s32[]{:T(128)S(6)} %sub.14), kind=kLoop, calls=%fused_computation.126 | loop fusion | flops 144 | bytes 80 | tf_op jit(solution)/shard_map/lt | solution.py:100
  24.2 0.7 %fusion.62 = pred[136]{0:T(512)(128)(4,1)S(1)} fusion(s32[]{:T(128)} %bitcast, s32[]{:T(128)S(6)} %sub.12), kind=kLoop, calls=%fused_computation.122 | loop fusion | flops 272 | bytes 144 | tf_op jit(solution)/shard_map/lt | solution.py:100
  25.8 0.3 convolution_bitcast_fusion.1
  26.2 0.3 convolution_bitcast_fusion
  28.4 6.1 %convert_multiply_fusion = (bf16[72,136,64]{1,2,0:T(8,128)(2,1)S(1)}, bf16[72,136,64]{1,2,0:T(8,128)(2,1)S(1)}) fusion(f32[72,136]{1,0:T(8,128)S(1)} %fusion.36, f32[72,64]{1,0:T(8,128)S(1)} %copy.24, f32[72,64]{1,0:T(8,128)S(1)} %copy.23, f32[72,64]{1,0:T(8,128)S(1)} %copy.22, f32[136,64]{0,1:T(8,128)S(1)} %get-tuple-element.17, ...), kind=kLoop, calls=%fused_computation.1 | loop fusion | flops 14413824 | bytes 2865824 | tf_op jit(solution)/shard_map/mul | solution.py:140
  34.5 0.5 %fusion.4 = bf16[64,128,576]{1,2,0:T(8,128)(2,1)S(1)} fusion(bf16[72,136,64]{1,2,0:T(8,128)(2,1)S(1)} %get-tuple-element.5, s32[]{:T(128)S(6)} %select_n.128, s32[]{:T(128)S(6)} %select_n.129), kind=kLoop, calls=%fused_computation.27 | loop fusion | bytes 2097160
  35.0 0.7 %fusion.5 = bf16[64,128,576]{1,2,0:T(8,128)(2,1)S(1)} fusion(bf16[64,128,576]{1,2,0:T(8,128)(2,1)S(1)} %fusion.4, bf16[72,136,64]{1,2,0:T(8,128)(2,1)S(1)} %get-tuple-element.5, s32[]{:T(128)S(6)} %select_n.128), kind=kLoop, calls=%fused_computation.28 | loop fusion | bytes 2097156
  35.7 0.8 %fusion.6 = bf16[64,128,576]{1,2,0:T(8,128)(2,1)S(1)} fusion(bf16[64,128,576]{1,2,0:T(8,128)(2,1)S(1)} %fusion.5, bf16[72,136,64]{1,2,0:T(8,128)(2,1)S(1)} %get-tuple-element.5, s32[]{:T(128)S(6)} %select_n.128, s32[]{:T(128)S(6)} %select_n.130), kind=kLoop, calls=%fused_computation.29 | loop fusion | bytes 2097160
  36.5 0.8 %fusion.7 = bf16[64,128,576]{1,2,0:T(8,128)(2,1)S(1)} fusion(bf16[64,128,576]{1,2,0:T(8,128)(2,1)S(1)} %fusion.6, bf16[72,136,64]{1,2,0:T(8,128)(2,1)S(1)} %get-tuple-element.5, s32[]{:T(128)S(6)} %select_n.129), kind=kLoop, calls=%fused_computation.30 | loop fusion | bytes 2097156
  37.3 0.7 %fusion.13 = bf16[64,128,576]{1,2,0:T(8,128)(2,1)S(1)} fusion(bf16[64,128,576]{1,2,0:T(8,128)(2,1)S(1)} %fusion.7, bf16[72,136,64]{1,2,0:T(8,128)(2,1)S(1)} %get-tuple-element.5), kind=kLoop, calls=%fused_computation.36 | loop fusion | bytes 2097152
  38.0 0.8 %fusion.8 = bf16[64,128,576]{1,2,0:T(8,128)(2,1)S(1)} fusion(bf16[64,128,576]{1,2,0:T(8,128)(2,1)S(1)} %fusion.13, bf16[72,136,64]{1,2,0:T(8,128)(2,1)S(1)} %get-tuple-element.5, s32[]{:T(128)S(6)} %select_n.130), kind=kLoop, calls=%fused_computation.31 | loop fusion | bytes 2097156
  38.8 0.8 %fusion.9 = bf16[64,128,576]{1,2,0:T(8,128)(2,1)S(1)} fusion(bf16[64,128,576]{1,2,0:T(8,128)(2,1)S(1)} %fusion.8, bf16[72,136,64]{1,2,0:T(8,128)(2,1)S(1)} %get-tuple-element.5, s32[]{:T(128)S(6)} %select_n.131, s32[]{:T(128)S(6)} %select_n.129), kind=kLoop, calls=%fused_computation.32 | loop fusion | bytes 2097160
  39.5 0.7 %fusion.10 = bf16[64,128,576]{1,2,0:T(8,128)(2,1)S(1)} fusion(bf16[64,128,576]{1,2,0:T(8,128)(2,1)S(1)} %fusion.9, bf16[72,136,64]{1,2,0:T(8,128)(2,1)S(1)} %get-tuple-element.5, s32[]{:T(128)S(6)} %select_n.131), kind=kLoop, calls=%fused_computation.33 | loop fusion | bytes 2097156
  40.3 0.8 %fusion.11 = bf16[64,128,576]{1,2,0:T(8,128)(2,1)S(1)} fusion(bf16[64,128,576]{1,2,0:T(8,128)(2,1)S(1)} %fusion.10, bf16[72,136,64]{1,2,0:T(8,128)(2,1)S(1)} %get-tuple-element.5, s32[]{:T(128)S(6)} %select_n.131, s32[]{:T(128)S(6)} %select_n.130), kind=kLoop, calls=%fused_computation.34 | loop fusion | bytes 2097160 | tf_op jit(solution)/shard_map/concatenate | solution.py:36
  41.0 1.9 %fusion.87 = f32[64,128,128]{1,2,0:T(8,128)S(1)} fusion(bf16[64,128,576]{1,2,0:T(8,128)(2,1)S(1)} %fusion.11, bf16[576,128,1]{1,0,2:T(8,128)(2,1)S(1)} %bitcast.126), kind=kOutput, calls=%fused_computation.144 | convolution fusion | flops 1207959552 | bytes 13778944 | tf_op jit(solution)/shard_map/dot_general | solution.py:38
  42.9 0.9 %fusion.2 = bf16[8,8,64,128]{3,1,2,0:T(8,128)(2,1)S(1)} fusion(f32[64,128,128]{1,2,0:T(8,128)S(1)} %fusion.87, bf16[72,136,64]{1,2,0:T(8,128)(2,1)S(1)} %get-tuple-element.6, f32[64]{0:T(128)S(1)} %get-tuple-element.54), kind=kOutput, calls=%fused_computation.20 | convolution fusion | flops 73404416 | bytes 6291968 | tf_op jit(solution)/shard_map/ck,nk->cn/dot_general | solution.py:151
  43.8 1.3 %copy.30 = bf16[8,8,64,128]{3,2,1,0:T(8,128)(2,1)} copy(bf16[8,8,64,128]{3,1,2,0:T(8,128)(2,1)S(1)} %fusion.2) | data formatting | bytes 2097152
  (30 shorter events, 3.3 us)
Async XLA Ops:
  0.0 0.7 %copy-start = (bf16[8,128]{1,0:T(8,128)(2,1)S(1)}, bf16[8,128]{1,0:T(8,128)(2,1)}, u32[]{:S(2)}) copy-start(bf16[8,128]{1,0:T(8,128)(2,1)} %param.6) | copy-start | bytes 6148
  2.3 22.6 %all-to-all-start = ((bf16[128,2,256]{2,1,0:T(2,128)(2,1)}), bf16[128,2,256]{2,1,0:T(2,128)(2,1)S(1)}, u32[]{:S(2)}, u32[]{:S(2)}) async-start(bf16[128,2,256]{2,1,0:T(2,128)(2,1)} %broadcast_in_dim.174), calls=%async_computation | async-start | bytes 262144 | tf_op jit(solution)/shard_map/all_to_all | solution.py:15

commit v12 on v9

--- a/solution.py
+++ b/solution.py
@@ -50,29 +50,31 @@
     active = jnp.pad(jax.nn.relu(every), ((REACH, REACH), (0, 0)))
     padded = jnp.pad(every, ((MAXDIL, MAXDIL), (0, 0)))
 
+    grid = taps.reshape(3, 3, *taps.shape[1:])
+    out_ch = taps.shape[1]
+    by_shift_row = jnp.transpose(grid[..., :half], (0, 3, 1, 2)).reshape(3, half, 3 * out_ch)
+    by_shift_col = jnp.transpose(grid[..., half:], (1, 3, 0, 2)).reshape(3, half, 3 * out_ch)
+    nothing = jnp.zeros_like(by_shift_row)
+    weight = jnp.concatenate(
+        [
+            jnp.concatenate([by_shift_row, nothing], axis=2),
+            jnp.concatenate([nothing, by_shift_col], axis=2),
+        ],
+        axis=1,
+    ).reshape(3 * 2 * half, 6 * out_ch)
+
     def tables(start, count):
         window = lax.dynamic_slice_in_dim(active, start, count + 2 * MAXDIL, 0)
-        row_part = jnp.einsum(
-            "nk,tok->tno", window[:, :half], taps[:, :, :half], preferred_element_type=jnp.float32
+        shifted = jnp.concatenate(
+            [
+                lax.dynamic_slice_in_dim(window, MAXDIL + (step - 1) * dilation, count, 0)
+                for step in range(3)
+            ],
+            axis=1,
         )
-        col_part = jnp.einsum(
-            "nk,tok->tno", window[:, half:], taps[:, :, half:], preferred_element_type=jnp.float32
-        )
-        by_col, by_row = [], []
-        for outer in range(3):
-            along_rows = None
-            along_cols = None
-            for inner in range(3):
-                piece_r = lax.dynamic_slice_in_dim(
-                    row_part[3 * inner + outer], MAXDIL + (inner - 1) * dilation, count, 0
-                )
-                piece_c = lax.dynamic_slice_in_dim(
-                    col_part[3 * outer + inner], MAXDIL + (inner - 1) * dilation, count, 0
-                )
-                along_rows = piece_r if along_rows is None else along_rows + piece_r
-                along_cols = piece_c if along_cols is None else along_cols + piece_c
-            by_col.append(along_rows)
-            by_row.append(along_cols)
+        parts = jnp.dot(shifted, weight, preferred_element_type=jnp.float32)
+        by_col = [parts[:, out_ch * k : out_ch * (k + 1)] for k in range(3)]
+        by_row = [parts[:, out_ch * (3 + k) : out_ch * (4 + k)] for k in range(3)]
         own = lax.dynamic_slice_in_dim(padded, start, count, 0)
         own_row = jnp.where(lower, own, 0.0) + shift_bias[None, :]
         own_col = jnp.where(lower, 0.0, own)

time: 45 us -> 42.9 us (0.953)
  other arithmetic: 8.42 us -> 7.36 us
  matrix products: 4.77 us -> 4.01 us
  between operations: 6.28 us -> 5.65 us
    lt x2 -> x0, other arithmetic: 1.29 us -> none  [pick(): near_low = (places < dilation).reshape(shape)]
    ge x0 -> x2, other arithmetic: none -> 1.13 us  [pick(): near_high = (places >= bins_total - dilation).reshape(shape)]
    dot_general x4 -> x2, matrix products: 1.2 us -> 0.44 us  [tables(): parts = jnp.dot(shifted, weight, preferred_element_type=jnp.float32)]
    add x2 -> x0, other arithmetic: 0.53 us -> none  [the longest x1 0.32 us: tables(): own_col + by_row[1] + by_row[2]]
    unnamed x12 -> x13, local copies, waits for them, and re-layouts: 7.8 us -> 7.94 us
  transfers between devices with their start and end apart: 1 -> 1, of which waited for: 0 -> 0; matrix products, arithmetic and copies ran while one was open for 11% -> 13% of each run, Pallas kernels for 0% -> 0%
where the time goes in v12:
time: 42.9 us; the launch traced here: 42.6 us
  local copies, waits for them, and re-layouts  14.1 us (33%)
  starting transfers between devices  11.5 us (27%)
  other arithmetic  7.36 us (17%)
  between operations  5.65 us (13%)
  matrix products  4.01 us (9%)
    all_to_all x1, starting transfers between devices, gather_projections(): lax.all_to_all(copies, axes, 0, 0, tiled=True).reshape(-1, proj.shape[1])  11.5 us
    unnamed x13, local copies, waits for them, and re-layouts  7.94 us
    mul x1, other arithmetic, local(): conv1 = tap_groups(jax.nn.relu(map1) * mask1, taps1, dilations[1])  5.71 us
    dot_general x1, matrix products, tap_groups(): summed = jnp.dot(stacked, flat_weight, preferred_element_type=jnp.float32)  1.85 us
    slice x1, local copies, waits for them, and re-layouts, local(): conv1 = tap_groups(jax.nn.relu(map1) * mask1, taps1, dilations[1])  1.38 us
    ge x2, other arithmetic, pick(): near_high = (places >= bins_total - dilation).reshape(shape)  1.13 us
    squeeze x1, local copies, waits for them, and re-layouts, local(): conv_weight[1]  1.05 us
    dot_general x1, matrix products, local(): jnp.einsum('ck,nk->cn', jnp.eye(channels, dtype=pair.dtype), flat, prefer...  0.89 us
  transfers between devices with their start and end apart: 1, of which 0 were waited for; matrix products, arithmetic and copies ran while one was open for 13% of the time, Pallas kernels for 0%

profile of v12, /device:TPU:1, one launch (start us, length us, event | category | flops | bytes accessed | tf_op | source)
XLA Modules:
  0.0 42.6 jit_solution(11182066590688857508)
XLA Ops:
  0.0 0.7 %copy-done = bf16[8,128]{1,0:T(8,128)(2,1)S(1)} copy-done((bf16[8,128]{1,0:T(8,128)(2,1)S(1)}, bf16[8,128]{1,0:T(8,128)(2,1)}, u32[]{:S(2)}) %copy-start) | copy-done | bytes 2072
  0.7 0.8 %fusion.3 = bf16[8,64]{1,0:T(8,128)(2,1)S(1)} fusion(bf16[8,128]{1,0:T(8,128)(2,1)S(1)} %copy-done, bf16[128,32]{0,1:T(8,128)(2,1)} %param.8, bf16[128,32]{0,1:T(8,128)(2,1)} %param.7), kind=kOutput, calls=%fused_computation.13 | convolution fusion | flops 164352 | bytes 19456 | tf_op jit(solution)/shard_map/dot_general | solution.py:121
  1.6 0.7 %broadcast_in_dim.175 = bf16[128,2,256]{2,1,0:T(2,128)(2,1)} broadcast(bf16[2,256]{1,0:T(2,128)(2,1)S(1)} %broadcast_in_dim.174), dimensions={1,2} | broadcast | bytes 132096 | tf_op jit(solution)/shard_map/broadcast_in_dim | solution.py:14
  2.3 11.5 %all-to-all-start = ((bf16[128,2,256]{2,1,0:T(2,128)(2,1)}), bf16[128,2,256]{2,1,0:T(2,128)(2,1)S(1)}, u32[]{:S(2)}, u32[]{:S(2)}) async-start(bf16[128,2,256]{2,1,0:T(2,128)(2,1)} %broadcast_in_dim.175), calls=%async_computation | async-start | bytes 262144 | tf_op jit(solution)/shard_map/all_to_all | solution.py:15
  13.9 1.4 %fusion.43 = (s32[1]{0:T(128)}, s32[1]{0:T(128)}) fusion(s32[2]{0:T(128)} %param.11), kind=kLoop, calls=%fused_computation.98 | loop fusion | bytes 16 | tf_op jit(solution)/shard_map/slice | solution.py:142
  15.8 0.6 %fusion.33 = (pred[72]{0:T(512)(128)(4,1)S(1)}, pred[72]{0:T(512)(128)(4,1)S(1)}) fusion(s32[]{:T(128)S(6)} %sub.13, s32[]{:T(128)S(6)} %sub.14, s32[]{:T(128)} %bitcast), kind=kLoop, calls=%fused_computation.89 | loop fusion | flops 216 | bytes 156 | tf_op jit(solution)/shard_map/ge | solution.py:103
  16.4 0.6 %fusion.31 = (pred[136]{0:T(512)(128)(4,1)S(1)}, pred[136]{0:T(512)(128)(4,1)S(1)}) fusion(s32[]{:T(128)S(6)} %sub.13, s32[]{:T(128)S(6)} %sub.12, s32[]{:T(128)} %bitcast), kind=kLoop, calls=%fused_computation.85 | loop fusion | flops 408 | bytes 284 | tf_op jit(solution)/shard_map/ge | solution.py:103
  17.0 0.8 %slice_bitcast_fusion = (f32[64]{0:T(128)S(1)}, f32[64]{0:T(128)S(1)}) fusion(f32[2,64]{1,0:T(2,128)} %param.10), kind=kLoop, calls=%fused_computation.87 | loop fusion | bytes 1024 | tf_op jit(solution)/shard_map/add | solution.py:145
  17.7 1.1 %slice_bitcast_fusion.2 = (bf16[9,64,64]{2,1,0:T(8,128)(2,1)S(1)}, bf16[1,9,64,64]{3,2,1,0:T(8,128)(2,1)S(1)}, bf16[1,9,64,64]{3,2,1,0:T(8,128)(2,1)S(1)}) fusion(bf16[2,9,64,64]{3,2,1,0:T(8,128)(2,1)} %param.9), kind=kLoop, calls=%fused_computation.96 | loop fusion | bytes 368640 | tf_op jit(solution)/shard_map/squeeze | solution.py:141
  24.7 0.2 reshape.151
  25.0 0.2 fusion.13
  26.3 5.7 %maximum_multiply_fusion = (bf16[72,136,64]{1,2,0:T(8,128)(2,1)S(1)}, bf16[72,136,64]{1,2,0:T(8,128)(2,1)S(1)}) fusion(bf16[72,136]{1,0:T(8,128)(2,1)S(1)} %multiply_convert_fusion.2, f32[72,64]{1,0:T(8,128)S(1)} %get-tuple-element.22, f32[72,64]{1,0:T(8,128)S(1)} %get-tuple-element.23, f32[72,64]{1,0:T(8,128)S(1)} %get-tuple-element.24, ...), kind=kLoop, calls=%fused_computation.4 | loop fusion | flops 11907072 | bytes 2846240 | tf_op jit(solution)/shard_map/mul | solution.py:142
  32.0 0.5 %dynamic-slice_dynamic-update-slice_fusion.7 = bf16[64,128,576]{1,2,0:T(8,128)(2,1)S(1)} fusion(bf16[72,136,64]{1,2,0:T(8,128)(2,1)S(1)} %get-tuple-element.5, s32[]{:T(128)S(6)} %select_n.126, s32[]{:T(128)S(6)} %select_n.127), kind=kLoop, calls=%fused_computation.25 | loop fusion | bytes 2097160
  32.5 0.7 %dynamic-slice_dynamic-update-slice_fusion.6 = bf16[64,128,576]{1,2,0:T(8,128)(2,1)S(1)} fusion(bf16[64,128,576]{1,2,0:T(8,128)(2,1)S(1)} %dynamic-slice_dynamic-update-slice_fusion.7, bf16[72,136,64]{1,2,0:T(8,128)(2,1)S(1)} %get-tuple-element.5, s32[]{:T(128)S(6)} %select_n.126), kind=kLoop, calls=%fused_computation.24 | loop fusion | bytes 2097156
  33.2 0.8 %dynamic-slice_dynamic-update-slice_fusion.5 = bf16[64,128,576]{1,2,0:T(8,128)(2,1)S(1)} fusion(bf16[64,128,576]{1,2,0:T(8,128)(2,1)S(1)} %dynamic-slice_dynamic-update-slice_fusion.6, bf16[72,136,64]{1,2,0:T(8,128)(2,1)S(1)} %get-tuple-element.5, s32[]{:T(128)S(6)} %select_n.126, s32[]{:T(128)S(6)} %select_n.128), kind=kLoop, calls=%fused_computation.23 | loop fusion | bytes 2097160
  34.0 0.8 %dynamic-slice_dynamic-update-slice_fusion.4 = bf16[64,128,576]{1,2,0:T(8,128)(2,1)S(1)} fusion(bf16[64,128,576]{1,2,0:T(8,128)(2,1)S(1)} %dynamic-slice_dynamic-update-slice_fusion.5, bf16[72,136,64]{1,2,0:T(8,128)(2,1)S(1)} %get-tuple-element.5, s32[]{:T(128)S(6)} %select_n.127), kind=kLoop, calls=%fused_computation.22 | loop fusion | bytes 2097156
  34.8 0.7 %slice_dynamic-update-slice_fusion = bf16[64,128,576]{1,2,0:T(8,128)(2,1)S(1)} fusion(bf16[64,128,576]{1,2,0:T(8,128)(2,1)S(1)} %dynamic-slice_dynamic-update-slice_fusion.4, bf16[72,136,64]{1,2,0:T(8,128)(2,1)S(1)} %get-tuple-element.5), kind=kLoop, calls=%fused_computation.17 | loop fusion | bytes 2097152
  35.5 0.8 %dynamic-slice_dynamic-update-slice_fusion.3 = bf16[64,128,576]{1,2,0:T(8,128)(2,1)S(1)} fusion(bf16[64,128,576]{1,2,0:T(8,128)(2,1)S(1)} %slice_dynamic-update-slice_fusion, bf16[72,136,64]{1,2,0:T(8,128)(2,1)S(1)} %get-tuple-element.5, s32[]{:T(128)S(6)} %select_n.128), kind=kLoop, calls=%fused_computation.21 | loop fusion | bytes 2097156
  36.3 0.8 %dynamic-slice_dynamic-update-slice_fusion.2 = bf16[64,128,576]{1,2,0:T(8,128)(2,1)S(1)} fusion(bf16[64,128,576]{1,2,0:T(8,128)(2,1)S(1)} %dynamic-slice_dynamic-update-slice_fusion.3, bf16[72,136,64]{1,2,0:T(8,128)(2,1)S(1)} %get-tuple-element.5, s32[]{:T(128)S(6)} %select_n.129, s32[]{:T(128)S(6)} %select_n.127), kind=kLoop, calls=%fused_computation.20 | loop fusion | bytes 2097160
  37.1 0.7 %dynamic-slice_dynamic-update-slice_fusion.1 = bf16[64,128,576]{1,2,0:T(8,128)(2,1)S(1)} fusion(bf16[64,128,576]{1,2,0:T(8,128)(2,1)S(1)} %dynamic-slice_dynamic-update-slice_fusion.2, bf16[72,136,64]{1,2,0:T(8,128)(2,1)S(1)} %get-tuple-element.5, s32[]{:T(128)S(6)} %select_n.129), kind=kLoop, calls=%fused_computation.19 | loop fusion | bytes 2097156
  37.8 0.8 %dynamic-slice_dynamic-update-slice_fusion = bf16[64,128,576]{1,2,0:T(8,128)(2,1)S(1)} fusion(bf16[64,128,576]{1,2,0:T(8,128)(2,1)S(1)} %dynamic-slice_dynamic-update-slice_fusion.1, bf16[72,136,64]{1,2,0:T(8,128)(2,1)S(1)} %get-tuple-element.5, s32[]{:T(128)S(6)} %select_n.129, s32[]{:T(128)S(6)} %select_n.128), kind=kLoop, calls=%fused_computation.18 | loop fusion | bytes 2097160 | tf_op jit(solution)/shard_map/concatenate | solution.py:36
  38.6 1.9 %fusion.44 = f32[64,128,128]{1,2,0:T(8,128)S(1)} fusion(bf16[64,128,576]{1,2,0:T(8,128)(2,1)S(1)} %dynamic-slice_dynamic-update-slice_fusion, bf16[576,128,1]{1,0,2:T(8,128)(2,1)S(1)} %bitcast.46), kind=kOutput, calls=%fused_computation.99 | convolution fusion | flops 1207959552 | bytes 13778944 | tf_op jit(solution)/shard_map/dot_general | solution.py:38
  40.4 0.9 %fusion.2 = bf16[8,8,64,128]{3,1,2,0:T(8,128)(2,1)S(1)} fusion(f32[64,128,128]{1,2,0:T(8,128)S(1)} %fusion.44, bf16[72,136,64]{1,2,0:T(8,128)(2,1)S(1)} %get-tuple-element.6, f32[64]{0:T(128)S(1)} %get-tuple-element.36), kind=kOutput, calls=%fused_computation.11 | convolution fusion | flops 73404416 | bytes 6291968 | tf_op jit(solution)/shard_map/ck,nk->cn/dot_general | solution.py:152
  41.3 1.3 %copy.40 = bf16[8,8,64,128]{3,2,1,0:T(8,128)(2,1)} copy(bf16[8,8,64,128]{3,1,2,0:T(8,128)(2,1)S(1)} %fusion.2) | data formatting | bytes 2097152
  (28 shorter events, 2.2 us)
Async XLA Ops:
  0.0 0.7 %copy-start = (bf16[8,128]{1,0:T(8,128)(2,1)S(1)}, bf16[8,128]{1,0:T(8,128)(2,1)}, u32[]{:S(2)}) copy-start(bf16[8,128]{1,0:T(8,128)(2,1)} %param.6) | copy-start | bytes 6148
  2.3 22.4 %all-to-all-start = ((bf16[128,2,256]{2,1,0:T(2,128)(2,1)}), bf16[128,2,256]{2,1,0:T(2,128)(2,1)S(1)}, u32[]{:S(2)}, u32[]{:S(2)}) async-start(bf16[128,2,256]{2,1,0:T(2,128)(2,1)} %broadcast_in_dim.175), calls=%async_computation | async-start | bytes 262144 | tf_op jit(solution)/shard_map/all_to_all | solution.py:15

commit v13 on v12

--- a/solution.py
+++ b/solution.py
@@ -54,6 +54,13 @@
     out_ch = taps.shape[1]
     by_shift_row = jnp.transpose(grid[..., :half], (0, 3, 1, 2)).reshape(3, half, 3 * out_ch)
     by_shift_col = jnp.transpose(grid[..., half:], (1, 3, 0, 2)).reshape(3, half, 3 * out_ch)
+    lane_group = 2 * out_ch
+    by_shift_row, by_shift_col = (
+        jnp.pad(w.reshape(3, half, 3, out_ch), ((0, 0), (0, 0), (0, 0), (0, lane_group - out_ch))).reshape(
+            3, half, 3 * lane_group
+        )
+        for w in (by_shift_row, by_shift_col)
+    )
     nothing = jnp.zeros_like(by_shift_row)
     weight = jnp.concatenate(
         [
@@ -61,7 +68,7 @@
             jnp.concatenate([nothing, by_shift_col], axis=2),
         ],
         axis=1,
-    ).reshape(3 * 2 * half, 6 * out_ch)
+    ).reshape(3 * 2 * half, 6 * lane_group)
 
     def tables(start, count):
         window = lax.dynamic_slice_in_dim(active, start, count + 2 * MAXDIL, 0)
@@ -73,8 +80,8 @@
             axis=1,
         )
         parts = jnp.dot(shifted, weight, preferred_element_type=jnp.float32)
-        by_col = [parts[:, out_ch * k : out_ch * (k + 1)] for k in range(3)]
-        by_row = [parts[:, out_ch * (3 + k) : out_ch * (4 + k)] for k in range(3)]
+        by_col = [parts[:, lane_group * k : lane_group * k + out_ch] for k in range(3)]
+        by_row = [parts[:, lane_group * (3 + k) : lane_group * (3 + k) + out_ch] for k in range(3)]
         own = lax.dynamic_slice_in_dim(padded, start, count, 0)
         own_row = jnp.where(lower, own, 0.0) + shift_bias[None, :]
         own_col = jnp.where(lower, 0.0, own)

time: 42.9 us -> 42.8 us (level)
  no operation moved by 1% of the time
where the time goes in v13:
time: 42.8 us; the launch traced here: 42.4 us
  local copies, waits for them, and re-layouts  14.1 us (33%)
  starting transfers between devices  11.5 us (27%)
  other arithmetic  7.16 us (17%)
  between operations  5.68 us (13%)
  matrix products  4.06 us (9%)
    all_to_all x1, starting transfers between devices, gather_projections(): lax.all_to_all(copies, axes, 0, 0, tiled=True).reshape(-1, proj.shape[1])  11.5 us
    unnamed x13, local copies, waits for them, and re-layouts  7.93 us
    mul x1, other arithmetic, local(): conv1 = tap_groups(jax.nn.relu(map1) * mask1, taps1, dilations[1])  5.72 us
    dot_general x1, matrix products, tap_groups(): summed = jnp.dot(stacked, flat_weight, preferred_element_type=jnp.float32)  1.85 us
    slice x1, local copies, waits for them, and re-layouts, local(): conv1 = tap_groups(jax.nn.relu(map1) * mask1, taps1, dilations[1])  1.38 us
    ge x2, other arithmetic, pick(): near_high = (places >= bins_total - dilation).reshape(shape)  1.13 us
    squeeze x1, local copies, waits for them, and re-layouts, local(): conv_weight[1]  1.05 us
    dot_general x1, matrix products, local(): jnp.einsum('ck,nk->cn', jnp.eye(channels, dtype=pair.dtype), flat, prefer...  0.89 us
  transfers between devices with their start and end apart: 1, of which 0 were waited for; matrix products, arithmetic and copies ran while one was open for 13% of the time, Pallas kernels for 0%

profile of v13, /device:TPU:1, one launch (start us, length us, event | category | flops | bytes accessed | tf_op | source)
XLA Modules:
  0.0 42.4 jit_solution(3096029051418905144)
XLA Ops:
  0.0 0.7 %copy-done = bf16[8,128]{1,0:T(8,128)(2,1)S(1)} copy-done((bf16[8,128]{1,0:T(8,128)(2,1)S(1)}, bf16[8,128]{1,0:T(8,128)(2,1)}, u32[]{:S(2)}) %copy-start) | copy-done | bytes 2072
  0.7 0.8 %fusion.3 = bf16[8,64]{1,0:T(8,128)(2,1)S(1)} fusion(bf16[8,128]{1,0:T(8,128)(2,1)S(1)} %copy-done, bf16[128,32]{0,1:T(8,128)(2,1)} %param.8, bf16[128,32]{0,1:T(8,128)(2,1)} %param.7), kind=kOutput, calls=%fused_computation.13 | convolution fusion | flops 164352 | bytes 19456 | tf_op jit(solution)/shard_map/dot_general | solution.py:128
  1.6 0.7 %broadcast_in_dim.175 = bf16[128,2,256]{2,1,0:T(2,128)(2,1)} broadcast(bf16[2,256]{1,0:T(2,128)(2,1)S(1)} %broadcast_in_dim.174), dimensions={1,2} | broadcast | bytes 132096 | tf_op jit(solution)/shard_map/broadcast_in_dim | solution.py:14
  2.3 11.5 %all-to-all-start = ((bf16[128,2,256]{2,1,0:T(2,128)(2,1)}), bf16[128,2,256]{2,1,0:T(2,128)(2,1)S(1)}, u32[]{:S(2)}, u32[]{:S(2)}) async-start(bf16[128,2,256]{2,1,0:T(2,128)(2,1)} %broadcast_in_dim.175), calls=%async_computation | async-start | bytes 262144 | tf_op jit(solution)/shard_map/all_to_all | solution.py:15
  13.9 1.4 %fusion.43 = (s32[1]{0:T(128)}, s32[1]{0:T(128)}) fusion(s32[2]{0:T(128)} %param.11), kind=kLoop, calls=%fused_computation.98 | loop fusion | bytes 16 | tf_op jit(solution)/shard_map/slice | solution.py:149
  15.8 0.6 %fusion.33 = (pred[72]{0:T(512)(128)(4,1)S(1)}, pred[72]{0:T(512)(128)(4,1)S(1)}) fusion(s32[]{:T(128)S(6)} %sub.13, s32[]{:T(128)S(6)} %sub.14, s32[]{:T(128)} %bitcast), kind=kLoop, calls=%fused_computation.89 | loop fusion | flops 216 | bytes 156 | tf_op jit(solution)/shard_map/ge | solution.py:110
  16.4 0.6 %fusion.31 = (pred[136]{0:T(512)(128)(4,1)S(1)}, pred[136]{0:T(512)(128)(4,1)S(1)}) fusion(s32[]{:T(128)S(6)} %sub.13, s32[]{:T(128)S(6)} %sub.12, s32[]{:T(128)} %bitcast), kind=kLoop, calls=%fused_computation.85 | loop fusion | flops 408 | bytes 284 | tf_op jit(solution)/shard_map/ge | solution.py:110
  17.0 0.8 %slice_bitcast_fusion = (f32[64]{0:T(128)S(1)}, f32[64]{0:T(128)S(1)}) fusion(f32[2,64]{1,0:T(2,128)} %param.10), kind=kLoop, calls=%fused_computation.87 | loop fusion | bytes 1024 | tf_op jit(solution)/shard_map/add | solution.py:152
  17.7 1.1 %slice_bitcast_fusion.2 = (bf16[9,64,64]{2,1,0:T(8,128)(2,1)S(1)}, bf16[1,9,64,64]{3,2,1,0:T(8,128)(2,1)S(1)}, bf16[1,9,64,64]{3,2,1,0:T(8,128)(2,1)S(1)}) fusion(bf16[2,9,64,64]{3,2,1,0:T(8,128)(2,1)} %param.9), kind=kLoop, calls=%fused_computation.96 | loop fusion | bytes 368640 | tf_op jit(solution)/shard_map/squeeze | solution.py:148
  25.0 0.3 fusion.13
  25.9 0.2 fusion.22
  26.2 5.7 %maximum_multiply_fusion = (bf16[72,136,64]{1,2,0:T(8,128)(2,1)S(1)}, bf16[72,136,64]{1,2,0:T(8,128)(2,1)S(1)}) fusion(bf16[72,136]{1,0:T(8,128)(2,1)S(1)} %multiply_convert_fusion.2, f32[72,64]{1,0:T(8,128)S(1)} %get-tuple-element.22, f32[72,64]{1,0:T(8,128)S(1)} %get-tuple-element.23, f32[72,64]{1,0:T(8,128)S(1)} %get-tuple-element.24, ...), kind=kLoop, calls=%fused_computation.4 | loop fusion | flops 11907072 | bytes 2846240 | tf_op jit(solution)/shard_map/mul | solution.py:149
  31.9 0.5 %dynamic-slice_dynamic-update-slice_fusion.7 = bf16[64,128,576]{1,2,0:T(8,128)(2,1)S(1)} fusion(bf16[72,136,64]{1,2,0:T(8,128)(2,1)S(1)} %get-tuple-element.5, s32[]{:T(128)S(6)} %select_n.126, s32[]{:T(128)S(6)} %select_n.127), kind=kLoop, calls=%fused_computation.25 | loop fusion | bytes 2097160
  32.4 0.7 %dynamic-slice_dynamic-update-slice_fusion.6 = bf16[64,128,576]{1,2,0:T(8,128)(2,1)S(1)} fusion(bf16[64,128,576]{1,2,0:T(8,128)(2,1)S(1)} %dynamic-slice_dynamic-update-slice_fusion.7, bf16[72,136,64]{1,2,0:T(8,128)(2,1)S(1)} %get-tuple-element.5, s32[]{:T(128)S(6)} %select_n.126), kind=kLoop, calls=%fused_computation.24 | loop fusion | bytes 2097156
  33.1 0.8 %dynamic-slice_dynamic-update-slice_fusion.5 = bf16[64,128,576]{1,2,0:T(8,128)(2,1)S(1)} fusion(bf16[64,128,576]{1,2,0:T(8,128)(2,1)S(1)} %dynamic-slice_dynamic-update-slice_fusion.6, bf16[72,136,64]{1,2,0:T(8,128)(2,1)S(1)} %get-tuple-element.5, s32[]{:T(128)S(6)} %select_n.126, s32[]{:T(128)S(6)} %select_n.128), kind=kLoop, calls=%fused_computation.23 | loop fusion | bytes 2097160
  33.9 0.8 %dynamic-slice_dynamic-update-slice_fusion.4 = bf16[64,128,576]{1,2,0:T(8,128)(2,1)S(1)} fusion(bf16[64,128,576]{1,2,0:T(8,128)(2,1)S(1)} %dynamic-slice_dynamic-update-slice_fusion.5, bf16[72,136,64]{1,2,0:T(8,128)(2,1)S(1)} %get-tuple-element.5, s32[]{:T(128)S(6)} %select_n.127), kind=kLoop, calls=%fused_computation.22 | loop fusion | bytes 2097156
  34.7 0.7 %slice_dynamic-update-slice_fusion = bf16[64,128,576]{1,2,0:T(8,128)(2,1)S(1)} fusion(bf16[64,128,576]{1,2,0:T(8,128)(2,1)S(1)} %dynamic-slice_dynamic-update-slice_fusion.4, bf16[72,136,64]{1,2,0:T(8,128)(2,1)S(1)} %get-tuple-element.5), kind=kLoop, calls=%fused_computation.17 | loop fusion | bytes 2097152
  35.4 0.8 %dynamic-slice_dynamic-update-slice_fusion.3 = bf16[64,128,576]{1,2,0:T(8,128)(2,1)S(1)} fusion(bf16[64,128,576]{1,2,0:T(8,128)(2,1)S(1)} %slice_dynamic-update-slice_fusion, bf16[72,136,64]{1,2,0:T(8,128)(2,1)S(1)} %get-tuple-element.5, s32[]{:T(128)S(6)} %select_n.128), kind=kLoop, calls=%fused_computation.21 | loop fusion | bytes 2097156
  36.2 0.8 %dynamic-slice_dynamic-update-slice_fusion.2 = bf16[64,128,576]{1,2,0:T(8,128)(2,1)S(1)} fusion(bf16[64,128,576]{1,2,0:T(8,128)(2,1)S(1)} %dynamic-slice_dynamic-update-slice_fusion.3, bf16[72,136,64]{1,2,0:T(8,128)(2,1)S(1)} %get-tuple-element.5, s32[]{:T(128)S(6)} %select_n.129, s32[]{:T(128)S(6)} %select_n.127), kind=kLoop, calls=%fused_computation.20 | loop fusion | bytes 2097160
  36.9 0.7 %dynamic-slice_dynamic-update-slice_fusion.1 = bf16[64,128,576]{1,2,0:T(8,128)(2,1)S(1)} fusion(bf16[64,128,576]{1,2,0:T(8,128)(2,1)S(1)} %dynamic-slice_dynamic-update-slice_fusion.2, bf16[72,136,64]{1,2,0:T(8,128)(2,1)S(1)} %get-tuple-element.5, s32[]{:T(128)S(6)} %select_n.129), kind=kLoop, calls=%fused_computation.19 | loop fusion | bytes 2097156
  37.7 0.8 %dynamic-slice_dynamic-update-slice_fusion = bf16[64,128,576]{1,2,0:T(8,128)(2,1)S(1)} fusion(bf16[64,128,576]{1,2,0:T(8,128)(2,1)S(1)} %dynamic-slice_dynamic-update-slice_fusion.1, bf16[72,136,64]{1,2,0:T(8,128)(2,1)S(1)} %get-tuple-element.5, s32[]{:T(128)S(6)} %select_n.129, s32[]{:T(128)S(6)} %select_n.128), kind=kLoop, calls=%fused_computation.18 | loop fusion | bytes 2097160 | tf_op jit(solution)/shard_map/concatenate | solution.py:36
  38.4 1.9 %fusion.44 = f32[64,128,128]{1,2,0:T(8,128)S(1)} fusion(bf16[64,128,576]{1,2,0:T(8,128)(2,1)S(1)} %dynamic-slice_dynamic-update-slice_fusion, bf16[576,128,1]{1,0,2:T(8,128)(2,1)S(1)} %bitcast.46), kind=kOutput, calls=%fused_computation.99 | convolution fusion | flops 1207959552 | bytes 13778944 | tf_op jit(solution)/shard_map/dot_general | solution.py:38
  40.3 0.9 %fusion.2 = bf16[8,8,64,128]{3,1,2,0:T(8,128)(2,1)S(1)} fusion(f32[64,128,128]{1,2,0:T(8,128)S(1)} %fusion.44, bf16[72,136,64]{1,2,0:T(8,128)(2,1)S(1)} %get-tuple-element.6, f32[64]{0:T(128)S(1)} %get-tuple-element.36), kind=kOutput, calls=%fused_computation.11 | convolution fusion | flops 73404416 | bytes 6291968 | tf_op jit(solution)/shard_map/ck,nk->cn/dot_general | solution.py:159
  41.2 1.3 %copy.40 = bf16[8,8,64,128]{3,2,1,0:T(8,128)(2,1)} copy(bf16[8,8,64,128]{3,1,2,0:T(8,128)(2,1)S(1)} %fusion.2) | data formatting | bytes 2097152
  (30 shorter events, 2.0 us)
Async XLA Ops:
  0.0 0.7 %copy-start = (bf16[8,128]{1,0:T(8,128)(2,1)S(1)}, bf16[8,128]{1,0:T(8,128)(2,1)}, u32[]{:S(2)}) copy-start(bf16[8,128]{1,0:T(8,128)(2,1)} %param.6) | copy-start | bytes 6148
  2.3 22.3 %all-to-all-start = ((bf16[128,2,256]{2,1,0:T(2,128)(2,1)}), bf16[128,2,256]{2,1,0:T(2,128)(2,1)S(1)}, u32[]{:S(2)}, u32[]{:S(2)}) async-start(bf16[128,2,256]{2,1,0:T(2,128)(2,1)} %broadcast_in_dim.175), calls=%async_computation | async-start | bytes 262144 | tf_op jit(solution)/shard_map/all_to_all | solution.py:15

commit v14 on v13

--- a/solution.py
+++ b/solution.py
@@ -155,11 +155,10 @@
     pair = (0.5 * (mixed1.astype(jnp.float32) + mixed1_mirror.astype(jnp.float32))).astype(
         jnp.bfloat16
     )
-    flat = pair.reshape(row_size * col_size, channels)
     turned = jnp.einsum(
-        "ck,nk->cn", jnp.eye(channels, dtype=pair.dtype), flat, preferred_element_type=jnp.float32
+        "ck,ijk->cij", jnp.eye(channels, dtype=pair.dtype), pair, preferred_element_type=jnp.float32
     )
-    return turned.astype(jnp.bfloat16).reshape(channels, row_size, col_size)
+    return turned.astype(jnp.bfloat16)
 
 
 def solution(mesh):

time: 42.8 us -> 43.2 us (level)
    convert_element_type x0 -> x1, local copies, waits for them, and re-layouts: none -> 1.65 us  [local(): return turned.astype(jnp.bfloat16)]
    unnamed x13 -> x12, local copies, waits for them, and re-layouts: 7.93 us -> 6.68 us
  transfers between devices with their start and end apart: 1 -> 1, of which waited for: 0 -> 0; matrix products, arithmetic and copies ran while one was open for 13% -> 12% of each run, Pallas kernels for 0% -> 0%
where the time goes in v14:
time: 43.2 us; the launch traced here: 42.9 us
  local copies, waits for them, and re-layouts  14.5 us (34%)
  starting transfers between devices  11.5 us (27%)
  other arithmetic  7.16 us (17%)
  between operations  5.68 us (13%)
  matrix products  4.08 us (9%)
    all_to_all x1, starting transfers between devices, gather_projections(): lax.all_to_all(copies, axes, 0, 0, tiled=True).reshape(-1, proj.shape[1])  11.5 us
    unnamed x12, local copies, waits for them, and re-layouts  6.68 us
    mul x1, other arithmetic, local(): conv1 = tap_groups(jax.nn.relu(map1) * mask1, taps1, dilations[1])  5.72 us
    dot_general x1, matrix products, tap_groups(): summed = jnp.dot(stacked, flat_weight, preferred_element_type=jnp.float32)  1.85 us
    convert_element_type x1, local copies, waits for them, and re-layouts, local(): return turned.astype(jnp.bfloat16)  1.65 us
    slice x1, local copies, waits for them, and re-layouts, local(): conv1 = tap_groups(jax.nn.relu(map1) * mask1, taps1, dilations[1])  1.38 us
    ge x2, other arithmetic, pick(): near_high = (places >= bins_total - dilation).reshape(shape)  1.13 us
    squeeze x1, local copies, waits for them, and re-layouts, local(): conv_weight[1]  1.05 us
  transfers between devices with their start and end apart: 1, of which 0 were waited for; matrix products, arithmetic and copies ran while one was open for 12% of the time, Pallas kernels for 0%

profile of v14, /device:TPU:1, one launch (start us, length us, event | category | flops | bytes accessed | tf_op | source)
XLA Modules:
  0.0 42.9 jit_solution(3653453879892966913)
XLA Ops:
  0.0 0.7 %copy-done = bf16[8,128]{1,0:T(8,128)(2,1)S(1)} copy-done((bf16[8,128]{1,0:T(8,128)(2,1)S(1)}, bf16[8,128]{1,0:T(8,128)(2,1)}, u32[]{:S(2)}) %copy-start) | copy-done | bytes 2072
  0.7 0.8 %fusion.2 = bf16[8,64]{1,0:T(8,128)(2,1)S(1)} fusion(bf16[8,128]{1,0:T(8,128)(2,1)S(1)} %copy-done, bf16[128,32]{0,1:T(8,128)(2,1)} %param.8, bf16[128,32]{0,1:T(8,128)(2,1)} %param.7), kind=kOutput, calls=%fused_computation.12 | convolution fusion | flops 164352 | bytes 19456 | tf_op jit(solution)/shard_map/dot_general | solution.py:128
  1.6 0.7 %broadcast_in_dim.175 = bf16[128,2,256]{2,1,0:T(2,128)(2,1)} broadcast(bf16[2,256]{1,0:T(2,128)(2,1)S(1)} %broadcast_in_dim.174), dimensions={1,2} | broadcast | bytes 132096 | tf_op jit(solution)/shard_map/broadcast_in_dim | solution.py:14
  2.3 11.5 %all-to-all-start = ((bf16[128,2,256]{2,1,0:T(2,128)(2,1)}), bf16[128,2,256]{2,1,0:T(2,128)(2,1)S(1)}, u32[]{:S(2)}, u32[]{:S(2)}) async-start(bf16[128,2,256]{2,1,0:T(2,128)(2,1)} %broadcast_in_dim.175), calls=%async_computation | async-start | bytes 262144 | tf_op jit(solution)/shard_map/all_to_all | solution.py:15
  13.9 1.4 %fusion.47 = (s32[1]{0:T(128)}, s32[1]{0:T(128)}) fusion(s32[2]{0:T(128)} %param.11), kind=kLoop, calls=%fused_computation.99 | loop fusion | bytes 16 | tf_op jit(solution)/shard_map/slice | solution.py:149
  15.8 0.6 %fusion.36 = (pred[72]{0:T(512)(128)(4,1)S(1)}, pred[72]{0:T(512)(128)(4,1)S(1)}) fusion(s32[]{:T(128)S(6)} %sub.13, s32[]{:T(128)S(6)} %sub.14, s32[]{:T(128)} %bitcast.1), kind=kLoop, calls=%fused_computation.89 | loop fusion | flops 216 | bytes 156 | tf_op jit(solution)/shard_map/ge | solution.py:110
  16.4 0.6 %fusion.34 = (pred[136]{0:T(512)(128)(4,1)S(1)}, pred[136]{0:T(512)(128)(4,1)S(1)}) fusion(s32[]{:T(128)S(6)} %sub.13, s32[]{:T(128)S(6)} %sub.12, s32[]{:T(128)} %bitcast.1), kind=kLoop, calls=%fused_computation.85 | loop fusion | flops 408 | bytes 284 | tf_op jit(solution)/shard_map/ge | solution.py:110
  17.0 0.8 %slice_bitcast_fusion = (f32[64]{0:T(128)S(1)}, f32[64]{0:T(128)S(1)}) fusion(f32[2,64]{1,0:T(2,128)} %param.10), kind=kLoop, calls=%fused_computation.87 | loop fusion | bytes 1024 | tf_op jit(solution)/shard_map/add | solution.py:152
  17.7 1.1 %slice_bitcast_fusion.2 = (bf16[9,64,64]{2,1,0:T(8,128)(2,1)S(1)}, bf16[1,9,64,64]{3,2,1,0:T(8,128)(2,1)S(1)}, bf16[1,9,64,64]{3,2,1,0:T(8,128)(2,1)S(1)}) fusion(bf16[2,9,64,64]{3,2,1,0:T(8,128)(2,1)} %param.9), kind=kLoop, calls=%fused_computation.97 | loop fusion | bytes 368640 | tf_op jit(solution)/shard_map/squeeze | solution.py:148
  25.0 0.3 fusion.14
  25.9 0.2 fusion.23
  26.2 5.7 %maximum_multiply_fusion = (bf16[72,136,64]{1,2,0:T(8,128)(2,1)S(1)}, bf16[72,136,64]{1,2,0:T(8,128)(2,1)S(1)}) fusion(bf16[72,136]{1,0:T(8,128)(2,1)S(1)} %multiply_convert_fusion.3, f32[72,64]{1,0:T(8,128)S(1)} %get-tuple-element.22, f32[72,64]{1,0:T(8,128)S(1)} %get-tuple-element.23, f32[72,64]{1,0:T(8,128)S(1)} %get-tuple-element.24, ...), kind=kLoop, calls=%fused_computation.3 | loop fusion | flops 11907072 | bytes 2846240 | tf_op jit(solution)/shard_map/mul | solution.py:149
  31.9 0.5 %dynamic-slice_dynamic-update-slice_fusion.7 = bf16[64,128,576]{1,2,0:T(8,128)(2,1)S(1)} fusion(bf16[72,136,64]{1,2,0:T(8,128)(2,1)S(1)} %get-tuple-element.5, s32[]{:T(128)S(6)} %select_n.126, s32[]{:T(128)S(6)} %select_n.127), kind=kLoop, calls=%fused_computation.23 | loop fusion | bytes 2097160
  32.4 0.7 %dynamic-slice_dynamic-update-slice_fusion.6 = bf16[64,128,576]{1,2,0:T(8,128)(2,1)S(1)} fusion(bf16[64,128,576]{1,2,0:T(8,128)(2,1)S(1)} %dynamic-slice_dynamic-update-slice_fusion.7, bf16[72,136,64]{1,2,0:T(8,128)(2,1)S(1)} %get-tuple-element.5, s32[]{:T(128)S(6)} %select_n.126), kind=kLoop, calls=%fused_computation.22 | loop fusion | bytes 2097156
  33.1 0.8 %dynamic-slice_dynamic-update-slice_fusion.5 = bf16[64,128,576]{1,2,0:T(8,128)(2,1)S(1)} fusion(bf16[64,128,576]{1,2,0:T(8,128)(2,1)S(1)} %dynamic-slice_dynamic-update-slice_fusion.6, bf16[72,136,64]{1,2,0:T(8,128)(2,1)S(1)} %get-tuple-element.5, s32[]{:T(128)S(6)} %select_n.126, s32[]{:T(128)S(6)} %select_n.128), kind=kLoop, calls=%fused_computation.21 | loop fusion | bytes 2097160
  33.9 0.8 %dynamic-slice_dynamic-update-slice_fusion.4 = bf16[64,128,576]{1,2,0:T(8,128)(2,1)S(1)} fusion(bf16[64,128,576]{1,2,0:T(8,128)(2,1)S(1)} %dynamic-slice_dynamic-update-slice_fusion.5, bf16[72,136,64]{1,2,0:T(8,128)(2,1)S(1)} %get-tuple-element.5, s32[]{:T(128)S(6)} %select_n.127), kind=kLoop, calls=%fused_computation.20 | loop fusion | bytes 2097156
  34.7 0.7 %slice_dynamic-update-slice_fusion = bf16[64,128,576]{1,2,0:T(8,128)(2,1)S(1)} fusion(bf16[64,128,576]{1,2,0:T(8,128)(2,1)S(1)} %dynamic-slice_dynamic-update-slice_fusion.4, bf16[72,136,64]{1,2,0:T(8,128)(2,1)S(1)} %get-tuple-element.5), kind=kLoop, calls=%fused_computation.13 | loop fusion | bytes 2097152
  35.4 0.8 %dynamic-slice_dynamic-update-slice_fusion.3 = bf16[64,128,576]{1,2,0:T(8,128)(2,1)S(1)} fusion(bf16[64,128,576]{1,2,0:T(8,128)(2,1)S(1)} %slice_dynamic-update-slice_fusion, bf16[72,136,64]{1,2,0:T(8,128)(2,1)S(1)} %get-tuple-element.5, s32[]{:T(128)S(6)} %select_n.128), kind=kLoop, calls=%fused_computation.19 | loop fusion | bytes 2097156
  36.2 0.8 %dynamic-slice_dynamic-update-slice_fusion.2 = bf16[64,128,576]{1,2,0:T(8,128)(2,1)S(1)} fusion(bf16[64,128,576]{1,2,0:T(8,128)(2,1)S(1)} %dynamic-slice_dynamic-update-slice_fusion.3, bf16[72,136,64]{1,2,0:T(8,128)(2,1)S(1)} %get-tuple-element.5, s32[]{:T(128)S(6)} %select_n.129, s32[]{:T(128)S(6)} %select_n.127), kind=kLoop, calls=%fused_computation.18 | loop fusion | bytes 2097160
  36.9 0.7 %dynamic-slice_dynamic-update-slice_fusion.1 = bf16[64,128,576]{1,2,0:T(8,128)(2,1)S(1)} fusion(bf16[64,128,576]{1,2,0:T(8,128)(2,1)S(1)} %dynamic-slice_dynamic-update-slice_fusion.2, bf16[72,136,64]{1,2,0:T(8,128)(2,1)S(1)} %get-tuple-element.5, s32[]{:T(128)S(6)} %select_n.129), kind=kLoop, calls=%fused_computation.17 | loop fusion | bytes 2097156
  37.7 0.8 %dynamic-slice_dynamic-update-slice_fusion = bf16[64,128,576]{1,2,0:T(8,128)(2,1)S(1)} fusion(bf16[64,128,576]{1,2,0:T(8,128)(2,1)S(1)} %dynamic-slice_dynamic-update-slice_fusion.1, bf16[72,136,64]{1,2,0:T(8,128)(2,1)S(1)} %get-tuple-element.5, s32[]{:T(128)S(6)} %select_n.129, s32[]{:T(128)S(6)} %select_n.128), kind=kLoop, calls=%fused_computation.16 | loop fusion | bytes 2097160 | tf_op jit(solution)/shard_map/concatenate | solution.py:36
  38.4 1.9 %fusion.48 = f32[64,128,128]{1,2,0:T(8,128)S(1)} fusion(bf16[64,128,576]{1,2,0:T(8,128)(2,1)S(1)} %dynamic-slice_dynamic-update-slice_fusion, bf16[576,128,1]{1,0,2:T(8,128)(2,1)S(1)} %bitcast.39), kind=kOutput, calls=%fused_computation.100 | convolution fusion | flops 1207959552 | bytes 13778944 | tf_op jit(solution)/shard_map/dot_general | solution.py:38
  40.3 0.9 %convolution_convert_fusion = bf16[64,64,128]{2,0,1:T(8,128)(2,1)S(1)} fusion(f32[64,128,128]{1,2,0:T(8,128)S(1)} %fusion.48, bf16[72,136,64]{1,2,0:T(8,128)(2,1)S(1)} %get-tuple-element.6, f32[64]{0:T(128)S(1)} %get-tuple-element.36), kind=kOutput, calls=%fused_computation.10 | convolution fusion | flops 73404416 | bytes 6291968 | tf_op jit(solution)/shard_map/ck,ijk->cij/dot_general | solution.py:158
  41.2 1.6 %copy.37 = bf16[64,64,128]{2,1,0:T(8,128)(2,1)} copy(bf16[64,64,128]{2,0,1:T(8,128)(2,1)S(1)} %convolution_convert_fusion) | data formatting | bytes 2097152 | tf_op jit(solution)/shard_map/convert_element_type | solution.py:161
  (30 shorter events, 2.0 us)
Async XLA Ops:
  0.0 0.7 %copy-start = (bf16[8,128]{1,0:T(8,128)(2,1)S(1)}, bf16[8,128]{1,0:T(8,128)(2,1)}, u32[]{:S(2)}) copy-start(bf16[8,128]{1,0:T(8,128)(2,1)} %param.6) | copy-start | bytes 6148
  2.3 22.3 %all-to-all-start = ((bf16[128,2,256]{2,1,0:T(2,128)(2,1)}), bf16[128,2,256]{2,1,0:T(2,128)(2,1)S(1)}, u32[]{:S(2)}, u32[]{:S(2)}) async-start(bf16[128,2,256]{2,1,0:T(2,128)(2,1)} %broadcast_in_dim.175), calls=%async_computation | async-start | bytes 262144 | tf_op jit(solution)/shard_map/all_to_all | solution.py:15

commit v15 on v13

--- a/solution.py
+++ b/solution.py
@@ -70,16 +70,17 @@
         axis=1,
     ).reshape(3 * 2 * half, 6 * lane_group)
 
-    def tables(start, count):
+    def shifted_rows(start, count):
         window = lax.dynamic_slice_in_dim(active, start, count + 2 * MAXDIL, 0)
-        shifted = jnp.concatenate(
+        return jnp.concatenate(
             [
                 lax.dynamic_slice_in_dim(window, MAXDIL + (step - 1) * dilation, count, 0)
                 for step in range(3)
             ],
             axis=1,
         )
-        parts = jnp.dot(shifted, weight, preferred_element_type=jnp.float32)
+
+    def tables(start, count, parts):
         by_col = [parts[:, lane_group * k : lane_group * k + out_ch] for k in range(3)]
         by_row = [parts[:, lane_group * (3 + k) : lane_group * (3 + k) + out_ch] for k in range(3)]
         own = lax.dynamic_slice_in_dim(padded, start, count, 0)
@@ -99,8 +100,13 @@
 
     row_places = row_start - MAXDIL + jnp.arange(rows)
     col_places = col_start - MAXDIL + jnp.arange(cols)
-    rows_row_tables, rows_col_tables = tables(row_start, rows)
-    cols_row_tables, cols_col_tables = tables(col_start, cols)
+    both_parts = jnp.dot(
+        jnp.concatenate([shifted_rows(row_start, rows), shifted_rows(col_start, cols)], axis=0),
+        weight,
+        preferred_element_type=jnp.float32,
+    )
+    rows_row_tables, rows_col_tables = tables(row_start, rows, both_parts[:rows])
+    cols_row_tables, cols_col_tables = tables(col_start, cols, both_parts[rows:])
 
     def pick(tables_here, places, axis):
         low, mid, high = tables_here

time: 42.8 us -> 42.6 us (level)
  no operation moved by 1% of the time
where the time goes in v15:
time: 42.6 us; the launch traced here: 42.2 us
  local copies, waits for them, and re-layouts  14.1 us (33%)
  starting transfers between devices  11.5 us (27%)
  other arithmetic  7.15 us (17%)
  between operations  5.67 us (13%)
  matrix products  3.86 us (9%)
    all_to_all x1, starting transfers between devices, gather_projections(): lax.all_to_all(copies, axes, 0, 0, tiled=True).reshape(-1, proj.shape[1])  11.5 us
    unnamed x13, local copies, waits for them, and re-layouts  7.93 us
    mul x1, other arithmetic, local(): conv1 = tap_groups(jax.nn.relu(map1) * mask1, taps1, dilations[1])  5.72 us
    dot_general x1, matrix products, tap_groups(): summed = jnp.dot(stacked, flat_weight, preferred_element_type=jnp.float32)  1.85 us
    slice x1, local copies, waits for them, and re-layouts, local(): conv1 = tap_groups(jax.nn.relu(map1) * mask1, taps1, dilations[1])  1.38 us
    ge x2, other arithmetic, pick(): near_high = (places >= bins_total - dilation).reshape(shape)  1.13 us
    squeeze x1, local copies, waits for them, and re-layouts, local(): conv_weight[1]  1.05 us
    dot_general x1, matrix products, local(): jnp.einsum('ck,nk->cn', jnp.eye(channels, dtype=pair.dtype), flat, prefer...  0.88 us
  transfers between devices with their start and end apart: 1, of which 0 were waited for; matrix products, arithmetic and copies ran while one was open for 13% of the time, Pallas kernels for 0%

profile of v15, /device:TPU:1, one launch (start us, length us, event | category | flops | bytes accessed | tf_op | source)
XLA Modules:
  0.0 42.2 jit_solution(976514814956584232)
XLA Ops:
  0.0 0.7 %copy-done = bf16[8,128]{1,0:T(8,128)(2,1)S(1)} copy-done((bf16[8,128]{1,0:T(8,128)(2,1)S(1)}, bf16[8,128]{1,0:T(8,128)(2,1)}, u32[]{:S(2)}) %copy-start) | copy-done | bytes 2072
  0.7 0.8 %fusion.3 = bf16[8,64]{1,0:T(8,128)(2,1)S(1)} fusion(bf16[8,128]{1,0:T(8,128)(2,1)S(1)} %copy-done, bf16[128,32]{0,1:T(8,128)(2,1)} %param.8, bf16[128,32]{0,1:T(8,128)(2,1)} %param.7), kind=kOutput, calls=%fused_computation.13 | convolution fusion | flops 164352 | bytes 19456 | tf_op jit(solution)/shard_map/dot_general | solution.py:134
  1.6 0.7 %broadcast_in_dim.175 = bf16[128,2,256]{2,1,0:T(2,128)(2,1)} broadcast(bf16[2,256]{1,0:T(2,128)(2,1)S(1)} %broadcast_in_dim.174), dimensions={1,2} | broadcast | bytes 132096 | tf_op jit(solution)/shard_map/broadcast_in_dim | solution.py:14
  2.3 11.5 %all-to-all-start = ((bf16[128,2,256]{2,1,0:T(2,128)(2,1)}), bf16[128,2,256]{2,1,0:T(2,128)(2,1)S(1)}, u32[]{:S(2)}, u32[]{:S(2)}) async-start(bf16[128,2,256]{2,1,0:T(2,128)(2,1)} %broadcast_in_dim.175), calls=%async_computation | async-start | bytes 262144 | tf_op jit(solution)/shard_map/all_to_all | solution.py:15
  13.9 1.4 %fusion.42 = (s32[1]{0:T(128)}, s32[1]{0:T(128)}) fusion(s32[2]{0:T(128)} %param.11), kind=kLoop, calls=%fused_computation.97 | loop fusion | bytes 16 | tf_op jit(solution)/shard_map/slice | solution.py:155
  15.8 0.6 %fusion.33 = (pred[72]{0:T(512)(128)(4,1)S(1)}, pred[72]{0:T(512)(128)(4,1)S(1)}) fusion(s32[]{:T(128)S(6)} %sub.13, s32[]{:T(128)S(6)} %sub.14, s32[]{:T(128)} %bitcast), kind=kLoop, calls=%fused_computation.89 | loop fusion | flops 216 | bytes 156 | tf_op jit(solution)/shard_map/ge | solution.py:116
  16.4 0.6 %fusion.31 = (pred[136]{0:T(512)(128)(4,1)S(1)}, pred[136]{0:T(512)(128)(4,1)S(1)}) fusion(s32[]{:T(128)S(6)} %sub.13, s32[]{:T(128)S(6)} %sub.12, s32[]{:T(128)} %bitcast), kind=kLoop, calls=%fused_computation.85 | loop fusion | flops 408 | bytes 284 | tf_op jit(solution)/shard_map/ge | solution.py:116
  17.0 0.8 %slice_bitcast_fusion = (f32[64]{0:T(128)S(1)}, f32[64]{0:T(128)S(1)}) fusion(f32[2,64]{1,0:T(2,128)} %param.10), kind=kLoop, calls=%fused_computation.87 | loop fusion | bytes 1024 | tf_op jit(solution)/shard_map/add | solution.py:158
  17.7 1.1 %slice_bitcast_fusion.2 = (bf16[9,64,64]{2,1,0:T(8,128)(2,1)S(1)}, bf16[1,9,64,64]{3,2,1,0:T(8,128)(2,1)S(1)}, bf16[1,9,64,64]{3,2,1,0:T(8,128)(2,1)S(1)}) fusion(bf16[2,9,64,64]{3,2,1,0:T(8,128)(2,1)} %param.9), kind=kLoop, calls=%fused_computation.95 | loop fusion | bytes 368640 | tf_op jit(solution)/shard_map/squeeze | solution.py:154
  24.7 0.2 reshape.151
  25.0 0.3 fusion.10
  26.0 5.7 %maximum_multiply_fusion = (bf16[72,136,64]{1,2,0:T(8,128)(2,1)S(1)}, bf16[72,136,64]{1,2,0:T(8,128)(2,1)S(1)}) fusion(bf16[72,136]{1,0:T(8,128)(2,1)S(1)} %multiply_convert_fusion.2, f32[72,64]{1,0:T(8,128)S(1)} %get-tuple-element.18, f32[72,64]{1,0:T(8,128)S(1)} %get-tuple-element.19, f32[72,64]{1,0:T(8,128)S(1)} %get-tuple-element.17, ...), kind=kLoop, calls=%fused_computation.4 | loop fusion | flops 11907072 | bytes 2846240 | tf_op jit(solution)/shard_map/mul | solution.py:155
  31.7 0.5 %dynamic-slice_dynamic-update-slice_fusion.7 = bf16[64,128,576]{1,2,0:T(8,128)(2,1)S(1)} fusion(bf16[72,136,64]{1,2,0:T(8,128)(2,1)S(1)} %get-tuple-element.5, s32[]{:T(128)S(6)} %select_n.126, s32[]{:T(128)S(6)} %select_n.127), kind=kLoop, calls=%fused_computation.25 | loop fusion | bytes 2097160
  32.2 0.7 %dynamic-slice_dynamic-update-slice_fusion.6 = bf16[64,128,576]{1,2,0:T(8,128)(2,1)S(1)} fusion(bf16[64,128,576]{1,2,0:T(8,128)(2,1)S(1)} %dynamic-slice_dynamic-update-slice_fusion.7, bf16[72,136,64]{1,2,0:T(8,128)(2,1)S(1)} %get-tuple-element.5, s32[]{:T(128)S(6)} %select_n.126), kind=kLoop, calls=%fused_computation.24 | loop fusion | bytes 2097156
  32.9 0.8 %dynamic-slice_dynamic-update-slice_fusion.5 = bf16[64,128,576]{1,2,0:T(8,128)(2,1)S(1)} fusion(bf16[64,128,576]{1,2,0:T(8,128)(2,1)S(1)} %dynamic-slice_dynamic-update-slice_fusion.6, bf16[72,136,64]{1,2,0:T(8,128)(2,1)S(1)} %get-tuple-element.5, s32[]{:T(128)S(6)} %select_n.126, s32[]{:T(128)S(6)} %select_n.128), kind=kLoop, calls=%fused_computation.23 | loop fusion | bytes 2097160
  33.7 0.8 %dynamic-slice_dynamic-update-slice_fusion.4 = bf16[64,128,576]{1,2,0:T(8,128)(2,1)S(1)} fusion(bf16[64,128,576]{1,2,0:T(8,128)(2,1)S(1)} %dynamic-slice_dynamic-update-slice_fusion.5, bf16[72,136,64]{1,2,0:T(8,128)(2,1)S(1)} %get-tuple-element.5, s32[]{:T(128)S(6)} %select_n.127), kind=kLoop, calls=%fused_computation.22 | loop fusion | bytes 2097156
  34.5 0.7 %slice_dynamic-update-slice_fusion = bf16[64,128,576]{1,2,0:T(8,128)(2,1)S(1)} fusion(bf16[64,128,576]{1,2,0:T(8,128)(2,1)S(1)} %dynamic-slice_dynamic-update-slice_fusion.4, bf16[72,136,64]{1,2,0:T(8,128)(2,1)S(1)} %get-tuple-element.5), kind=kLoop, calls=%fused_computation.17 | loop fusion | bytes 2097152
  35.2 0.8 %dynamic-slice_dynamic-update-slice_fusion.3 = bf16[64,128,576]{1,2,0:T(8,128)(2,1)S(1)} fusion(bf16[64,128,576]{1,2,0:T(8,128)(2,1)S(1)} %slice_dynamic-update-slice_fusion, bf16[72,136,64]{1,2,0:T(8,128)(2,1)S(1)} %get-tuple-element.5, s32[]{:T(128)S(6)} %select_n.128), kind=kLoop, calls=%fused_computation.21 | loop fusion | bytes 2097156
  36.0 0.8 %dynamic-slice_dynamic-update-slice_fusion.2 = bf16[64,128,576]{1,2,0:T(8,128)(2,1)S(1)} fusion(bf16[64,128,576]{1,2,0:T(8,128)(2,1)S(1)} %dynamic-slice_dynamic-update-slice_fusion.3, bf16[72,136,64]{1,2,0:T(8,128)(2,1)S(1)} %get-tuple-element.5, s32[]{:T(128)S(6)} %select_n.129, s32[]{:T(128)S(6)} %select_n.127), kind=kLoop, calls=%fused_computation.20 | loop fusion | bytes 2097160
  36.7 0.7 %dynamic-slice_dynamic-update-slice_fusion.1 = bf16[64,128,576]{1,2,0:T(8,128)(2,1)S(1)} fusion(bf16[64,128,576]{1,2,0:T(8,128)(2,1)S(1)} %dynamic-slice_dynamic-update-slice_fusion.2, bf16[72,136,64]{1,2,0:T(8,128)(2,1)S(1)} %get-tuple-element.5, s32[]{:T(128)S(6)} %select_n.129), kind=kLoop, calls=%fused_computation.19 | loop fusion | bytes 2097156
  37.5 0.8 %dynamic-slice_dynamic-update-slice_fusion = bf16[64,128,576]{1,2,0:T(8,128)(2,1)S(1)} fusion(bf16[64,128,576]{1,2,0:T(8,128)(2,1)S(1)} %dynamic-slice_dynamic-update-slice_fusion.1, bf16[72,136,64]{1,2,0:T(8,128)(2,1)S(1)} %get-tuple-element.5, s32[]{:T(128)S(6)} %select_n.129, s32[]{:T(128)S(6)} %select_n.128), kind=kLoop, calls=%fused_computation.18 | loop fusion | bytes 2097160 | tf_op jit(solution)/shard_map/concatenate | solution.py:36
  38.2 1.9 %fusion.43 = f32[64,128,128]{1,2,0:T(8,128)S(1)} fusion(bf16[64,128,576]{1,2,0:T(8,128)(2,1)S(1)} %dynamic-slice_dynamic-update-slice_fusion, bf16[576,128,1]{1,0,2:T(8,128)(2,1)S(1)} %bitcast.44), kind=kOutput, calls=%fused_computation.98 | convolution fusion | flops 1207959552 | bytes 13778944 | tf_op jit(solution)/shard_map/dot_general | solution.py:38
  40.1 0.9 %fusion.2 = bf16[8,8,64,128]{3,1,2,0:T(8,128)(2,1)S(1)} fusion(f32[64,128,128]{1,2,0:T(8,128)S(1)} %fusion.43, bf16[72,136,64]{1,2,0:T(8,128)(2,1)S(1)} %get-tuple-element.6, f32[64]{0:T(128)S(1)} %get-tuple-element.36), kind=kOutput, calls=%fused_computation.11 | convolution fusion | flops 73404416 | bytes 6291968 | tf_op jit(solution)/shard_map/ck,nk->cn/dot_general | solution.py:165
  41.0 1.3 %copy.40 = bf16[8,8,64,128]{3,2,1,0:T(8,128)(2,1)} copy(bf16[8,8,64,128]{3,1,2,0:T(8,128)(2,1)S(1)} %fusion.2) | data formatting | bytes 2097152
  (29 shorter events, 1.8 us)
Async XLA Ops:
  0.0 0.7 %copy-start = (bf16[8,128]{1,0:T(8,128)(2,1)S(1)}, bf16[8,128]{1,0:T(8,128)(2,1)}, u32[]{:S(2)}) copy-start(bf16[8,128]{1,0:T(8,128)(2,1)} %param.6) | copy-start | bytes 6148
  2.3 22.3 %all-to-all-start = ((bf16[128,2,256]{2,1,0:T(2,128)(2,1)}), bf16[128,2,256]{2,1,0:T(2,128)(2,1)S(1)}, u32[]{:S(2)}, u32[]{:S(2)}) async-start(bf16[128,2,256]{2,1,0:T(2,128)(2,1)} %broadcast_in_dim.175), calls=%async_computation | async-start | bytes 262144 | tf_op jit(solution)/shard_map/all_to_all | solution.py:15
